TPU v7x, 128 devices: a whole 4x4x4 slice. The times are simulated.
128 devices in a mesh: ia: 4 (over y), ja: 16 (over z, x), ha: 2 (over core).
Axes of the slice: x: 4, y: 4, z: 4, core: 2. Of those that a mesh axis runs over, the one named last changes fastest.
Arguments:
- phase_space: float32 [6, 65536], P(None, ('ja', 'ha')), may hold values from -5 to 5
- derivatives: float32 [6, 65536], P(None, ('ja', 'ha')), may hold values from -8 to 8
- body_mass: float32 [65536], P(('ja', 'ha')), may hold values from 4.577637e-06 to 0.018310547
- active_lists: int32 [4, 4, 32], replicated, may hold values from -1 to 511, as said below
Outputs:
- phase_out: float32 [6, 65536], P(None, ('ja', 'ha'))
- deriv_out: float32 [6, 65536], P(None, ('ja', 'ha'))
Inputs may be any that keep to these rules, and one draw needn't show every extreme that they name: `active_lists`: each block has a rung of 0 to 4 and is active in step s (1 to 4) exactly when s is a multiple of 2 ** (4 - rung). In each step a block id stands in at most one slot of one group, the live slots of a group come first, a group has at most 32 live slots, and in the last step every group has exactly 32.
All inputs are finite; a program needn't handle non-finite values.
Results may differ from a plain program's by a relative error of at most 0.0003.
Values sent between devices are 32-bit elements; how exact they have to be, the bound alone decides.
A program may use at most 64 MiB of HBM per device.

v0:
```python
import math

import jax
import jax.numpy as jnp
from jax import lax
from jax.sharding import PartitionSpec as P

BLK = 128
STEPS = 4


time_step = 0.02
soften_sq = 0.0025


def predict(phase_space, derivatives, elapsed):
    position = phase_space[0:3]
    velocity = phase_space[3:6]
    acceleration = derivatives[0:3]
    jerk_old = derivatives[3:6]
    pos_next = position + elapsed * (
        velocity + elapsed * (acceleration * 0.5 + elapsed * jerk_old / 6.0)
    )
    vel_next = velocity + elapsed * (acceleration + elapsed * jerk_old * 0.5)
    return jnp.concatenate([pos_next, vel_next], axis=0)


def pair_terms(targets, field_rows, body_mass):
    sep_x = field_rows[0][None, :] - targets[0][:, None]
    sep_y = field_rows[1][None, :] - targets[1][:, None]
    sep_z = field_rows[2][None, :] - targets[2][:, None]
    rel_x = field_rows[3][None, :] - targets[3][:, None]
    rel_y = field_rows[4][None, :] - targets[4][:, None]
    rel_z = field_rows[5][None, :] - targets[5][:, None]
    dist_sq = sep_x * sep_x + sep_y * sep_y + sep_z * sep_z + soften_sq
    inv_r = lax.rsqrt(dist_sq)
    inv_cube = body_mass[None, :] * inv_r * inv_r * inv_r
    radial = 3.0 * (sep_x * rel_x + sep_y * rel_y + sep_z * rel_z) * inv_r * inv_r
    return jnp.stack(
        [
            jnp.sum(inv_cube * sep_x, axis=1),
            jnp.sum(inv_cube * sep_y, axis=1),
            jnp.sum(inv_cube * sep_z, axis=1),
            jnp.sum(inv_cube * (rel_x - radial * sep_x), axis=1),
            jnp.sum(inv_cube * (rel_y - radial * sep_y), axis=1),
            jnp.sum(inv_cube * (rel_z - radial * sep_z), axis=1),
        ],
        axis=0,
    )


def star_terms(predicted):
    position = predicted[0:3]
    velocity = predicted[3:6]
    inv_r = lax.rsqrt(jnp.sum(position * position, axis=0))
    inv_cube = inv_r * inv_r * inv_r
    radial = 3.0 * jnp.sum(position * velocity, axis=0) * inv_r * inv_r
    accel = -inv_cube[None, :] * position
    jerk_star = -inv_cube[None, :] * (velocity - radial[None, :] * position)
    return jnp.concatenate([accel, jerk_star], axis=0)


def correct(phase_space, derivatives, fresh, elapsed):
    half_dt = 0.5 * elapsed
    twelfth = elapsed * elapsed / 12.0
    vel_new = (
        phase_space[3:6]
        + half_dt * (derivatives[0:3] + fresh[0:3])
        + twelfth * (derivatives[3:6] - fresh[3:6])
    )
    pos_new = (
        phase_space[0:3]
        + half_dt * (phase_space[3:6] + vel_new)
        + twelfth * (derivatives[0:3] - fresh[0:3])
    )
    return jnp.concatenate([pos_new, vel_new], axis=0)


def tile_forces(targets, field_rows, body_mass):
    slot_count = targets.shape[1]
    block_len = targets.shape[2]
    group_width = math.gcd(slot_count, 8)
    grouped = targets.reshape(6, slot_count // group_width, group_width * block_len).transpose(
        1, 0, 2
    )
    results = lax.map(lambda tile_rows: pair_terms(tile_rows, field_rows, body_mass), grouped)
    return results.transpose(1, 0, 2).reshape(6, slot_count, block_len)


def shards(phase_space, derivatives, body_mass, active_lists):
    local_count = phase_space.shape[1]
    blocks_local = local_count // BLK
    my_part = lax.axis_index("ja") * lax.axis_size("ha") + lax.axis_index("ha")
    my_group = lax.axis_index("ia")
    own_blocks = my_part * blocks_local + jnp.arange(blocks_local, dtype=jnp.int32)
    last_time = jnp.zeros((local_count,), jnp.float32)
    for step_index in range(STEPS):
        now_time = (step_index + 1) * time_step
        step_lists = active_lists[step_index]
        elapsed = (now_time - last_time)[None, :]
        predicted = predict(phase_space, derivatives, elapsed)
        block_ids = lax.dynamic_index_in_dim(step_lists, my_group, 0, keepdims=False)
        owner_part = block_ids // blocks_local
        local_index = jnp.clip(block_ids - owner_part * blocks_local, 0, blocks_local - 1)
        is_mine = (owner_part == my_part) & (block_ids >= 0)
        picked = jnp.take(predicted.reshape(6, blocks_local, BLK), local_index, axis=1)
        picked = jnp.where(is_mine[None, :, None], picked, 0.0)
        targets = lax.psum(picked, ("ja", "ha"))
        partial_terms = tile_forces(targets, predicted, body_mass)
        totals = lax.psum(partial_terms, ("ja", "ha"))
        kept_terms = jnp.where(is_mine[None, :, None], totals, 0.0)
        mine_terms = (
            jnp.zeros((6, blocks_local, BLK), jnp.float32).at[:, local_index].add(kept_terms)
        )
        mine_terms = mine_terms.reshape(6, local_count)
        fresh = lax.psum(mine_terms, "ia") + star_terms(predicted)
        active_flags = jnp.any(step_lists.reshape(-1)[:, None] == own_blocks[None, :], axis=0)
        active = jnp.repeat(active_flags, BLK)[None, :]
        corrected = correct(phase_space, derivatives, fresh, elapsed)
        phase_space = jnp.where(active, corrected, phase_space)
        derivatives = jnp.where(active, fresh, derivatives)
        last_time = jnp.where(active[0], jnp.float32(now_time), last_time)
    return (phase_space, derivatives)


def solution(mesh):
    return jax.shard_map(
        shards,
        mesh=mesh,
        in_specs=(P(None, ("ja", "ha")), P(None, ("ja", "ha")), P(("ja", "ha")), P()),
        out_specs=(P(None, ("ja", "ha")), P(None, ("ja", "ha"))),
        check_vma=False,
    )
```

profile of v0, /device:TPU:1, one launch (start us, length us, event | category | flops | bytes accessed | tf_op | source)
XLA Modules:
  0.0 1166.4 jit_solution(15828723331666491306)
XLA Ops:
  11.7 104.0 %all-reduce.9.cloned.1.call-done = f32[4,6,1024]{2,1,0:T(8,128)} async-done(((f32[4,6,1024]{2,1,0:T(8,128)}), f32[4,6,1024]{2,1,0:T(8,128)}) %all-reduce.9.cloned.1.call-update) | async-done | bytes 98320 | tf_op jit(solution)/shard_map/psum | solution.py:108
  115.7 64.3 %while.40 = (s32[]{:T(128)}, f32[4,6,1024]{2,1,0:T(8,128)S(1)}, f32[2048]{0:T(1024)S(1)}, f32[3,2048]{1,0:T(4,128)S(1)}, f32[4,6,1024]{2,1,0:T(8,128)}, /*index=...) while((s32[]{:T(128)}, f32[4,6,1024]{2,1,0:T(8,128)S(1)}, ...), condition=%wide.region_12.14_spmd, body=%wide.region_5.13_spmd.sunk | while | flops 85977096 | bytes 368853 | solution.py:86
  116.8 14.9 %fusion.115 = (f32[1024]{0:T(1024)S(1)}, f32[1024]{0:T(1024)S(1)}, f32[1024]{0:T(1024)S(1)}, f32[1024]{0:T(1024)S(1)}, f32[1024]{0:T(1024)S(1)}, /*index=5*/f32[1024]{0:T(1024)S(1)}) fusion(f32[1024]{0:T(1024)S(1)} %bitcast.521, f32[2048]{0:T(1024)S(1)} %bitcast.469, f32[1024]{0:T(1024)S(1)} %bitcast.518, f32[2048]{0:T(1024)S(1)} %bitcast.472, ...), kind=kLoop, calls=%fused_computation.30.clone.1 | loop fusion | flops 85977088 | bytes 106496 | tf_op jit(solution)/shard_map/while/body/eval_jaxpr/reduce_sum | solution.py:46
  132.9 14.9 %fusion.115 = (f32[1024]{0:T(1024)S(1)}, f32[1024]{0:T(1024)S(1)}, f32[1024]{0:T(1024)S(1)}, f32[1024]{0:T(1024)S(1)}, f32[1024]{0:T(1024)S(1)}, /*index=5*/f32[1024]{0:T(1024)S(1)}) fusion(f32[1024]{0:T(1024)S(1)} %bitcast.521, f32[2048]{0:T(1024)S(1)} %bitcast.469, f32[1024]{0:T(1024)S(1)} %bitcast.518, f32[2048]{0:T(1024)S(1)} %bitcast.472, ...), kind=kLoop, calls=%fused_computation.30.clone.1 | loop fusion | flops 85977088 | bytes 106496 | tf_op jit(solution)/shard_map/while/body/eval_jaxpr/reduce_sum | solution.py:46
  149.0 14.9 %fusion.115 = (f32[1024]{0:T(1024)S(1)}, f32[1024]{0:T(1024)S(1)}, f32[1024]{0:T(1024)S(1)}, f32[1024]{0:T(1024)S(1)}, f32[1024]{0:T(1024)S(1)}, /*index=5*/f32[1024]{0:T(1024)S(1)}) fusion(f32[1024]{0:T(1024)S(1)} %bitcast.521, f32[2048]{0:T(1024)S(1)} %bitcast.469, f32[1024]{0:T(1024)S(1)} %bitcast.518, f32[2048]{0:T(1024)S(1)} %bitcast.472, ...), kind=kLoop, calls=%fused_computation.30.clone.1 | loop fusion | flops 85977088 | bytes 106496 | tf_op jit(solution)/shard_map/while/body/eval_jaxpr/reduce_sum | solution.py:46
  165.1 14.9 %fusion.115 = (f32[1024]{0:T(1024)S(1)}, f32[1024]{0:T(1024)S(1)}, f32[1024]{0:T(1024)S(1)}, f32[1024]{0:T(1024)S(1)}, f32[1024]{0:T(1024)S(1)}, /*index=5*/f32[1024]{0:T(1024)S(1)}) fusion(f32[1024]{0:T(1024)S(1)} %bitcast.521, f32[2048]{0:T(1024)S(1)} %bitcast.469, f32[1024]{0:T(1024)S(1)} %bitcast.518, f32[2048]{0:T(1024)S(1)} %bitcast.472, ...), kind=kLoop, calls=%fused_computation.30.clone.1 | loop fusion | flops 85977088 | bytes 106496 | tf_op jit(solution)/shard_map/while/body/eval_jaxpr/reduce_sum | solution.py:46
  180.8 100.8 %all-reduce.11.cloned.1.call-done = f32[6,32,128]{2,0,1:T(8,128)} async-done(((f32[6,32,128]{2,0,1:T(8,128)}), f32[6,32,128]{2,0,1:T(8,128)}) %all-reduce.11.cloned.1.call-update) | async-done | bytes 98320 | tf_op jit(solution)/shard_map/psum | solution.py:110
  300.7 102.6 %all-reduce.13.cloned.1.call-done = f32[4,6,1024]{2,1,0:T(8,128)} async-done(((f32[4,6,1024]{2,1,0:T(8,128)}), f32[4,6,1024]{2,1,0:T(8,128)}) %all-reduce.13.cloned.1.call-update) | async-done | bytes 98320 | tf_op jit(solution)/shard_map/psum | solution.py:108
  403.3 64.3 %while.41 = (s32[]{:T(128)}, f32[4,6,1024]{2,1,0:T(8,128)S(1)}, f32[2048]{0:T(1024)S(1)}, f32[3,2048]{1,0:T(4,128)S(1)}, f32[4,6,1024]{2,1,0:T(8,128)}, /*index=...) while((s32[]{:T(128)}, f32[4,6,1024]{2,1,0:T(8,128)S(1)}, ...), condition=%wide.region_26.28_spmd, body=%wide.region_19.27_spmd.sunk | while | flops 85977096 | bytes 368853 | solution.py:86
  404.4 14.9 %fusion.117 = (f32[1024]{0:T(1024)S(1)}, f32[1024]{0:T(1024)S(1)}, f32[1024]{0:T(1024)S(1)}, f32[1024]{0:T(1024)S(1)}, f32[1024]{0:T(1024)S(1)}, /*index=5*/f32[1024]{0:T(1024)S(1)}) fusion(f32[1024]{0:T(1024)S(1)} %bitcast.527, f32[2048]{0:T(1024)S(1)} %bitcast.475, f32[1024]{0:T(1024)S(1)} %bitcast.524, f32[2048]{0:T(1024)S(1)} %bitcast.478, ...), kind=kLoop, calls=%fused_computation.70.clone.1 | loop fusion | flops 85977088 | bytes 106496 | tf_op jit(solution)/shard_map/while/body/eval_jaxpr/reduce_sum | solution.py:46
  420.5 14.9 %fusion.117 = (f32[1024]{0:T(1024)S(1)}, f32[1024]{0:T(1024)S(1)}, f32[1024]{0:T(1024)S(1)}, f32[1024]{0:T(1024)S(1)}, f32[1024]{0:T(1024)S(1)}, /*index=5*/f32[1024]{0:T(1024)S(1)}) fusion(f32[1024]{0:T(1024)S(1)} %bitcast.527, f32[2048]{0:T(1024)S(1)} %bitcast.475, f32[1024]{0:T(1024)S(1)} %bitcast.524, f32[2048]{0:T(1024)S(1)} %bitcast.478, ...), kind=kLoop, calls=%fused_computation.70.clone.1 | loop fusion | flops 85977088 | bytes 106496 | tf_op jit(solution)/shard_map/while/body/eval_jaxpr/reduce_sum | solution.py:46
  436.6 14.9 %fusion.117 = (f32[1024]{0:T(1024)S(1)}, f32[1024]{0:T(1024)S(1)}, f32[1024]{0:T(1024)S(1)}, f32[1024]{0:T(1024)S(1)}, f32[1024]{0:T(1024)S(1)}, /*index=5*/f32[1024]{0:T(1024)S(1)}) fusion(f32[1024]{0:T(1024)S(1)} %bitcast.527, f32[2048]{0:T(1024)S(1)} %bitcast.475, f32[1024]{0:T(1024)S(1)} %bitcast.524, f32[2048]{0:T(1024)S(1)} %bitcast.478, ...), kind=kLoop, calls=%fused_computation.70.clone.1 | loop fusion | flops 85977088 | bytes 106496 | tf_op jit(solution)/shard_map/while/body/eval_jaxpr/reduce_sum | solution.py:46
  452.7 14.9 %fusion.117 = (f32[1024]{0:T(1024)S(1)}, f32[1024]{0:T(1024)S(1)}, f32[1024]{0:T(1024)S(1)}, f32[1024]{0:T(1024)S(1)}, f32[1024]{0:T(1024)S(1)}, /*index=5*/f32[1024]{0:T(1024)S(1)}) fusion(f32[1024]{0:T(1024)S(1)} %bitcast.527, f32[2048]{0:T(1024)S(1)} %bitcast.475, f32[1024]{0:T(1024)S(1)} %bitcast.524, f32[2048]{0:T(1024)S(1)} %bitcast.478, ...), kind=kLoop, calls=%fused_computation.70.clone.1 | loop fusion | flops 85977088 | bytes 106496 | tf_op jit(solution)/shard_map/while/body/eval_jaxpr/reduce_sum | solution.py:46
  468.4 100.7 %all-reduce.15.cloned.1.call-done = f32[6,32,128]{2,0,1:T(8,128)} async-done(((f32[6,32,128]{2,0,1:T(8,128)}), f32[6,32,128]{2,0,1:T(8,128)}) %all-reduce.15.cloned.1.call-update) | async-done | bytes 98320 | tf_op jit(solution)/shard_map/psum | solution.py:110
  587.3 102.6 %all-reduce.17.cloned.1.call-done = f32[4,6,1024]{2,1,0:T(8,128)} async-done(((f32[4,6,1024]{2,1,0:T(8,128)}), f32[4,6,1024]{2,1,0:T(8,128)}) %all-reduce.17.cloned.1.call-update) | async-done | bytes 98320 | tf_op jit(solution)/shard_map/psum | solution.py:108
  689.9 63.7 %while.42 = (s32[]{:T(128)}, f32[4,6,1024]{2,1,0:T(8,128)S(1)}, f32[2048]{0:T(1024)S(1)}, f32[3,2048]{1,0:T(4,128)S(1)}, f32[4,6,1024]{2,1,0:T(8,128)}, /*index=...) while((s32[]{:T(128)}, f32[4,6,1024]{2,1,0:T(8,128)S(1)}, ...), condition=%wide.region_40.42_spmd, body=%wide.region_33.41_spmd.sunk | while | flops 85977096 | bytes 368853 | solution.py:86
  754.4 100.7 %all-reduce.19.cloned.1.call-done = f32[6,32,128]{2,0,1:T(8,128)} async-done(((f32[6,32,128]{2,0,1:T(8,128)}), f32[6,32,128]{2,0,1:T(8,128)}) %all-reduce.19.cloned.1.call-update) | async-done | bytes 98320 | tf_op jit(solution)/shard_map/psum | solution.py:110
  873.5 102.4 %all-reduce.21.cloned.1.call-done = f32[4,6,1024]{2,1,0:T(8,128)} async-done(((f32[4,6,1024]{2,1,0:T(8,128)}), f32[4,6,1024]{2,1,0:T(8,128)}) %all-reduce.21.cloned.1.call-update) | async-done | bytes 98320 | tf_op jit(solution)/shard_map/psum | solution.py:108
  975.9 64.3 %while.43 = (s32[]{:T(128)}, f32[4,6,1024]{2,1,0:T(8,128)S(1)}, f32[2048]{0:T(1024)S(1)}, f32[3,2048]{1,0:T(4,128)S(1)}, f32[4,6,1024]{2,1,0:T(8,128)}, /*index=...) while((s32[]{:T(128)}, f32[4,6,1024]{2,1,0:T(8,128)S(1)}, ...), condition=%wide.region_54.56_spmd, body=%wide.region_47.55_spmd.sunk | while | flops 85977096 | bytes 368853 | solution.py:86
  977.0 14.9 %fusion.121 = (f32[1024]{0:T(1024)S(1)}, f32[1024]{0:T(1024)S(1)}, f32[1024]{0:T(1024)S(1)}, f32[1024]{0:T(1024)S(1)}, f32[1024]{0:T(1024)S(1)}, /*index=5*/f32[1024]{0:T(1024)S(1)}) fusion(f32[1024]{0:T(1024)S(1)} %bitcast.539, f32[2048]{0:T(1024)S(1)} %bitcast.487, f32[1024]{0:T(1024)S(1)} %bitcast.536, f32[2048]{0:T(1024)S(1)} %bitcast.490, ...), kind=kLoop, calls=%fused_computation.150.clone.1 | loop fusion | flops 85977088 | bytes 106496 | tf_op jit(solution)/shard_map/while/body/eval_jaxpr/reduce_sum | solution.py:46
  993.1 14.9 %fusion.121 = (f32[1024]{0:T(1024)S(1)}, f32[1024]{0:T(1024)S(1)}, f32[1024]{0:T(1024)S(1)}, f32[1024]{0:T(1024)S(1)}, f32[1024]{0:T(1024)S(1)}, /*index=5*/f32[1024]{0:T(1024)S(1)}) fusion(f32[1024]{0:T(1024)S(1)} %bitcast.539, f32[2048]{0:T(1024)S(1)} %bitcast.487, f32[1024]{0:T(1024)S(1)} %bitcast.536, f32[2048]{0:T(1024)S(1)} %bitcast.490, ...), kind=kLoop, calls=%fused_computation.150.clone.1 | loop fusion | flops 85977088 | bytes 106496 | tf_op jit(solution)/shard_map/while/body/eval_jaxpr/reduce_sum | solution.py:46
  1009.2 14.9 %fusion.121 = (f32[1024]{0:T(1024)S(1)}, f32[1024]{0:T(1024)S(1)}, f32[1024]{0:T(1024)S(1)}, f32[1024]{0:T(1024)S(1)}, f32[1024]{0:T(1024)S(1)}, /*index=5*/f32[1024]{0:T(1024)S(1)}) fusion(f32[1024]{0:T(1024)S(1)} %bitcast.539, f32[2048]{0:T(1024)S(1)} %bitcast.487, f32[1024]{0:T(1024)S(1)} %bitcast.536, f32[2048]{0:T(1024)S(1)} %bitcast.490, ...), kind=kLoop, calls=%fused_computation.150.clone.1 | loop fusion | flops 85977088 | bytes 106496 | tf_op jit(solution)/shard_map/while/body/eval_jaxpr/reduce_sum | solution.py:46
  1025.3 14.9 %fusion.121 = (f32[1024]{0:T(1024)S(1)}, f32[1024]{0:T(1024)S(1)}, f32[1024]{0:T(1024)S(1)}, f32[1024]{0:T(1024)S(1)}, f32[1024]{0:T(1024)S(1)}, /*index=5*/f32[1024]{0:T(1024)S(1)}) fusion(f32[1024]{0:T(1024)S(1)} %bitcast.539, f32[2048]{0:T(1024)S(1)} %bitcast.487, f32[1024]{0:T(1024)S(1)} %bitcast.536, f32[2048]{0:T(1024)S(1)} %bitcast.490, ...), kind=kLoop, calls=%fused_computation.150.clone.1 | loop fusion | flops 85977088 | bytes 106496 | tf_op jit(solution)/shard_map/while/body/eval_jaxpr/reduce_sum | solution.py:46
  1041.0 100.8 %all-reduce.23.cloned.1.call-done = f32[6,32,128]{2,0,1:T(8,128)} async-done(((f32[6,32,128]{2,0,1:T(8,128)}), f32[6,32,128]{2,0,1:T(8,128)}) %all-reduce.23.cloned.1.call-update) | async-done | bytes 98320 | tf_op jit(solution)/shard_map/psum | solution.py:110
  (180 shorter events, 157.5 us)
Async XLA Ops:
  7.2 108.5 %all-reduce.9.cloned.1.call-start = ((), (), s32[]{:S(2)}) async-start(), calls=%async_computation | async-start | bytes 262144 | tf_op jit(solution)/shard_map/psum | solution.py:108
  10.5 271.1 %all-reduce.11.cloned.1.call-start = ((), (), s32[]{:S(2)}) async-start(), calls=%async_computation.1 | async-start | bytes 262144 | tf_op jit(solution)/shard_map/psum | solution.py:110
  11.6 104.1 %copy-start.6 = (f32[2048]{0:T(1024)S(1)}, f32[2048]{0:T(1024)}, u32[]{:S(2)}) copy-start(f32[2048]{0:T(1024)} %param.16) | copy-start | bytes 24580
  180.1 0.7 copy-start.2
  180.7 222.6 %all-reduce.13.cloned.1.call-start = ((), (), s32[]{:S(2)}) async-start(), calls=%async_computation.2 | async-start | bytes 262144 | tf_op jit(solution)/shard_map/psum | solution.py:108
  284.3 14.0 %copy-start = (f32[6,2048]{1,0:T(8,128)S(1)}, f32[6,2048]{1,0:T(8,128)}, u32[]{:S(2)}) copy-start(f32[6,2048]{1,0:T(8,128)} %param.15) | copy-start | bytes 147460
  298.2 0.8 copy-start.1
  300.7 268.5 %all-reduce.15.cloned.1.call-start = ((), (), s32[]{:S(2)}) async-start(), calls=%async_computation.3 | async-start | bytes 262144 | tf_op jit(solution)/shard_map/psum | solution.py:110
  467.7 0.7 copy-start.3
  468.4 221.6 %all-reduce.17.cloned.1.call-start = ((), (), s32[]{:S(2)}) async-start(), calls=%async_computation.4 | async-start | bytes 262144 | tf_op jit(solution)/shard_map/psum | solution.py:108
  587.3 267.8 %all-reduce.19.cloned.1.call-start = ((), (), s32[]{:S(2)}) async-start(), calls=%async_computation.5 | async-start | bytes 262144 | tf_op jit(solution)/shard_map/psum | solution.py:110
  753.6 0.7 copy-start.4
  754.3 221.6 %all-reduce.21.cloned.1.call-start = ((), (), s32[]{:S(2)}) async-start(), calls=%async_computation.6 | async-start | bytes 262144 | tf_op jit(solution)/shard_map/psum | solution.py:108
  873.3 268.5 %all-reduce.23.cloned.1.call-start = ((), (), s32[]{:S(2)}) async-start(), calls=%async_computation.7 | async-start | bytes 262144 | tf_op jit(solution)/shard_map/psum | solution.py:110
  1040.3 0.7 copy-start.5
Sparse Core Ops, SparseCore 0:
  11.2 104.4 all-reduce.8
  180.9 100.6 all-reduce.10
  300.8 102.4 all-reduce.12
  468.5 100.6 all-reduce.14
  587.4 102.4 all-reduce.16
  754.4 100.6 all-reduce.18
  873.4 102.4 all-reduce.20
  1041.1 100.6 all-reduce.22
where the time goes:
time: 1170 us
  waiting for transfers between devices  815 us (70%)
  other arithmetic  256 us (22%)
  blocking collectives  55.2 us (5%)
  local copies, waits for them, and re-layouts  25.1 us (2%)
  between operations  14.7 us (1%)
    psum x4, waiting for transfers between devices, shards(): targets = lax.psum(picked, ('ja', 'ha'))  412 us
    psum x4, waiting for transfers between devices, shards(): totals = lax.psum(partial_terms, ('ja', 'ha'))  403 us
    reduce_sum x16, other arithmetic, pair_terms(): jnp.sum(inv_cube * (rel_z - radial * sep_z), axis=1)  238 us
    psum x4, blocking collectives, shards(): fresh = lax.psum(mine_terms, 'ia') + star_terms(predicted)  55.2 us
  transfers between devices with their start and end apart: 8, of which 8 were waited for; matrix products, arithmetic and copies ran while one was open for 0% of the time, Pallas kernels for 0%

commit v1 on v0

--- a/solution.py
+++ b/solution.py
@@ -76,51 +76,70 @@
     return jnp.concatenate([pos_new, vel_new], axis=0)
 
 
-def tile_forces(targets, field_rows, body_mass):
-    slot_count = targets.shape[1]
-    block_len = targets.shape[2]
-    group_width = math.gcd(slot_count, 8)
-    grouped = targets.reshape(6, slot_count // group_width, group_width * block_len).transpose(
-        1, 0, 2
-    )
-    results = lax.map(lambda tile_rows: pair_terms(tile_rows, field_rows, body_mass), grouped)
-    return results.transpose(1, 0, 2).reshape(6, slot_count, block_len)
+def field_forces(targets, field_rows, body_mass, chunks=4):
+    count = field_rows.shape[1]
+    width = count // chunks
+    rows = field_rows.reshape(6, chunks, width).transpose(1, 0, 2)
+    masses = body_mass.reshape(chunks, width)
+    parts = lax.map(lambda c: pair_terms(targets, c[0], c[1]), (rows, masses))
+    return jnp.sum(parts, axis=0)
 
 
 def shards(phase_space, derivatives, body_mass, active_lists):
-    local_count = phase_space.shape[1]
-    blocks_local = local_count // BLK
-    my_part = lax.axis_index("ja") * lax.axis_size("ha") + lax.axis_index("ha")
+    every = ("ia", "ja", "ha")
+    plane = ("ja", "ha")
+    local = jnp.concatenate([phase_space, derivatives, body_mass[None, :]], axis=0)
+    full = lax.all_gather(local, plane, axis=1, tiled=True)
+    phase = full[0:6]
+    deriv = full[6:12]
+    mass = full[12]
+    total = phase.shape[1]
+    block_total = total // BLK
+    slots = active_lists.shape[1] * active_lists.shape[2]
     my_group = lax.axis_index("ia")
-    own_blocks = my_part * blocks_local + jnp.arange(blocks_local, dtype=jnp.int32)
-    last_time = jnp.zeros((local_count,), jnp.float32)
+    my_slot = lax.axis_index("ja") * lax.axis_size("ha") + lax.axis_index("ha")
+    all_blocks = jnp.arange(block_total, dtype=jnp.int32)
+    last_blk = jnp.zeros((block_total,), jnp.float32)
     for step_index in range(STEPS):
         now_time = (step_index + 1) * time_step
         step_lists = active_lists[step_index]
-        elapsed = (now_time - last_time)[None, :]
-        predicted = predict(phase_space, derivatives, elapsed)
-        block_ids = lax.dynamic_index_in_dim(step_lists, my_group, 0, keepdims=False)
-        owner_part = block_ids // blocks_local
-        local_index = jnp.clip(block_ids - owner_part * blocks_local, 0, blocks_local - 1)
-        is_mine = (owner_part == my_part) & (block_ids >= 0)
-        picked = jnp.take(predicted.reshape(6, blocks_local, BLK), local_index, axis=1)
-        picked = jnp.where(is_mine[None, :, None], picked, 0.0)
-        targets = lax.psum(picked, ("ja", "ha"))
-        partial_terms = tile_forces(targets, predicted, body_mass)
-        totals = lax.psum(partial_terms, ("ja", "ha"))
-        kept_terms = jnp.where(is_mine[None, :, None], totals, 0.0)
-        mine_terms = (
-            jnp.zeros((6, blocks_local, BLK), jnp.float32).at[:, local_index].add(kept_terms)
+        flat = step_lists.reshape(-1)
+        elapsed_blk = now_time - last_blk
+        elapsed = jnp.repeat(elapsed_blk, BLK)[None, :]
+        predicted = predict(phase, deriv, elapsed)
+        my_id = step_lists[my_group, my_slot]
+        safe = jnp.clip(my_id, 0, block_total - 1)
+        start = safe * BLK
+        targets = lax.dynamic_slice_in_dim(predicted, start, BLK, axis=1)
+        mutual = field_forces(targets, predicted, mass)
+        fresh = mutual + star_terms(targets)
+        own_phase = lax.dynamic_slice_in_dim(phase, start, BLK, axis=1)
+        own_deriv = lax.dynamic_slice_in_dim(deriv, start, BLK, axis=1)
+        own_elapsed = lax.dynamic_slice_in_dim(elapsed, start, BLK, axis=1)
+        corrected = correct(own_phase, own_deriv, fresh, own_elapsed)
+        packed = jnp.concatenate([corrected, fresh], axis=0)
+        sent = jnp.broadcast_to(packed[None], (slots,) + packed.shape)
+        got = lax.all_to_all(sent, every, 0, 0, tiled=True)
+        ids = jnp.where(flat >= 0, flat, block_total)
+        phase = (
+            phase.reshape(6, block_total, BLK)
+            .at[:, ids]
+            .set(got[:, 0:6].transpose(1, 0, 2), mode="drop")
+            .reshape(6, total)
         )
-        mine_terms = mine_terms.reshape(6, local_count)
-        fresh = lax.psum(mine_terms, "ia") + star_terms(predicted)
-        active_flags = jnp.any(step_lists.reshape(-1)[:, None] == own_blocks[None, :], axis=0)
-        active = jnp.repeat(active_flags, BLK)[None, :]
-        corrected = correct(phase_space, derivatives, fresh, elapsed)
-        phase_space = jnp.where(active, corrected, phase_space)
-        derivatives = jnp.where(active, fresh, derivatives)
-        last_time = jnp.where(active[0], jnp.float32(now_time), last_time)
-    return (phase_space, derivatives)
+        deriv = (
+            deriv.reshape(6, block_total, BLK)
+            .at[:, ids]
+            .set(got[:, 6:12].transpose(1, 0, 2), mode="drop")
+            .reshape(6, total)
+        )
+        active_flags = jnp.any(flat[:, None] == all_blocks[None, :], axis=0)
+        last_blk = jnp.where(active_flags, jnp.float32(now_time), last_blk)
+    local_count = phase_space.shape[1]
+    offset = my_slot * local_count
+    phase_out = lax.dynamic_slice_in_dim(phase, offset, local_count, axis=1)
+    deriv_out = lax.dynamic_slice_in_dim(deriv, offset, local_count, axis=1)
+    return (phase_out, deriv_out)
 
 
 def solution(mesh):

time: 1170 us -> 642 us (0.55)
  waiting for transfers between devices: 815 us -> 115 us
  local copies, waits for them, and re-layouts: 25.1 us -> 161 us
  other arithmetic: 256 us -> 315 us
  blocking collectives: 55.2 us -> 0 us
  starting transfers between devices: 0.51 us -> 21.1 us
    psum x8 -> x0, waiting for transfers between devices: 815 us -> none  [the longest x4 412 us: shards(): targets = lax.psum(picked, ('ja', 'ha'))]
    scatter x0 -> x8, local copies, waits for them, and re-layouts: none -> 85.9 us  [the longest x4 53.7 us: shards(): deriv = deriv.reshape(6, block_total, BLK).at[:, ids].set(got[:, 6:12].tr...]
    all_to_all x0 -> x4, waiting for transfers between devices: none -> 66.7 us  [shards(): got = lax.all_to_all(sent, every, 0, 0, tiled=True)]
    reduce_sum x16, other arithmetic: 238 us -> 293 us  [pair_terms(): jnp.sum(inv_cube * (rel_z - radial * sep_z), axis=1)]
    psum x4 -> x0, blocking collectives: 55.2 us -> none  [shards(): fresh = lax.psum(mine_terms, 'ia') + star_terms(predicted)]
    all_gather x0 -> x1, waiting for transfers between devices: none -> 48.7 us  [shards(): full = lax.all_gather(local, plane, axis=1, tiled=True)]
    all_to_all x0 -> x4, starting transfers between devices: none -> 21.1 us  [shards(): got = lax.all_to_all(sent, every, 0, 0, tiled=True)]
    slice x0 -> x11, local copies, waits for them, and re-layouts: none -> 17.1 us  [the longest x3 9.31 us: predict(): jerk_old = derivatives[3:6]]
  transfers between devices with their start and end apart: 8 -> 5, of which waited for: 8 -> 5; matrix products, arithmetic and copies ran while one was open for 0% -> 2% of each run, Pallas kernels for 0% -> 0%
where the time goes in v1:
time: 642 us; the launch traced here: 630 us
  other arithmetic  315 us (49%)
  local copies, waits for them, and re-layouts  161 us (25%)
  waiting for transfers between devices  115 us (18%)
  starting transfers between devices  21.1 us (3%)
  between operations  17.3 us (3%)
    reduce_sum x16, other arithmetic, pair_terms(): jnp.sum(inv_cube * (rel_z - radial * sep_z), axis=1)  293 us
    all_to_all x4, waiting for transfers between devices, shards(): got = lax.all_to_all(sent, every, 0, 0, tiled=True)  66.7 us
    scatter x4, local copies, waits for them, and re-layouts, shards(): deriv = deriv.reshape(6, block_total, BLK).at[:, ids].set(got[:, 6:12].tr...  53.7 us
    all_gather x1, waiting for transfers between devices, shards(): full = lax.all_gather(local, plane, axis=1, tiled=True)  48.7 us
    slice x16, local copies, waits for them, and re-layouts, pair_terms(): rel_x = field_rows[3][None, :] - targets[3][:, None]  33.3 us
    scatter x4, local copies, waits for them, and re-layouts, shards(): phase = phase.reshape(6, block_total, BLK).at[:, ids].set(got[:, 0:6].tra...  32.2 us
    all_to_all x4, starting transfers between devices, shards(): got = lax.all_to_all(sent, every, 0, 0, tiled=True)  21.1 us
  transfers between devices with their start and end apart: 5, of which 5 were waited for; matrix products, arithmetic and copies ran while one was open for 2% of the time, Pallas kernels for 0%

profile of v1, /device:TPU:1, one launch (start us, length us, event | category | flops | bytes accessed | tf_op | source)
XLA Modules:
  0.0 630.0 jit_solution(8845861415480449810)
XLA Ops:
  11.4 48.7 %all-gather.2.cloned.1.call-done = f32[13,65536]{1,0:T(8,128)} async-done(((f32[13,2048]{1,0:T(8,128)}), f32[13,65536]{1,0:T(8,128)}) %all-gather.2.cloned.1.call-update) | async-done | bytes 3407888 | tf_op jit(solution)/shard_map/all_gather | solution.py:92
  68.3 75.3 %while.40 = (s32[]{:T(128)}, f32[4,6,128]{2,1,0:T(8,128)S(1)}, f32[4,16384]{1,0:T(4,128)S(1)}, f32[4,6,16384]{2,1,0:T(8,128)S(1)}, f32[6,128]{1,0:T(8,128)S(1)},...) while((s32[]{:T(128)}, f32[4,6,128]{2,1,0:T(8,128)S(1)}, ...), condition=%wide.region_7.8_spmd, body=%wide.region_0.7_spmd.sunk | while | flops 85982472 | bytes 1403089 | solution.py:84
  68.8 18.3 %fusion.125 = (f32[128]{0:T(128)S(1)}, f32[128]{0:T(128)S(1)}, f32[128]{0:T(128)S(1)}, f32[128]{0:T(128)S(1)}, f32[128]{0:T(128)S(1)}, /*index=5*/f32[128]{0:T(128)S(1)}) fusion(f32[128]{0:T(128)S(1)} %get-tuple-element.501, f32[16384]{0:T(1024)S(1)} %bitcast.426, f32[128]{0:T(128)S(1)} %get-tuple-element.503, f32[16384]{0:T(1024)S(1)} %bitcast.423, ...), kind=kLoop, calls=%fused_computation.30.clone.1 | loop fusion | flops 85982464 | bytes 464896 | tf_op jit(solution)/shard_map/while/body/eval_jaxpr/reduce_sum | solution.py:46
  87.6 18.3 %fusion.125 = (f32[128]{0:T(128)S(1)}, f32[128]{0:T(128)S(1)}, f32[128]{0:T(128)S(1)}, f32[128]{0:T(128)S(1)}, f32[128]{0:T(128)S(1)}, /*index=5*/f32[128]{0:T(128)S(1)}) fusion(f32[128]{0:T(128)S(1)} %get-tuple-element.501, f32[16384]{0:T(1024)S(1)} %bitcast.426, f32[128]{0:T(128)S(1)} %get-tuple-element.503, f32[16384]{0:T(1024)S(1)} %bitcast.423, ...), kind=kLoop, calls=%fused_computation.30.clone.1 | loop fusion | flops 85982464 | bytes 464896 | tf_op jit(solution)/shard_map/while/body/eval_jaxpr/reduce_sum | solution.py:46
  106.5 18.3 %fusion.125 = (f32[128]{0:T(128)S(1)}, f32[128]{0:T(128)S(1)}, f32[128]{0:T(128)S(1)}, f32[128]{0:T(128)S(1)}, f32[128]{0:T(128)S(1)}, /*index=5*/f32[128]{0:T(128)S(1)}) fusion(f32[128]{0:T(128)S(1)} %get-tuple-element.501, f32[16384]{0:T(1024)S(1)} %bitcast.426, f32[128]{0:T(128)S(1)} %get-tuple-element.503, f32[16384]{0:T(1024)S(1)} %bitcast.423, ...), kind=kLoop, calls=%fused_computation.30.clone.1 | loop fusion | flops 85982464 | bytes 464896 | tf_op jit(solution)/shard_map/while/body/eval_jaxpr/reduce_sum | solution.py:46
  125.3 18.3 %fusion.125 = (f32[128]{0:T(128)S(1)}, f32[128]{0:T(128)S(1)}, f32[128]{0:T(128)S(1)}, f32[128]{0:T(128)S(1)}, f32[128]{0:T(128)S(1)}, /*index=5*/f32[128]{0:T(128)S(1)}) fusion(f32[128]{0:T(128)S(1)} %get-tuple-element.501, f32[16384]{0:T(1024)S(1)} %bitcast.426, f32[128]{0:T(128)S(1)} %get-tuple-element.503, f32[16384]{0:T(1024)S(1)} %bitcast.423, ...), kind=kLoop, calls=%fused_computation.30.clone.1 | loop fusion | flops 85982464 | bytes 464896 | tf_op jit(solution)/shard_map/while/body/eval_jaxpr/reduce_sum | solution.py:46
  160.4 15.8 %all-to-all-done = f32[128,12,128]{2,1,0:T(8,128)S(1)} async-done(((f32[128,12,128]{2,1,0:T(8,128)}), f32[128,12,128]{2,1,0:T(8,128)S(1)}, u32[]{:S(2)}, u32[]{:S(2)}) %all-to-all-start) | async-done | bytes 786464 | tf_op jit(solution)/shard_map/all_to_all | solution.py:122
  207.0 84.5 %while.41 = (s32[]{:T(128)}, f32[4,6,128]{2,1,0:T(8,128)S(1)}, f32[4,16384]{1,0:T(4,128)S(1)}, f32[4,6,16384]{2,1,0:T(8,128)}, f32[6,128]{1,0:T(8,128)S(1)}, /*i...) while((s32[]{:T(128)}, f32[4,6,128]{2,1,0:T(8,128)S(1)}, ...), condition=%wide.region_21.22_spmd, body=%wide.region_14.21_spmd.sunk | while | flops 85982472 | bytes 1403089 | solution.py:84
  209.6 18.3 %fusion.126 = (f32[128]{0:T(128)S(1)}, f32[128]{0:T(128)S(1)}, f32[128]{0:T(128)S(1)}, f32[128]{0:T(128)S(1)}, f32[128]{0:T(128)S(1)}, /*index=5*/f32[128]{0:T(128)S(1)}) fusion(f32[128]{0:T(128)S(1)} %get-tuple-element.524, f32[16384]{0:T(1024)S(1)} %bitcast.432, f32[128]{0:T(128)S(1)} %get-tuple-element.526, f32[16384]{0:T(1024)S(1)} %bitcast.429, ...), kind=kLoop, calls=%fused_computation.77.clone.1 | loop fusion | flops 85982464 | bytes 464896 | tf_op jit(solution)/shard_map/while/body/eval_jaxpr/reduce_sum | solution.py:46
  230.9 18.3 %fusion.126 = (f32[128]{0:T(128)S(1)}, f32[128]{0:T(128)S(1)}, f32[128]{0:T(128)S(1)}, f32[128]{0:T(128)S(1)}, f32[128]{0:T(128)S(1)}, /*index=5*/f32[128]{0:T(128)S(1)}) fusion(f32[128]{0:T(128)S(1)} %get-tuple-element.524, f32[16384]{0:T(1024)S(1)} %bitcast.432, f32[128]{0:T(128)S(1)} %get-tuple-element.526, f32[16384]{0:T(1024)S(1)} %bitcast.429, ...), kind=kLoop, calls=%fused_computation.77.clone.1 | loop fusion | flops 85982464 | bytes 464896 | tf_op jit(solution)/shard_map/while/body/eval_jaxpr/reduce_sum | solution.py:46
  251.8 18.3 %fusion.126 = (f32[128]{0:T(128)S(1)}, f32[128]{0:T(128)S(1)}, f32[128]{0:T(128)S(1)}, f32[128]{0:T(128)S(1)}, f32[128]{0:T(128)S(1)}, /*index=5*/f32[128]{0:T(128)S(1)}) fusion(f32[128]{0:T(128)S(1)} %get-tuple-element.524, f32[16384]{0:T(1024)S(1)} %bitcast.432, f32[128]{0:T(128)S(1)} %get-tuple-element.526, f32[16384]{0:T(1024)S(1)} %bitcast.429, ...), kind=kLoop, calls=%fused_computation.77.clone.1 | loop fusion | flops 85982464 | bytes 464896 | tf_op jit(solution)/shard_map/while/body/eval_jaxpr/reduce_sum | solution.py:46
  273.2 18.3 %fusion.126 = (f32[128]{0:T(128)S(1)}, f32[128]{0:T(128)S(1)}, f32[128]{0:T(128)S(1)}, f32[128]{0:T(128)S(1)}, f32[128]{0:T(128)S(1)}, /*index=5*/f32[128]{0:T(128)S(1)}) fusion(f32[128]{0:T(128)S(1)} %get-tuple-element.524, f32[16384]{0:T(1024)S(1)} %bitcast.432, f32[128]{0:T(128)S(1)} %get-tuple-element.526, f32[16384]{0:T(1024)S(1)} %bitcast.429, ...), kind=kLoop, calls=%fused_computation.77.clone.1 | loop fusion | flops 85982464 | bytes 464896 | tf_op jit(solution)/shard_map/while/body/eval_jaxpr/reduce_sum | solution.py:46
  348.1 84.7 %while.42 = (s32[]{:T(128)}, f32[4,6,128]{2,1,0:T(8,128)S(1)}, f32[4,16384]{1,0:T(4,128)S(1)}, f32[4,6,16384]{2,1,0:T(8,128)}, f32[6,128]{1,0:T(8,128)S(1)}, /*i...) while((s32[]{:T(128)}, f32[4,6,128]{2,1,0:T(8,128)S(1)}, ...), condition=%wide.region_35.36_spmd, body=%wide.region_28.35_spmd.sunk | while | flops 85982472 | bytes 1403089 | solution.py:84
  350.8 18.3 %fusion.127 = (f32[128]{0:T(128)S(1)}, f32[128]{0:T(128)S(1)}, f32[128]{0:T(128)S(1)}, f32[128]{0:T(128)S(1)}, f32[128]{0:T(128)S(1)}, /*index=5*/f32[128]{0:T(128)S(1)}) fusion(f32[128]{0:T(128)S(1)} %get-tuple-element.547, f32[16384]{0:T(1024)S(1)} %bitcast.438, f32[128]{0:T(128)S(1)} %get-tuple-element.549, f32[16384]{0:T(1024)S(1)} %bitcast.435, ...), kind=kLoop, calls=%fused_computation.124.clone.1 | loop fusion | flops 85982464 | bytes 464896 | tf_op jit(solution)/shard_map/while/body/eval_jaxpr/reduce_sum | solution.py:46
  372.0 18.3 %fusion.127 = (f32[128]{0:T(128)S(1)}, f32[128]{0:T(128)S(1)}, f32[128]{0:T(128)S(1)}, f32[128]{0:T(128)S(1)}, f32[128]{0:T(128)S(1)}, /*index=5*/f32[128]{0:T(128)S(1)}) fusion(f32[128]{0:T(128)S(1)} %get-tuple-element.547, f32[16384]{0:T(1024)S(1)} %bitcast.438, f32[128]{0:T(128)S(1)} %get-tuple-element.549, f32[16384]{0:T(1024)S(1)} %bitcast.435, ...), kind=kLoop, calls=%fused_computation.124.clone.1 | loop fusion | flops 85982464 | bytes 464896 | tf_op jit(solution)/shard_map/while/body/eval_jaxpr/reduce_sum | solution.py:46
  393.0 18.3 %fusion.127 = (f32[128]{0:T(128)S(1)}, f32[128]{0:T(128)S(1)}, f32[128]{0:T(128)S(1)}, f32[128]{0:T(128)S(1)}, f32[128]{0:T(128)S(1)}, /*index=5*/f32[128]{0:T(128)S(1)}) fusion(f32[128]{0:T(128)S(1)} %get-tuple-element.547, f32[16384]{0:T(1024)S(1)} %bitcast.438, f32[128]{0:T(128)S(1)} %get-tuple-element.549, f32[16384]{0:T(1024)S(1)} %bitcast.435, ...), kind=kLoop, calls=%fused_computation.124.clone.1 | loop fusion | flops 85982464 | bytes 464896 | tf_op jit(solution)/shard_map/while/body/eval_jaxpr/reduce_sum | solution.py:46
  414.3 18.3 %fusion.127 = (f32[128]{0:T(128)S(1)}, f32[128]{0:T(128)S(1)}, f32[128]{0:T(128)S(1)}, f32[128]{0:T(128)S(1)}, f32[128]{0:T(128)S(1)}, /*index=5*/f32[128]{0:T(128)S(1)}) fusion(f32[128]{0:T(128)S(1)} %get-tuple-element.547, f32[16384]{0:T(1024)S(1)} %bitcast.438, f32[128]{0:T(128)S(1)} %get-tuple-element.549, f32[16384]{0:T(1024)S(1)} %bitcast.435, ...), kind=kLoop, calls=%fused_computation.124.clone.1 | loop fusion | flops 85982464 | bytes 464896 | tf_op jit(solution)/shard_map/while/body/eval_jaxpr/reduce_sum | solution.py:46
  442.4 16.0 %all-to-all-done.2 = f32[128,12,128]{2,1,0:T(8,128)S(1)} async-done(((f32[128,12,128]{2,1,0:T(8,128)}), f32[128,12,128]{2,1,0:T(8,128)S(1)}, u32[]{:S(2)}, u32[]{:S(2)}) %all-to-all-start.2) | async-done | bytes 786464 | tf_op jit(solution)/shard_map/all_to_all | solution.py:122
  487.3 84.5 %while.43 = (s32[]{:T(128)}, f32[4,6,128]{2,1,0:T(8,128)S(1)}, f32[4,16384]{1,0:T(4,128)S(1)}, f32[4,6,16384]{2,1,0:T(8,128)}, f32[6,128]{1,0:T(8,128)S(1)}, /*i...) while((s32[]{:T(128)}, f32[4,6,128]{2,1,0:T(8,128)S(1)}, ...), condition=%wide.region_49.50_spmd, body=%wide.region_42.49_spmd.sunk | while | flops 85982472 | bytes 1403089 | solution.py:84
  489.9 18.3 %fusion.128 = (f32[128]{0:T(128)S(1)}, f32[128]{0:T(128)S(1)}, f32[128]{0:T(128)S(1)}, f32[128]{0:T(128)S(1)}, f32[128]{0:T(128)S(1)}, /*index=5*/f32[128]{0:T(128)S(1)}) fusion(f32[128]{0:T(128)S(1)} %get-tuple-element.570, f32[16384]{0:T(1024)S(1)} %bitcast.444, f32[128]{0:T(128)S(1)} %get-tuple-element.572, f32[16384]{0:T(1024)S(1)} %bitcast.441, ...), kind=kLoop, calls=%fused_computation.171.clone.1 | loop fusion | flops 85982464 | bytes 464896 | tf_op jit(solution)/shard_map/while/body/eval_jaxpr/reduce_sum | solution.py:46
  511.2 18.3 %fusion.128 = (f32[128]{0:T(128)S(1)}, f32[128]{0:T(128)S(1)}, f32[128]{0:T(128)S(1)}, f32[128]{0:T(128)S(1)}, f32[128]{0:T(128)S(1)}, /*index=5*/f32[128]{0:T(128)S(1)}) fusion(f32[128]{0:T(128)S(1)} %get-tuple-element.570, f32[16384]{0:T(1024)S(1)} %bitcast.444, f32[128]{0:T(128)S(1)} %get-tuple-element.572, f32[16384]{0:T(1024)S(1)} %bitcast.441, ...), kind=kLoop, calls=%fused_computation.171.clone.1 | loop fusion | flops 85982464 | bytes 464896 | tf_op jit(solution)/shard_map/while/body/eval_jaxpr/reduce_sum | solution.py:46
  532.1 18.3 %fusion.128 = (f32[128]{0:T(128)S(1)}, f32[128]{0:T(128)S(1)}, f32[128]{0:T(128)S(1)}, f32[128]{0:T(128)S(1)}, f32[128]{0:T(128)S(1)}, /*index=5*/f32[128]{0:T(128)S(1)}) fusion(f32[128]{0:T(128)S(1)} %get-tuple-element.570, f32[16384]{0:T(1024)S(1)} %bitcast.444, f32[128]{0:T(128)S(1)} %get-tuple-element.572, f32[16384]{0:T(1024)S(1)} %bitcast.441, ...), kind=kLoop, calls=%fused_computation.171.clone.1 | loop fusion | flops 85982464 | bytes 464896 | tf_op jit(solution)/shard_map/while/body/eval_jaxpr/reduce_sum | solution.py:46
  553.4 18.3 %fusion.128 = (f32[128]{0:T(128)S(1)}, f32[128]{0:T(128)S(1)}, f32[128]{0:T(128)S(1)}, f32[128]{0:T(128)S(1)}, f32[128]{0:T(128)S(1)}, /*index=5*/f32[128]{0:T(128)S(1)}) fusion(f32[128]{0:T(128)S(1)} %get-tuple-element.570, f32[16384]{0:T(1024)S(1)} %bitcast.444, f32[128]{0:T(128)S(1)} %get-tuple-element.572, f32[16384]{0:T(1024)S(1)} %bitcast.441, ...), kind=kLoop, calls=%fused_computation.171.clone.1 | loop fusion | flops 85982464 | bytes 464896 | tf_op jit(solution)/shard_map/while/body/eval_jaxpr/reduce_sum | solution.py:46
  578.2 19.2 %all-to-all-done.3 = f32[128,12,128]{2,1,0:T(8,128)S(1)} async-done(((f32[128,12,128]{2,1,0:T(8,128)}), f32[128,12,128]{2,1,0:T(8,128)S(1)}, u32[]{:S(2)}, u32[]{:S(2)}) %all-to-all-start.3) | async-done | bytes 786464 | tf_op jit(solution)/shard_map/all_to_all | solution.py:122
  (221 shorter events, 218.9 us)
Async XLA Ops:
  7.2 52.9 %all-gather.2.cloned.1.call-start = ((), (), s32[]{:S(2)}) async-start(), calls=%async_computation.4 | async-start | bytes 4325376 | tf_op jit(solution)/shard_map/all_gather | solution.py:92
  149.6 26.6 %all-to-all-start = ((f32[128,12,128]{2,1,0:T(8,128)}), f32[128,12,128]{2,1,0:T(8,128)S(1)}, u32[]{:S(2)}, u32[]{:S(2)}) async-start(f32[128,12,128]{2,1,0:T(8,128)} %broadcast_in_dim.106), calls=%async_computation | async-start | bytes 2097152 | tf_op jit(solution)/shard_map/all_to_all | solution.py:122
  201.5 1.6 copy-start
  201.5 1.6 copy-start.6
  203.1 1.2 copy-start.3
  203.1 1.3 copy-start.7
  293.4 24.1 %all-to-all-start.1 = ((f32[128,12,128]{2,1,0:T(8,128)}), f32[128,12,128]{2,1,0:T(8,128)S(1)}, u32[]{:S(2)}, u32[]{:S(2)}) async-start(f32[128,12,128]{2,1,0:T(8,128)} %broadcast_in_dim.112), calls=%async_computation.1 | async-start | bytes 2097152 | tf_op jit(solution)/shard_map/all_to_all | solution.py:122
  341.0 3.3 copy-start.1
  341.0 3.3 copy-start.5
  344.2 1.2 copy-start.9
  434.7 23.8 %all-to-all-start.2 = ((f32[128,12,128]{2,1,0:T(8,128)}), f32[128,12,128]{2,1,0:T(8,128)S(1)}, u32[]{:S(2)}, u32[]{:S(2)}) async-start(f32[128,12,128]{2,1,0:T(8,128)} %broadcast_in_dim.116), calls=%async_computation.2 | async-start | bytes 2097152 | tf_op jit(solution)/shard_map/all_to_all | solution.py:122
  480.1 3.3 copy-start.2
  480.1 3.3 copy-start.4
  483.4 1.2 copy-start.8
  573.6 23.8 %all-to-all-start.3 = ((f32[128,12,128]{2,1,0:T(8,128)}), f32[128,12,128]{2,1,0:T(8,128)S(1)}, u32[]{:S(2)}, u32[]{:S(2)}) async-start(f32[128,12,128]{2,1,0:T(8,128)} %broadcast_in_dim.120), calls=%async_computation.3 | async-start | bytes 2097152 | tf_op jit(solution)/shard_map/all_to_all | solution.py:122
Sparse Core Ops, SparseCore 0:
  10.3 49.7 all-gather.1

commit v2 on v1

v2 whole, which is shorter than its diff:
```python
import math

import jax
import jax.numpy as jnp
from jax import lax
from jax.sharding import PartitionSpec as P
from jax.experimental import pallas as pl
from jax.experimental.pallas import tpu as pltpu

BLK = 128
STEPS = 4


time_step = 0.02
soften_sq = 0.0025


def predict(phase_space, derivatives, elapsed):
    position = phase_space[0:3]
    velocity = phase_space[3:6]
    acceleration = derivatives[0:3]
    jerk_old = derivatives[3:6]
    pos_next = position + elapsed * (
        velocity + elapsed * (acceleration * 0.5 + elapsed * jerk_old / 6.0)
    )
    vel_next = velocity + elapsed * (acceleration + elapsed * jerk_old * 0.5)
    return jnp.concatenate([pos_next, vel_next], axis=0)


def pair_terms(targets, field_rows, body_mass):
    sep_x = field_rows[0][:, None] - targets[0][None, :]
    sep_y = field_rows[1][:, None] - targets[1][None, :]
    sep_z = field_rows[2][:, None] - targets[2][None, :]
    rel_x = field_rows[3][:, None] - targets[3][None, :]
    rel_y = field_rows[4][:, None] - targets[4][None, :]
    rel_z = field_rows[5][:, None] - targets[5][None, :]
    dist_sq = sep_x * sep_x + sep_y * sep_y + sep_z * sep_z + soften_sq
    inv_r = lax.rsqrt(dist_sq)
    inv_cube = body_mass[:, None] * inv_r * inv_r * inv_r
    radial = 3.0 * (sep_x * rel_x + sep_y * rel_y + sep_z * rel_z) * inv_r * inv_r
    return jnp.stack(
        [
            jnp.sum(inv_cube * sep_x, axis=0),
            jnp.sum(inv_cube * sep_y, axis=0),
            jnp.sum(inv_cube * sep_z, axis=0),
            jnp.sum(inv_cube * (rel_x - radial * sep_x), axis=0),
            jnp.sum(inv_cube * (rel_y - radial * sep_y), axis=0),
            jnp.sum(inv_cube * (rel_z - radial * sep_z), axis=0),
        ],
        axis=0,
    )


def star_terms(predicted):
    position = predicted[0:3]
    velocity = predicted[3:6]
    inv_r = lax.rsqrt(jnp.sum(position * position, axis=0))
    inv_cube = inv_r * inv_r * inv_r
    radial = 3.0 * jnp.sum(position * velocity, axis=0) * inv_r * inv_r
    accel = -inv_cube[None, :] * position
    jerk_star = -inv_cube[None, :] * (velocity - radial[None, :] * position)
    return jnp.concatenate([accel, jerk_star], axis=0)


def correct(phase_space, derivatives, fresh, elapsed):
    half_dt = 0.5 * elapsed
    twelfth = elapsed * elapsed / 12.0
    vel_new = (
        phase_space[3:6]
        + half_dt * (derivatives[0:3] + fresh[0:3])
        + twelfth * (derivatives[3:6] - fresh[3:6])
    )
    pos_new = (
        phase_space[0:3]
        + half_dt * (phase_space[3:6] + vel_new)
        + twelfth * (derivatives[0:3] - fresh[0:3])
    )
    return jnp.concatenate([pos_new, vel_new], axis=0)


def field_forces(targets, field_rows, body_mass, first, count, chunks=4):
    width = field_rows.shape[1] // chunks

    def body(i, acc):
        at = (first + i) * width
        rows = lax.dynamic_slice_in_dim(field_rows, at, width, axis=1)
        masses = lax.dynamic_slice_in_dim(body_mass, at, width, axis=0)
        return acc + pair_terms(targets, rows, masses)

    return lax.fori_loop(0, count, body, jnp.zeros((6, targets.shape[1]), jnp.float32))


def shards(phase_space, derivatives, body_mass, active_lists):
    every = ("ia", "ja", "ha")
    plane = ("ja", "ha")
    chunks = 4
    local = jnp.concatenate([phase_space, derivatives, body_mass[None, :]], axis=0)
    full = lax.all_gather(local, plane, axis=1, tiled=True)
    total = full.shape[1]
    mass = full[12]
    phase = full[0:6]
    deriv = full[6:12]
    block_total = total // BLK
    slots = active_lists.shape[1] * active_lists.shape[2]
    my_unit = (
        lax.axis_index("ia") * lax.axis_size("ja") + lax.axis_index("ja")
    ) * lax.axis_size("ha") + lax.axis_index("ha")
    all_blocks = jnp.arange(block_total, dtype=jnp.int32)
    units = jnp.arange(slots, dtype=jnp.int32)
    last_blk = jnp.zeros((block_total,), jnp.float32)
    for step_index in range(STEPS):
        now_time = (step_index + 1) * time_step
        flat = active_lists[step_index].reshape(-1)
        live = flat >= 0
        live_count = jnp.sum(live.astype(jnp.int32))
        rank = jnp.cumsum(live.astype(jnp.int32)) - 1
        compact = (
            jnp.zeros((slots,), jnp.int32)
            .at[jnp.where(live, rank, slots)]
            .set(flat, mode="drop")
        )
        split = jnp.where(
            live_count * 4 <= slots, 4, jnp.where(live_count * 2 <= slots, 2, 1)
        ).astype(jnp.int32)
        elapsed_blk = now_time - last_blk
        elapsed = jnp.repeat(elapsed_blk, BLK)[None, :]
        predicted = predict(phase, deriv, elapsed)
        my_job = my_unit // split
        my_part = my_unit - my_job * split
        my_id = jnp.clip(compact[jnp.clip(my_job, 0, slots - 1)], 0, block_total - 1)
        span = chunks // split
        count = jnp.where(my_job < live_count, span, 0)
        targets = lax.dynamic_slice_in_dim(predicted, my_id * BLK, BLK, axis=1)
        partial = field_forces(targets, predicted, mass, my_part * span, count, chunks)
        sent = jnp.broadcast_to(partial[None], (slots,) + partial.shape)
        got = lax.all_to_all(sent, every, 0, 0, tiled=True)
        job_of = units // split
        owner = jnp.where(job_of < live_count, compact[jnp.clip(job_of, 0, slots - 1)], -1)
        onehot = (all_blocks[:, None] == owner[None, :]).astype(jnp.float32)
        mutual = jnp.einsum(
            "bu,ucl->cbl", onehot, got, precision=lax.Precision.HIGHEST,
            preferred_element_type=jnp.float32,
        ).reshape(6, total)
        fresh = mutual + star_terms(predicted)
        corrected = correct(phase, deriv, fresh, elapsed)
        active_flags = jnp.any(flat[:, None] == all_blocks[None, :], axis=0)
        active = jnp.repeat(active_flags, BLK)[None, :]
        phase = jnp.where(active, corrected, phase)
        deriv = jnp.where(active, fresh, deriv)
        last_blk = jnp.where(active_flags, jnp.float32(now_time), last_blk)
    local_count = phase_space.shape[1]
    offset = (lax.axis_index("ja") * lax.axis_size("ha") + lax.axis_index("ha")) * local_count
    phase_out = lax.dynamic_slice_in_dim(phase, offset, local_count, axis=1)
    deriv_out = lax.dynamic_slice_in_dim(deriv, offset, local_count, axis=1)
    return (phase_out, deriv_out)


def solution(mesh):
    return jax.shard_map(
        shards,
        mesh=mesh,
        in_specs=(P(None, ("ja", "ha")), P(None, ("ja", "ha")), P(("ja", "ha")), P()),
        out_specs=(P(None, ("ja", "ha")), P(None, ("ja", "ha"))),
        check_vma=False,
    )
```

time: 642 us -> 465 us (0.72); the launches traced: 630 us -> 460 us
  local copies, waits for them, and re-layouts: 161 us -> 68.3 us
  waiting for transfers between devices: 115 us -> 56.9 us
  other arithmetic: 315 us -> 273 us
  matrix products: 0 us -> 9.83 us
  between operations: 17.3 us -> 25.2 us
    reduce_sum x20 -> x13, other arithmetic: 293 us -> 202 us  [the longest x12 200 us: pair_terms(): jnp.sum(inv_cube * (rel_z - radial * sep_z), axis=0)]
    scatter x8 -> x4, local copies, waits for them, and re-layouts: 85.9 us -> 4.11 us  [shards(): compact = jnp.zeros((slots,), jnp.int32).at[jnp.where(live, rank, slots)]...]
    all_gather x1, waiting for transfers between devices: 48.7 us -> 13.7 us  [shards(): full = lax.all_gather(local, plane, axis=1, tiled=True)]
    all_to_all x4, waiting for transfers between devices: 66.7 us -> 43.2 us  [shards(): got = lax.all_to_all(sent, every, 0, 0, tiled=True)]
    select_n x4 -> x19, other arithmetic: 0.02 us -> 21.1 us  [the longest x4 12.6 us: shards(): deriv = jnp.where(active, fresh, deriv)]
    reduce_sum x4, other arithmetic: 0.09 us -> 20.1 us  [star_terms(): inv_r = lax.rsqrt(jnp.sum(position * position, axis=0))]
    slice x27 -> x12, local copies, waits for them, and re-layouts: 48.8 us -> 37.2 us  [pair_terms(): rel_x = field_rows[3][:, None] - targets[3][None, :]]
    dot_general x0 -> x4, matrix products: none -> 9.83 us  [shards(): jnp.einsum('bu,ucl->cbl', onehot, got, precision=lax.Precision.HIGHEST, p...]
  transfers between devices with their start and end apart: 5 -> 5, of which waited for: 5 -> 5; matrix products, arithmetic and copies ran while one was open for 2% -> 8% of each run, Pallas kernels for 0% -> 0%
where the time goes in v2:
time: 465 us; the launch traced here: 460 us
  other arithmetic  273 us (59%)
  local copies, waits for them, and re-layouts  68.3 us (15%)
  waiting for transfers between devices  56.9 us (12%)
  starting transfers between devices  25.6 us (6%)
  between operations  25.2 us (5%)
  matrix products  9.83 us (2%)
    reduce_sum x12, other arithmetic, pair_terms(): jnp.sum(inv_cube * (rel_z - radial * sep_z), axis=0)  200 us
    all_to_all x4, waiting for transfers between devices, shards(): got = lax.all_to_all(sent, every, 0, 0, tiled=True)  43.2 us
    slice x12, local copies, waits for them, and re-layouts, pair_terms(): rel_x = field_rows[3][:, None] - targets[3][None, :]  37.2 us
    all_to_all x4, starting transfers between devices, shards(): got = lax.all_to_all(sent, every, 0, 0, tiled=True)  25.6 us
    reduce_sum x4, other arithmetic, star_terms(): inv_r = lax.rsqrt(jnp.sum(position * position, axis=0))  20.1 us
    all_gather x1, waiting for transfers between devices, shards(): full = lax.all_gather(local, plane, axis=1, tiled=True)  13.7 us
    select_n x4, other arithmetic, shards(): deriv = jnp.where(active, fresh, deriv)  12.6 us
    dot_general x4, matrix products, shards(): jnp.einsum('bu,ucl->cbl', onehot, got, precision=lax.Precision.HIGHEST, p...  9.83 us
  transfers between devices with their start and end apart: 5, of which 5 were waited for; matrix products, arithmetic and copies ran while one was open for 8% of the time, Pallas kernels for 0%

profile of v2, /device:TPU:1, one launch (start us, length us, event | category | flops | bytes accessed | tf_op | source)
XLA Modules:
  0.0 459.7 jit_solution(5000488301943143734)
XLA Ops:
  46.7 13.7 %all-gather.2.cloned.1.call-done = f32[13,65536]{1,0:T(8,128)} async-done(((f32[13,2048]{1,0:T(8,128)}), f32[13,65536]{1,0:T(8,128)}) %all-gather.2.cloned.1.call-update) | async-done | bytes 3407888 | tf_op jit(solution)/shard_map/all_gather | solution.py:98
  60.4 6.7 %multiply_reduce_fusion.7 = (f32[65536]{0:T(1024)S(1)}, f32[65536]{0:T(1024)S(1)}, f32[3,65536]{1,0:T(4,128)S(1)}, f32[3,65536]{1,0:T(4,128)S(1)}) fusion(f32[13,65536]{1,0:T(8,128)} %all-gather.2.cloned.1.call-done), kind=kLoop, calls=%fused_computation.227 | loop fusion | flops 2818048 | bytes 5242880 | tf_op jit(solution)/shard_map/reduce_sum | solution.py:57
  70.7 39.8 %while.40 = (s32[]{:T(128)}, f32[6,128]{1,0:T(8,128)S(1)}, s32[]{:T(128)}, s32[]{:T(128)}, f32[65536]{0:T(1024)S(1)}, /*index=5*/f32[6,65536]{1,0:T(8,128)}, f32...) while((s32[]{:T(128)}, f32[6,128]{1,0:T(8,128)S(1)}, ...), condition=%wide.region_14.15_spmd, body=%wide.region_7.14_spmd.sunk | while | flops 85983240 | bytes 1404199 | solution.py:90
  73.8 16.7 %fusion.152 = (f32[128]{0:T(128)S(1)}, f32[128]{0:T(128)S(1)}, f32[128]{0:T(128)S(1)}, f32[128]{0:T(128)S(1)}, f32[128]{0:T(128)S(1)}, /*index=5*/f32[128]{0:T(128)S(1)}) fusion(f32[128]{0:T(128)S(1)} %get-tuple-element.592, f32[16384]{0:T(1024)S(1)} %bitcast.277, f32[128]{0:T(128)S(1)} %get-tuple-element.594, f32[16384]{0:T(1024)S(1)} %bitcast.274, ...), kind=kLoop, calls=%fused_computation.30.clone.1 | loop fusion | flops 85982464 | bytes 464896 | tf_op jit(solution)/shard_map/while/body/reduce_sum | solution.py:48
  93.8 16.7 %fusion.152 = (f32[128]{0:T(128)S(1)}, f32[128]{0:T(128)S(1)}, f32[128]{0:T(128)S(1)}, f32[128]{0:T(128)S(1)}, f32[128]{0:T(128)S(1)}, /*index=5*/f32[128]{0:T(128)S(1)}) fusion(f32[128]{0:T(128)S(1)} %get-tuple-element.592, f32[16384]{0:T(1024)S(1)} %bitcast.277, f32[128]{0:T(128)S(1)} %get-tuple-element.594, f32[16384]{0:T(1024)S(1)} %bitcast.274, ...), kind=kLoop, calls=%fused_computation.30.clone.1 | loop fusion | flops 85982464 | bytes 464896 | tf_op jit(solution)/shard_map/while/body/reduce_sum | solution.py:48
  111.4 8.1 %all-to-all-start = ((f32[128,6,128]{2,1,0:T(8,128)}), f32[128,6,128]{2,1,0:T(8,128)}, u32[]{:S(2)}, u32[]{:S(2)}) async-start(f32[128,6,128]{2,1,0:T(8,128)} %broadcast_in_dim.161), calls=%async_computation | async-start | bytes 1048576 | tf_op jit(solution)/shard_map/all_to_all | solution.py:136
  121.5 11.1 %all-to-all-done = f32[128,6,128]{2,1,0:T(8,128)} async-done(((f32[128,6,128]{2,1,0:T(8,128)}), f32[128,6,128]{2,1,0:T(8,128)}, u32[]{:S(2)}, u32[]{:S(2)}) %all-to-all-start) | async-done | bytes 393248 | tf_op jit(solution)/shard_map/all_to_all | solution.py:136
  147.9 79.6 %while.41 = (s32[]{:T(128)}, f32[6,128]{1,0:T(8,128)S(1)}, s32[]{:T(128)}, s32[]{:T(128)}, f32[65536]{0:T(1024)S(1)}, /*index=5*/f32[6,65536]{1,0:T(8,128)}, f32...) while((s32[]{:T(128)}, f32[6,128]{1,0:T(8,128)S(1)}, ...), condition=%wide.region_27.28_spmd, body=%wide.region_20.27_spmd.sunk | while | flops 85983240 | bytes 1404199 | solution.py:90
  150.7 16.7 %fusion.154 = (f32[128]{0:T(128)S(1)}, f32[128]{0:T(128)S(1)}, f32[128]{0:T(128)S(1)}, f32[128]{0:T(128)S(1)}, f32[128]{0:T(128)S(1)}, /*index=5*/f32[128]{0:T(128)S(1)}) fusion(f32[128]{0:T(128)S(1)} %get-tuple-element.617, f32[16384]{0:T(1024)S(1)} %bitcast.283, f32[128]{0:T(128)S(1)} %get-tuple-element.619, f32[16384]{0:T(1024)S(1)} %bitcast.280, ...), kind=kLoop, calls=%fused_computation.70.clone.1 | loop fusion | flops 85982464 | bytes 464896 | tf_op jit(solution)/shard_map/while/body/reduce_sum | solution.py:48
  170.9 16.7 %fusion.154 = (f32[128]{0:T(128)S(1)}, f32[128]{0:T(128)S(1)}, f32[128]{0:T(128)S(1)}, f32[128]{0:T(128)S(1)}, f32[128]{0:T(128)S(1)}, /*index=5*/f32[128]{0:T(128)S(1)}) fusion(f32[128]{0:T(128)S(1)} %get-tuple-element.617, f32[16384]{0:T(1024)S(1)} %bitcast.283, f32[128]{0:T(128)S(1)} %get-tuple-element.619, f32[16384]{0:T(1024)S(1)} %bitcast.280, ...), kind=kLoop, calls=%fused_computation.70.clone.1 | loop fusion | flops 85982464 | bytes 464896 | tf_op jit(solution)/shard_map/while/body/reduce_sum | solution.py:48
  190.9 16.7 %fusion.154 = (f32[128]{0:T(128)S(1)}, f32[128]{0:T(128)S(1)}, f32[128]{0:T(128)S(1)}, f32[128]{0:T(128)S(1)}, f32[128]{0:T(128)S(1)}, /*index=5*/f32[128]{0:T(128)S(1)}) fusion(f32[128]{0:T(128)S(1)} %get-tuple-element.617, f32[16384]{0:T(1024)S(1)} %bitcast.283, f32[128]{0:T(128)S(1)} %get-tuple-element.619, f32[16384]{0:T(1024)S(1)} %bitcast.280, ...), kind=kLoop, calls=%fused_computation.70.clone.1 | loop fusion | flops 85982464 | bytes 464896 | tf_op jit(solution)/shard_map/while/body/reduce_sum | solution.py:48
  210.7 16.7 %fusion.154 = (f32[128]{0:T(128)S(1)}, f32[128]{0:T(128)S(1)}, f32[128]{0:T(128)S(1)}, f32[128]{0:T(128)S(1)}, f32[128]{0:T(128)S(1)}, /*index=5*/f32[128]{0:T(128)S(1)}) fusion(f32[128]{0:T(128)S(1)} %get-tuple-element.617, f32[16384]{0:T(1024)S(1)} %bitcast.283, f32[128]{0:T(128)S(1)} %get-tuple-element.619, f32[16384]{0:T(1024)S(1)} %bitcast.280, ...), kind=kLoop, calls=%fused_computation.70.clone.1 | loop fusion | flops 85982464 | bytes 464896 | tf_op jit(solution)/shard_map/while/body/reduce_sum | solution.py:48
  228.3 6.0 %all-to-all-start.1 = ((f32[128,6,128]{2,1,0:T(8,128)}), f32[128,6,128]{2,1,0:T(8,128)}, u32[]{:S(2)}, u32[]{:S(2)}) async-start(f32[128,6,128]{2,1,0:T(8,128)} %broadcast_in_dim.165), calls=%async_computation.1 | async-start | bytes 1048576 | tf_op jit(solution)/shard_map/all_to_all | solution.py:136
  236.0 11.6 %all-to-all-done.1 = f32[128,6,128]{2,1,0:T(8,128)} async-done(((f32[128,6,128]{2,1,0:T(8,128)}), f32[128,6,128]{2,1,0:T(8,128)}, u32[]{:S(2)}, u32[]{:S(2)}) %all-to-all-start.1) | async-done | bytes 393248 | tf_op jit(solution)/shard_map/all_to_all | solution.py:136
  264.2 39.8 %while.42 = (s32[]{:T(128)}, f32[6,128]{1,0:T(8,128)S(1)}, s32[]{:T(128)}, s32[]{:T(128)}, f32[65536]{0:T(1024)S(1)}, /*index=5*/f32[6,65536]{1,0:T(8,128)}, f32...) while((s32[]{:T(128)}, f32[6,128]{1,0:T(8,128)S(1)}, ...), condition=%wide.region_40.41_spmd, body=%wide.region_33.40_spmd.sunk | while | flops 85983240 | bytes 1404199 | solution.py:90
  267.4 16.7 %fusion.156 = (f32[128]{0:T(128)S(1)}, f32[128]{0:T(128)S(1)}, f32[128]{0:T(128)S(1)}, f32[128]{0:T(128)S(1)}, f32[128]{0:T(128)S(1)}, /*index=5*/f32[128]{0:T(128)S(1)}) fusion(f32[128]{0:T(128)S(1)} %get-tuple-element.642, f32[16384]{0:T(1024)S(1)} %bitcast.289, f32[128]{0:T(128)S(1)} %get-tuple-element.644, f32[16384]{0:T(1024)S(1)} %bitcast.286, ...), kind=kLoop, calls=%fused_computation.110.clone.1 | loop fusion | flops 85982464 | bytes 464896 | tf_op jit(solution)/shard_map/while/body/reduce_sum | solution.py:48
  287.3 16.7 %fusion.156 = (f32[128]{0:T(128)S(1)}, f32[128]{0:T(128)S(1)}, f32[128]{0:T(128)S(1)}, f32[128]{0:T(128)S(1)}, f32[128]{0:T(128)S(1)}, /*index=5*/f32[128]{0:T(128)S(1)}) fusion(f32[128]{0:T(128)S(1)} %get-tuple-element.642, f32[16384]{0:T(1024)S(1)} %bitcast.289, f32[128]{0:T(128)S(1)} %get-tuple-element.644, f32[16384]{0:T(1024)S(1)} %bitcast.286, ...), kind=kLoop, calls=%fused_computation.110.clone.1 | loop fusion | flops 85982464 | bytes 464896 | tf_op jit(solution)/shard_map/while/body/reduce_sum | solution.py:48
  314.9 9.0 %all-to-all-done.2 = f32[128,6,128]{2,1,0:T(8,128)} async-done(((f32[128,6,128]{2,1,0:T(8,128)}), f32[128,6,128]{2,1,0:T(8,128)}, u32[]{:S(2)}, u32[]{:S(2)}) %all-to-all-start.2) | async-done | bytes 393248 | tf_op jit(solution)/shard_map/all_to_all | solution.py:136
  341.6 79.6 %while.43 = (s32[]{:T(128)}, f32[6,128]{1,0:T(8,128)S(1)}, s32[]{:T(128)}, s32[]{:T(128)}, f32[65536]{0:T(1024)S(1)}, /*index=5*/f32[6,65536]{1,0:T(8,128)}, f32...) while((s32[]{:T(128)}, f32[6,128]{1,0:T(8,128)S(1)}, ...), condition=%wide.region_53.54_spmd, body=%wide.region_46.53_spmd.sunk | while | flops 85983240 | bytes 1404199 | solution.py:90
  344.7 16.7 %fusion.158 = (f32[128]{0:T(128)S(1)}, f32[128]{0:T(128)S(1)}, f32[128]{0:T(128)S(1)}, f32[128]{0:T(128)S(1)}, f32[128]{0:T(128)S(1)}, /*index=5*/f32[128]{0:T(128)S(1)}) fusion(f32[128]{0:T(128)S(1)} %get-tuple-element.667, f32[16384]{0:T(1024)S(1)} %bitcast.295, f32[128]{0:T(128)S(1)} %get-tuple-element.669, f32[16384]{0:T(1024)S(1)} %bitcast.292, ...), kind=kLoop, calls=%fused_computation.150.clone.1 | loop fusion | flops 85982464 | bytes 464896 | tf_op jit(solution)/shard_map/while/body/reduce_sum | solution.py:48
  364.7 16.7 %fusion.158 = (f32[128]{0:T(128)S(1)}, f32[128]{0:T(128)S(1)}, f32[128]{0:T(128)S(1)}, f32[128]{0:T(128)S(1)}, f32[128]{0:T(128)S(1)}, /*index=5*/f32[128]{0:T(128)S(1)}) fusion(f32[128]{0:T(128)S(1)} %get-tuple-element.667, f32[16384]{0:T(1024)S(1)} %bitcast.295, f32[128]{0:T(128)S(1)} %get-tuple-element.669, f32[16384]{0:T(1024)S(1)} %bitcast.292, ...), kind=kLoop, calls=%fused_computation.150.clone.1 | loop fusion | flops 85982464 | bytes 464896 | tf_op jit(solution)/shard_map/while/body/reduce_sum | solution.py:48
  384.5 16.7 %fusion.158 = (f32[128]{0:T(128)S(1)}, f32[128]{0:T(128)S(1)}, f32[128]{0:T(128)S(1)}, f32[128]{0:T(128)S(1)}, f32[128]{0:T(128)S(1)}, /*index=5*/f32[128]{0:T(128)S(1)}) fusion(f32[128]{0:T(128)S(1)} %get-tuple-element.667, f32[16384]{0:T(1024)S(1)} %bitcast.295, f32[128]{0:T(128)S(1)} %get-tuple-element.669, f32[16384]{0:T(1024)S(1)} %bitcast.292, ...), kind=kLoop, calls=%fused_computation.150.clone.1 | loop fusion | flops 85982464 | bytes 464896 | tf_op jit(solution)/shard_map/while/body/reduce_sum | solution.py:48
  404.5 16.7 %fusion.158 = (f32[128]{0:T(128)S(1)}, f32[128]{0:T(128)S(1)}, f32[128]{0:T(128)S(1)}, f32[128]{0:T(128)S(1)}, f32[128]{0:T(128)S(1)}, /*index=5*/f32[128]{0:T(128)S(1)}) fusion(f32[128]{0:T(128)S(1)} %get-tuple-element.667, f32[16384]{0:T(1024)S(1)} %bitcast.295, f32[128]{0:T(128)S(1)} %get-tuple-element.669, f32[16384]{0:T(1024)S(1)} %bitcast.292, ...), kind=kLoop, calls=%fused_computation.150.clone.1 | loop fusion | flops 85982464 | bytes 464896 | tf_op jit(solution)/shard_map/while/body/reduce_sum | solution.py:48
  429.5 11.6 %all-to-all-done.3 = f32[128,6,128]{2,1,0:T(8,128)} async-done(((f32[128,6,128]{2,1,0:T(8,128)}), f32[128,6,128]{2,1,0:T(8,128)}, u32[]{:S(2)}, u32[]{:S(2)}) %all-to-all-start.3) | async-done | bytes 393248 | tf_op jit(solution)/shard_map/all_to_all | solution.py:136
  (229 shorter events, 155.8 us)
Async XLA Ops:
  7.2 53.2 %all-gather.2.cloned.1.call-start = ((), (), s32[]{:S(2)}) async-start(), calls=%async_computation.4 | async-start | bytes 4325376 | tf_op jit(solution)/shard_map/all_gather | solution.py:98
  43.4 23.7 %copy-start.23 = (pred[65536]{0:T(1024)(128)(4,1)}, pred[65536]{0:T(1024)(128)(4,1)S(1)}, u32[]{:S(2)}) copy-start(pred[65536]{0:T(1024)(128)(4,1)S(1)} %broadcast_bitcast_fusion.6) | copy-start | bytes 196612
  111.4 21.2 %all-to-all-start = ((f32[128,6,128]{2,1,0:T(8,128)}), f32[128,6,128]{2,1,0:T(8,128)}, u32[]{:S(2)}, u32[]{:S(2)}) async-start(f32[128,6,128]{2,1,0:T(8,128)} %broadcast_in_dim.161), calls=%async_computation | async-start | bytes 1048576 | tf_op jit(solution)/shard_map/all_to_all | solution.py:136
  135.0 4.5 copy-start
  139.5 2.0 copy-start.1
  141.5 6.3 %copy-start.3 = (f32[6,65536]{1,0:T(8,128)}, f32[6,65536]{1,0:T(8,128)S(1)}, u32[]{:S(2)}) copy-start(f32[6,65536]{1,0:T(8,128)S(1)} %slice_select_fusion.1) | copy-start | bytes 4718596
  228.3 19.2 %all-to-all-start.1 = ((f32[128,6,128]{2,1,0:T(8,128)}), f32[128,6,128]{2,1,0:T(8,128)}, u32[]{:S(2)}, u32[]{:S(2)}) async-start(f32[128,6,128]{2,1,0:T(8,128)} %broadcast_in_dim.165), calls=%async_computation.1 | async-start | bytes 1048576 | tf_op jit(solution)/shard_map/all_to_all | solution.py:136
  251.1 4.0 copy-start.2
  251.1 4.0 copy-start.4
  251.1 4.0 copy-start.16
  251.1 4.1 copy-start.17
  257.1 7.0 %copy-start.5 = (f32[6,65536]{1,0:T(8,128)}, f32[6,65536]{1,0:T(8,128)S(1)}, u32[]{:S(2)}) copy-start(f32[6,65536]{1,0:T(8,128)S(1)} %maximum_select_fusion) | copy-start | bytes 4718596
  304.9 19.0 %all-to-all-start.2 = ((f32[128,6,128]{2,1,0:T(8,128)}), f32[128,6,128]{2,1,0:T(8,128)}, u32[]{:S(2)}, u32[]{:S(2)}) async-start(f32[128,6,128]{2,1,0:T(8,128)} %broadcast_in_dim.167), calls=%async_computation.2 | async-start | bytes 1048576 | tf_op jit(solution)/shard_map/all_to_all | solution.py:136
  314.9 15.0 %copy-start.12 = (f32[3,65536]{1,0:T(4,128)S(1)}, f32[3,65536]{1,0:T(4,128)}, u32[]{:S(2)}) copy-start(f32[3,65536]{1,0:T(4,128)} %get-tuple-element.326) | copy-start | bytes 2359300
  329.9 3.4 copy-start.6
  329.9 3.4 copy-start.20
  329.9 3.4 copy-start.21
  333.3 2.0 copy-start.7
  335.3 6.2 %copy-start.9 = (f32[6,65536]{1,0:T(8,128)}, f32[6,65536]{1,0:T(8,128)S(1)}, u32[]{:S(2)}) copy-start(f32[6,65536]{1,0:T(8,128)S(1)} %maximum_select_fusion.1) | copy-start | bytes 4718596
  422.1 19.0 %all-to-all-start.3 = ((f32[128,6,128]{2,1,0:T(8,128)}), f32[128,6,128]{2,1,0:T(8,128)}, u32[]{:S(2)}, u32[]{:S(2)}) async-start(f32[128,6,128]{2,1,0:T(8,128)} %broadcast_in_dim.169), calls=%async_computation.3 | async-start | bytes 1048576 | tf_op jit(solution)/shard_map/all_to_all | solution.py:136
  444.2 6.3 %copy-start.8 = (f32[6,65536]{1,0:T(8,128)S(1)}, f32[6,65536]{1,0:T(8,128)}, u32[]{:S(2)}) copy-start(f32[6,65536]{1,0:T(8,128)} %copy-done.7) | copy-start | bytes 4718596
  444.2 6.3 %copy-start.18 = (f32[65536]{0:T(1024)S(1)}, f32[65536]{0:T(1024)}, u32[]{:S(2)}) copy-start(f32[65536]{0:T(1024)} %get-tuple-element.352) | copy-start | bytes 786436
  447.4 3.1 copy-start.10
  447.4 3.1 copy-start.19
  (6 other events, 7.3 us)
Sparse Core Ops, SparseCore 0:
  10.3 50.0 all-gather.1

commit v3 on v2

--- a/solution.py
+++ b/solution.py
@@ -78,13 +78,49 @@
     return jnp.concatenate([pos_new, vel_new], axis=0)
 
 
-def field_forces(targets, field_rows, body_mass, first, count, chunks=4):
-    width = field_rows.shape[1] // chunks
-
+def predict_chunked(phase, deriv, elapsed):
+    position = phase[:, 0:3]
+    velocity = phase[:, 3:6]
+    acceleration = deriv[:, 0:3]
+    jerk_old = deriv[:, 3:6]
+    pos_next = position + elapsed * (
+        velocity + elapsed * (acceleration * 0.5 + elapsed * jerk_old / 6.0)
+    )
+    vel_next = velocity + elapsed * (acceleration + elapsed * jerk_old * 0.5)
+    return jnp.concatenate([pos_next, vel_next], axis=1)
+
+
+def star_chunked(predicted):
+    position = predicted[:, 0:3]
+    velocity = predicted[:, 3:6]
+    inv_r = lax.rsqrt(jnp.sum(position * position, axis=1))
+    inv_cube = inv_r * inv_r * inv_r
+    radial = 3.0 * jnp.sum(position * velocity, axis=1) * inv_r * inv_r
+    accel = -inv_cube[:, None, :] * position
+    jerk_star = -inv_cube[:, None, :] * (velocity - radial[:, None, :] * position)
+    return jnp.concatenate([accel, jerk_star], axis=1)
+
+
+def correct_chunked(phase, deriv, fresh, elapsed):
+    half_dt = 0.5 * elapsed
+    twelfth = elapsed * elapsed / 12.0
+    vel_new = (
+        phase[:, 3:6]
+        + half_dt * (deriv[:, 0:3] + fresh[:, 0:3])
+        + twelfth * (deriv[:, 3:6] - fresh[:, 3:6])
+    )
+    pos_new = (
+        phase[:, 0:3]
+        + half_dt * (phase[:, 3:6] + vel_new)
+        + twelfth * (deriv[:, 0:3] - fresh[:, 0:3])
+    )
+    return jnp.concatenate([pos_new, vel_new], axis=1)
+
+
+def field_forces(targets, field_rows, body_mass, first, count):
     def body(i, acc):
-        at = (first + i) * width
-        rows = lax.dynamic_slice_in_dim(field_rows, at, width, axis=1)
-        masses = lax.dynamic_slice_in_dim(body_mass, at, width, axis=0)
+        rows = lax.dynamic_index_in_dim(field_rows, first + i, 0, keepdims=False)
+        masses = lax.dynamic_index_in_dim(body_mass, first + i, 0, keepdims=False)
         return acc + pair_terms(targets, rows, masses)
 
     return lax.fori_loop(0, count, body, jnp.zeros((6, targets.shape[1]), jnp.float32))
@@ -97,9 +133,12 @@
     local = jnp.concatenate([phase_space, derivatives, body_mass[None, :]], axis=0)
     full = lax.all_gather(local, plane, axis=1, tiled=True)
     total = full.shape[1]
-    mass = full[12]
-    phase = full[0:6]
-    deriv = full[6:12]
+    width = total // chunks
+    per_chunk = width // BLK
+    full = full.reshape(13, chunks, width).transpose(1, 0, 2)
+    mass = full[:, 12]
+    phase = full[:, 0:6]
+    deriv = full[:, 6:12]
     block_total = total // BLK
     slots = active_lists.shape[1] * active_lists.shape[2]
     my_unit = (
@@ -123,35 +162,38 @@
             live_count * 4 <= slots, 4, jnp.where(live_count * 2 <= slots, 2, 1)
         ).astype(jnp.int32)
         elapsed_blk = now_time - last_blk
-        elapsed = jnp.repeat(elapsed_blk, BLK)[None, :]
-        predicted = predict(phase, deriv, elapsed)
+        elapsed = jnp.repeat(elapsed_blk, BLK).reshape(chunks, 1, width)
+        predicted = predict_chunked(phase, deriv, elapsed)
         my_job = my_unit // split
         my_part = my_unit - my_job * split
         my_id = jnp.clip(compact[jnp.clip(my_job, 0, slots - 1)], 0, block_total - 1)
         span = chunks // split
         count = jnp.where(my_job < live_count, span, 0)
-        targets = lax.dynamic_slice_in_dim(predicted, my_id * BLK, BLK, axis=1)
-        partial = field_forces(targets, predicted, mass, my_part * span, count, chunks)
+        targets = lax.dynamic_slice(
+            predicted, (my_id // per_chunk, 0, (my_id % per_chunk) * BLK), (1, 6, BLK)
+        )[0]
+        partial = field_forces(targets, predicted, mass, my_part * span, count)
         sent = jnp.broadcast_to(partial[None], (slots,) + partial.shape)
         got = lax.all_to_all(sent, every, 0, 0, tiled=True)
         job_of = units // split
         owner = jnp.where(job_of < live_count, compact[jnp.clip(job_of, 0, slots - 1)], -1)
         onehot = (all_blocks[:, None] == owner[None, :]).astype(jnp.float32)
         mutual = jnp.einsum(
-            "bu,ucl->cbl", onehot, got, precision=lax.Precision.HIGHEST,
-            preferred_element_type=jnp.float32,
-        ).reshape(6, total)
-        fresh = mutual + star_terms(predicted)
-        corrected = correct(phase, deriv, fresh, elapsed)
+            "kbu,ucl->kcbl", onehot.reshape(chunks, per_chunk, slots), got,
+            precision=lax.Precision.HIGHEST, preferred_element_type=jnp.float32,
+        ).reshape(chunks, 6, width)
+        fresh = mutual + star_chunked(predicted)
+        corrected = correct_chunked(phase, deriv, fresh, elapsed)
         active_flags = jnp.any(flat[:, None] == all_blocks[None, :], axis=0)
-        active = jnp.repeat(active_flags, BLK)[None, :]
+        active = jnp.repeat(active_flags, BLK).reshape(chunks, 1, width)
         phase = jnp.where(active, corrected, phase)
         deriv = jnp.where(active, fresh, deriv)
         last_blk = jnp.where(active_flags, jnp.float32(now_time), last_blk)
     local_count = phase_space.shape[1]
     offset = (lax.axis_index("ja") * lax.axis_size("ha") + lax.axis_index("ha")) * local_count
-    phase_out = lax.dynamic_slice_in_dim(phase, offset, local_count, axis=1)
-    deriv_out = lax.dynamic_slice_in_dim(deriv, offset, local_count, axis=1)
+    at = (offset // width, 0, offset % width)
+    phase_out = lax.dynamic_slice(phase, at, (1, 6, local_count))[0]
+    deriv_out = lax.dynamic_slice(deriv, at, (1, 6, local_count))[0]
     return (phase_out, deriv_out)
 
 

time: 465 us -> 448 us (0.963)
  other arithmetic: 273 us -> 262 us
  waiting for transfers between devices: 56.9 us -> 47 us
    slice x12, local copies, waits for them, and re-layouts: 37.2 us -> 15.5 us  [pair_terms(): rel_x = field_rows[3][:, None] - targets[3][None, :]]
    reshape x0 -> x5, local copies, waits for them, and re-layouts: none -> 15.5 us  [the longest x4 11.5 us: shards(): mutual = jnp.einsum('kbu,ucl->kcbl', onehot.reshape(chunks, per_chunk, sl...]
    reduce_sum x4, other arithmetic: 20.1 us -> 7.34 us  [star_chunked(): inv_r = lax.rsqrt(jnp.sum(position * position, axis=1))]
    all_gather x1, waiting for transfers between devices: 13.7 us -> 7.44 us  [shards(): full = lax.all_gather(local, plane, axis=1, tiled=True)]
    unnamed x48 -> x71, local copies, waits for them, and re-layouts: 0.85 us -> 5.97 us
    mul x6 -> x7, other arithmetic: 10.5 us -> 11.8 us  [the longest x4 8.6 us: star_chunked(): accel = -inv_cube[:, None, :] * position]
  transfers between devices with their start and end apart: 5 -> 5, of which waited for: 5 -> 5; matrix products, arithmetic and copies ran while one was open for 8% -> 11% of each run, Pallas kernels for 0% -> 0%
where the time goes in v3:
time: 448 us; the launch traced here: 441 us
  other arithmetic  262 us (58%)
  local copies, waits for them, and re-layouts  71.6 us (16%)
  waiting for transfers between devices  47 us (10%)
  between operations  25.6 us (6%)
  starting transfers between devices  24.3 us (5%)
  matrix products  10.1 us (2%)
    reduce_sum x12, other arithmetic, pair_terms(): jnp.sum(inv_cube * (rel_z - radial * sep_z), axis=0)  204 us
    all_to_all x4, waiting for transfers between devices, shards(): got = lax.all_to_all(sent, every, 0, 0, tiled=True)  39.5 us
    all_to_all x4, starting transfers between devices, shards(): got = lax.all_to_all(sent, every, 0, 0, tiled=True)  24.3 us
    slice x12, local copies, waits for them, and re-layouts, pair_terms(): rel_x = field_rows[3][:, None] - targets[3][None, :]  15.5 us
    reshape x4, local copies, waits for them, and re-layouts, shards(): mutual = jnp.einsum('kbu,ucl->kcbl', onehot.reshape(chunks, per_chunk, sl...  11.5 us
    dot_general x4, matrix products, shards(): jnp.einsum('kbu,ucl->kcbl', onehot.reshape(chunks, per_chunk, slots), got...  10.1 us
    transpose x4, local copies, waits for them, and re-layouts, shards(): jnp.einsum('kbu,ucl->kcbl', onehot.reshape(chunks, per_chunk, slots), got...  9.3 us
  transfers between devices with their start and end apart: 5, of which 5 were waited for; matrix products, arithmetic and copies ran while one was open for 11% of the time, Pallas kernels for 0%

profile of v3, /device:TPU:1, one launch (start us, length us, event | category | flops | bytes accessed | tf_op | source)
XLA Modules:
  0.0 441.2 jit_solution(9682724418665384414)
XLA Ops:
  52.7 7.4 %all-gather.2.cloned.1.call-done = f32[13,65536]{1,0:T(8,128)} async-done(((f32[13,2048]{1,0:T(8,128)}), f32[13,65536]{1,0:T(8,128)}) %all-gather.2.cloned.1.call-update) | async-done | bytes 3407888 | tf_op jit(solution)/shard_map/all_gather | solution.py:134
  68.3 41.7 %while.40 = (s32[]{:T(128)}, f32[6,128]{1,0:T(8,128)S(1)}, s32[]{:T(128)}, s32[]{:T(128)}, f32[4,16384]{1,0:T(4,128)}, /*index=5*/f32[4,6,16384]{2,0,1:T(4,128)}...) while((s32[]{:T(128)}, f32[6,128]{1,0:T(8,128)S(1)}, ...), condition=%wide.region_14.15_spmd, body=%wide.region_7.14_spmd.sunk | while | flops 85983240 | bytes 1404179 | solution.py:126
  71.1 17.3 %fusion.144 = (f32[128]{0:T(128)}, f32[128]{0:T(128)}, f32[128]{0:T(128)}, f32[128]{0:T(128)}, f32[128]{0:T(128)}, /*index=5*/f32[128]{0:T(128)}) fusion(f32[128]{0:T(128)S(1)} %get-tuple-element.674, f32[16384]{0:T(1024)S(1)} %bitcast.401, f32[128]{0:T(128)S(1)} %get-tuple-element.676, f32[16384]{0:T(1024)S(1)} %bitcast.398, ...), kind=kLoop, calls=%fused_computation.30.clone.1 | loop fusion | flops 85982464 | bytes 464896 | tf_op jit(solution)/shard_map/while/body/reduce_sum | solution.py:48
  92.0 17.3 %fusion.144 = (f32[128]{0:T(128)}, f32[128]{0:T(128)}, f32[128]{0:T(128)}, f32[128]{0:T(128)}, f32[128]{0:T(128)}, /*index=5*/f32[128]{0:T(128)}) fusion(f32[128]{0:T(128)S(1)} %get-tuple-element.674, f32[16384]{0:T(1024)S(1)} %bitcast.401, f32[128]{0:T(128)S(1)} %get-tuple-element.676, f32[16384]{0:T(1024)S(1)} %bitcast.398, ...), kind=kLoop, calls=%fused_computation.30.clone.1 | loop fusion | flops 85982464 | bytes 464896 | tf_op jit(solution)/shard_map/while/body/reduce_sum | solution.py:48
  110.9 6.8 %all-to-all-start = ((f32[128,6,128]{2,1,0:T(8,128)}), f32[128,6,128]{2,1,0:T(8,128)}, u32[]{:S(2)}, u32[]{:S(2)}) async-start(f32[128,6,128]{2,1,0:T(8,128)} %broadcast_in_dim.179), calls=%async_computation | async-start | bytes 1048576 | tf_op jit(solution)/shard_map/all_to_all | solution.py:177
  121.6 9.1 %all-to-all-done = f32[128,6,128]{2,1,0:T(8,128)} async-done(((f32[128,6,128]{2,1,0:T(8,128)}), f32[128,6,128]{2,1,0:T(8,128)}, u32[]{:S(2)}, u32[]{:S(2)}) %all-to-all-start) | async-done | bytes 393248 | tf_op jit(solution)/shard_map/all_to_all | solution.py:177
  146.3 74.0 %while.41 = (s32[]{:T(128)}, f32[6,128]{1,0:T(8,128)S(1)}, s32[]{:T(128)}, s32[]{:T(128)}, f32[4,16384]{1,0:T(4,128)S(1)}, /*index=5*/f32[4,6,16384]{2,0,1:T(4,1...) while((s32[]{:T(128)}, f32[6,128]{1,0:T(8,128)S(1)}, ...), condition=%wide.region_27.28_spmd, body=%wide.region_20.27_spmd.sunk | while | flops 85983240 | bytes 1404179 | solution.py:126
  146.8 17.3 %fusion.145 = (f32[128]{0:T(128)}, f32[128]{0:T(128)}, f32[128]{0:T(128)}, f32[128]{0:T(128)}, f32[128]{0:T(128)}, /*index=5*/f32[128]{0:T(128)}) fusion(f32[128]{0:T(128)S(1)} %get-tuple-element.699, f32[16384]{0:T(1024)S(1)} %bitcast.407, f32[128]{0:T(128)S(1)} %get-tuple-element.701, f32[16384]{0:T(1024)S(1)} %bitcast.404, ...), kind=kLoop, calls=%fused_computation.76.clone.1 | loop fusion | flops 85982464 | bytes 464896 | tf_op jit(solution)/shard_map/while/body/reduce_sum | solution.py:48
  165.3 17.3 %fusion.145 = (f32[128]{0:T(128)}, f32[128]{0:T(128)}, f32[128]{0:T(128)}, f32[128]{0:T(128)}, f32[128]{0:T(128)}, /*index=5*/f32[128]{0:T(128)}) fusion(f32[128]{0:T(128)S(1)} %get-tuple-element.699, f32[16384]{0:T(1024)S(1)} %bitcast.407, f32[128]{0:T(128)S(1)} %get-tuple-element.701, f32[16384]{0:T(1024)S(1)} %bitcast.404, ...), kind=kLoop, calls=%fused_computation.76.clone.1 | loop fusion | flops 85982464 | bytes 464896 | tf_op jit(solution)/shard_map/while/body/reduce_sum | solution.py:48
  183.8 17.3 %fusion.145 = (f32[128]{0:T(128)}, f32[128]{0:T(128)}, f32[128]{0:T(128)}, f32[128]{0:T(128)}, f32[128]{0:T(128)}, /*index=5*/f32[128]{0:T(128)}) fusion(f32[128]{0:T(128)S(1)} %get-tuple-element.699, f32[16384]{0:T(1024)S(1)} %bitcast.407, f32[128]{0:T(128)S(1)} %get-tuple-element.701, f32[16384]{0:T(1024)S(1)} %bitcast.404, ...), kind=kLoop, calls=%fused_computation.76.clone.1 | loop fusion | flops 85982464 | bytes 464896 | tf_op jit(solution)/shard_map/while/body/reduce_sum | solution.py:48
  202.2 17.3 %fusion.145 = (f32[128]{0:T(128)}, f32[128]{0:T(128)}, f32[128]{0:T(128)}, f32[128]{0:T(128)}, f32[128]{0:T(128)}, /*index=5*/f32[128]{0:T(128)}) fusion(f32[128]{0:T(128)S(1)} %get-tuple-element.699, f32[16384]{0:T(1024)S(1)} %bitcast.407, f32[128]{0:T(128)S(1)} %get-tuple-element.701, f32[16384]{0:T(1024)S(1)} %bitcast.404, ...), kind=kLoop, calls=%fused_computation.76.clone.1 | loop fusion | flops 85982464 | bytes 464896 | tf_op jit(solution)/shard_map/while/body/reduce_sum | solution.py:48
  229.6 10.6 %all-to-all-done.1 = f32[128,6,128]{2,1,0:T(8,128)} async-done(((f32[128,6,128]{2,1,0:T(8,128)}), f32[128,6,128]{2,1,0:T(8,128)}, u32[]{:S(2)}, u32[]{:S(2)}) %all-to-all-start.1) | async-done | bytes 393248 | tf_op jit(solution)/shard_map/all_to_all | solution.py:177
  254.3 37.3 %while.42 = (s32[]{:T(128)}, f32[6,128]{1,0:T(8,128)S(1)}, s32[]{:T(128)}, s32[]{:T(128)}, f32[4,16384]{1,0:T(4,128)S(1)}, /*index=5*/f32[4,6,16384]{2,0,1:T(4,1...) while((s32[]{:T(128)}, f32[6,128]{1,0:T(8,128)S(1)}, ...), condition=%wide.region_40.41_spmd, body=%wide.region_33.40_spmd.sunk | while | flops 85983240 | bytes 1404179 | solution.py:126
  256.2 16.7 %fusion.146 = (f32[128]{0:T(128)S(1)}, f32[128]{0:T(128)S(1)}, f32[128]{0:T(128)S(1)}, f32[128]{0:T(128)S(1)}, f32[128]{0:T(128)S(1)}, /*index=5*/f32[128]{0:T(128)S(1)}) fusion(f32[128]{0:T(128)S(1)} %get-tuple-element.724, f32[16384]{0:T(1024)S(1)} %bitcast.413, f32[128]{0:T(128)S(1)} %get-tuple-element.726, f32[16384]{0:T(1024)S(1)} %bitcast.410, ...), kind=kLoop, calls=%fused_computation.122.clone.1 | loop fusion | flops 85982464 | bytes 464896 | tf_op jit(solution)/shard_map/while/body/reduce_sum | solution.py:48
  274.8 16.7 %fusion.146 = (f32[128]{0:T(128)S(1)}, f32[128]{0:T(128)S(1)}, f32[128]{0:T(128)S(1)}, f32[128]{0:T(128)S(1)}, f32[128]{0:T(128)S(1)}, /*index=5*/f32[128]{0:T(128)S(1)}) fusion(f32[128]{0:T(128)S(1)} %get-tuple-element.724, f32[16384]{0:T(1024)S(1)} %bitcast.413, f32[128]{0:T(128)S(1)} %get-tuple-element.726, f32[16384]{0:T(1024)S(1)} %bitcast.410, ...), kind=kLoop, calls=%fused_computation.122.clone.1 | loop fusion | flops 85982464 | bytes 464896 | tf_op jit(solution)/shard_map/while/body/reduce_sum | solution.py:48
  292.4 5.8 %all-to-all-start.2 = ((f32[128,6,128]{2,1,0:T(8,128)}), f32[128,6,128]{2,1,0:T(8,128)}, u32[]{:S(2)}, u32[]{:S(2)}) async-start(f32[128,6,128]{2,1,0:T(8,128)} %broadcast_in_dim.187), calls=%async_computation.2 | async-start | bytes 1048576 | tf_op jit(solution)/shard_map/all_to_all | solution.py:177
  302.2 9.2 %all-to-all-done.2 = f32[128,6,128]{2,1,0:T(8,128)} async-done(((f32[128,6,128]{2,1,0:T(8,128)}), f32[128,6,128]{2,1,0:T(8,128)}, u32[]{:S(2)}, u32[]{:S(2)}) %all-to-all-start.2) | async-done | bytes 393248 | tf_op jit(solution)/shard_map/all_to_all | solution.py:177
  327.9 74.5 %while.43 = (s32[]{:T(128)}, f32[6,128]{1,0:T(8,128)S(1)}, s32[]{:T(128)}, s32[]{:T(128)}, f32[4,16384]{1,0:T(4,128)S(1)}, /*index=5*/f32[4,6,16384]{2,0,1:T(4,1...) while((s32[]{:T(128)}, f32[6,128]{1,0:T(8,128)S(1)}, ...), condition=%wide.region_53.54_spmd, body=%wide.region_46.53_spmd.sunk | while | flops 85983240 | bytes 1404179 | solution.py:126
  329.8 16.7 %fusion.147 = (f32[128]{0:T(128)S(1)}, f32[128]{0:T(128)S(1)}, f32[128]{0:T(128)S(1)}, f32[128]{0:T(128)S(1)}, f32[128]{0:T(128)S(1)}, /*index=5*/f32[128]{0:T(128)S(1)}) fusion(f32[128]{0:T(128)S(1)} %get-tuple-element.749, f32[16384]{0:T(1024)S(1)} %bitcast.419, f32[128]{0:T(128)S(1)} %get-tuple-element.751, f32[16384]{0:T(1024)S(1)} %bitcast.416, ...), kind=kLoop, calls=%fused_computation.168.clone.1 | loop fusion | flops 85982464 | bytes 464896 | tf_op jit(solution)/shard_map/while/body/reduce_sum | solution.py:48
  348.4 16.7 %fusion.147 = (f32[128]{0:T(128)S(1)}, f32[128]{0:T(128)S(1)}, f32[128]{0:T(128)S(1)}, f32[128]{0:T(128)S(1)}, f32[128]{0:T(128)S(1)}, /*index=5*/f32[128]{0:T(128)S(1)}) fusion(f32[128]{0:T(128)S(1)} %get-tuple-element.749, f32[16384]{0:T(1024)S(1)} %bitcast.419, f32[128]{0:T(128)S(1)} %get-tuple-element.751, f32[16384]{0:T(1024)S(1)} %bitcast.416, ...), kind=kLoop, calls=%fused_computation.168.clone.1 | loop fusion | flops 85982464 | bytes 464896 | tf_op jit(solution)/shard_map/while/body/reduce_sum | solution.py:48
  367.0 16.7 %fusion.147 = (f32[128]{0:T(128)S(1)}, f32[128]{0:T(128)S(1)}, f32[128]{0:T(128)S(1)}, f32[128]{0:T(128)S(1)}, f32[128]{0:T(128)S(1)}, /*index=5*/f32[128]{0:T(128)S(1)}) fusion(f32[128]{0:T(128)S(1)} %get-tuple-element.749, f32[16384]{0:T(1024)S(1)} %bitcast.419, f32[128]{0:T(128)S(1)} %get-tuple-element.751, f32[16384]{0:T(1024)S(1)} %bitcast.416, ...), kind=kLoop, calls=%fused_computation.168.clone.1 | loop fusion | flops 85982464 | bytes 464896 | tf_op jit(solution)/shard_map/while/body/reduce_sum | solution.py:48
  385.7 16.7 %fusion.147 = (f32[128]{0:T(128)S(1)}, f32[128]{0:T(128)S(1)}, f32[128]{0:T(128)S(1)}, f32[128]{0:T(128)S(1)}, f32[128]{0:T(128)S(1)}, /*index=5*/f32[128]{0:T(128)S(1)}) fusion(f32[128]{0:T(128)S(1)} %get-tuple-element.749, f32[16384]{0:T(1024)S(1)} %bitcast.419, f32[128]{0:T(128)S(1)} %get-tuple-element.751, f32[16384]{0:T(1024)S(1)} %bitcast.416, ...), kind=kLoop, calls=%fused_computation.168.clone.1 | loop fusion | flops 85982464 | bytes 464896 | tf_op jit(solution)/shard_map/while/body/reduce_sum | solution.py:48
  403.3 5.9 %all-to-all-start.3 = ((f32[128,6,128]{2,1,0:T(8,128)}), f32[128,6,128]{2,1,0:T(8,128)}, u32[]{:S(2)}, u32[]{:S(2)}) async-start(f32[128,6,128]{2,1,0:T(8,128)} %broadcast_in_dim.190), calls=%async_computation.3 | async-start | bytes 1048576 | tf_op jit(solution)/shard_map/all_to_all | solution.py:177
  411.8 10.6 %all-to-all-done.3 = f32[128,6,128]{2,1,0:T(8,128)} async-done(((f32[128,6,128]{2,1,0:T(8,128)}), f32[128,6,128]{2,1,0:T(8,128)}, u32[]{:S(2)}, u32[]{:S(2)}) %all-to-all-start.3) | async-done | bytes 393248 | tf_op jit(solution)/shard_map/all_to_all | solution.py:177
  (252 shorter events, 145.4 us)
Async XLA Ops:
  7.2 53.0 %all-gather.2.cloned.1.call-start = ((), (), s32[]{:S(2)}) async-start(), calls=%async_computation.4 | async-start | bytes 4325376 | tf_op jit(solution)/shard_map/all_gather | solution.py:134
  65.9 2.3 copy-start.6
  65.9 2.3 copy-start.7
  110.0 20.7 %copy-start.25 = (s32[128]{0:T(128)S(1)}, s32[128]{0:T(128)}, u32[]{:S(2)}) copy-start(s32[128]{0:T(128)} %compare_select_fusion.11) | copy-start | bytes 1540
  110.9 19.9 %all-to-all-start = ((f32[128,6,128]{2,1,0:T(8,128)}), f32[128,6,128]{2,1,0:T(8,128)}, u32[]{:S(2)}, u32[]{:S(2)}) async-start(f32[128,6,128]{2,1,0:T(8,128)} %broadcast_in_dim.179), calls=%async_computation | async-start | bytes 1048576 | tf_op jit(solution)/shard_map/all_to_all | solution.py:177
  143.9 2.3 copy-start
  144.0 2.3 copy-start.10
  220.3 19.9 %copy-start.24 = (s32[128]{0:T(128)S(1)}, s32[128]{0:T(128)}, u32[]{:S(2)}) copy-start(s32[128]{0:T(128)} %compare_select_fusion.10) | copy-start | bytes 1540
  221.1 19.0 %all-to-all-start.1 = ((f32[128,6,128]{2,1,0:T(8,128)}), f32[128,6,128]{2,1,0:T(8,128)}, u32[]{:S(2)}, u32[]{:S(2)}) async-start(f32[128,6,128]{2,1,0:T(8,128)} %broadcast_in_dim.184), calls=%async_computation.1 | async-start | bytes 1048576 | tf_op jit(solution)/shard_map/all_to_all | solution.py:177
  229.6 17.0 %copy-start.3 = (f32[4,6,16384]{2,0,1:T(4,128)S(1)}, f32[4,6,16384]{2,0,1:T(4,128)}, u32[]{:S(2)}) copy-start(f32[4,6,16384]{2,0,1:T(4,128)} %copy-done.2) | copy-start | bytes 4718596
  246.6 2.8 copy-start.1
  246.6 2.9 copy-start.11
  246.6 2.9 copy-start.12
  252.6 1.7 copy-start.8
  252.6 1.7 copy-start.9
  291.6 19.9 %copy-start.23 = (s32[128]{0:T(128)S(1)}, s32[128]{0:T(128)}, u32[]{:S(2)}) copy-start(s32[128]{0:T(128)} %compare_select_fusion.9) | copy-start | bytes 1540
  292.4 19.1 %all-to-all-start.2 = ((f32[128,6,128]{2,1,0:T(8,128)}), f32[128,6,128]{2,1,0:T(8,128)}, u32[]{:S(2)}, u32[]{:S(2)}) async-start(f32[128,6,128]{2,1,0:T(8,128)} %broadcast_in_dim.187), calls=%async_computation.2 | async-start | bytes 1048576 | tf_op jit(solution)/shard_map/all_to_all | solution.py:177
  320.5 2.8 copy-start.15
  320.5 2.8 copy-start.16
  402.4 20.0 %copy-start.22 = (s32[128]{0:T(128)S(1)}, s32[128]{0:T(128)}, u32[]{:S(2)}) copy-start(s32[128]{0:T(128)} %compare_select_fusion.8) | copy-start | bytes 1540
  403.3 19.1 %all-to-all-start.3 = ((f32[128,6,128]{2,1,0:T(8,128)}), f32[128,6,128]{2,1,0:T(8,128)}, u32[]{:S(2)}, u32[]{:S(2)}) async-start(f32[128,6,128]{2,1,0:T(8,128)} %broadcast_in_dim.190), calls=%async_computation.3 | async-start | bytes 1048576 | tf_op jit(solution)/shard_map/all_to_all | solution.py:177
  426.0 5.4 %copy-start.5 = (f32[4,6,16384]{2,0,1:T(4,128)S(1)}, f32[4,6,16384]{2,0,1:T(4,128)}, u32[]{:S(2)}) copy-start(f32[4,6,16384]{2,0,1:T(4,128)} %copy-done.4) | copy-start | bytes 4718596
  426.0 5.4 %copy-start.13 = (f32[4,16384]{1,0:T(4,128)S(1)}, f32[4,16384]{1,0:T(4,128)}, u32[]{:S(2)}) copy-start(f32[4,16384]{1,0:T(4,128)} %get-tuple-element.416) | copy-start | bytes 786436
  428.9 2.4 copy-start.14
  (7 other events, 8.4 us)
Sparse Core Ops, SparseCore 0:
  10.3 49.8 all-gather.1

commit v4 on v2

--- a/solution.py
+++ b/solution.py
@@ -4,6 +4,8 @@
 import jax.numpy as jnp
 from jax import lax
 from jax.sharding import PartitionSpec as P
+from jax.experimental import pallas as pl
+from jax.experimental.pallas import tpu as pltpu
 from jax.experimental import pallas as pl
 from jax.experimental.pallas import tpu as pltpu
 
@@ -78,35 +80,84 @@
     return jnp.concatenate([pos_new, vel_new], axis=0)
 
 
-def field_forces(targets, field_rows, body_mass, first, count, chunks=4):
-    width = field_rows.shape[1] // chunks
-
-    def body(i, acc):
-        at = (first + i) * width
-        rows = lax.dynamic_slice_in_dim(field_rows, at, width, axis=1)
-        masses = lax.dynamic_slice_in_dim(body_mass, at, width, axis=0)
-        return acc + pair_terms(targets, rows, masses)
-
-    return lax.fori_loop(0, count, body, jnp.zeros((6, targets.shape[1]), jnp.float32))
+def _force_kernel(ctl_ref, tgt_ref, src_ref, mass_ref, out_ref):
+    targets = tgt_ref.shape[2]
+    for part in range(2):
+        lo = ctl_ref[2 * part]
+        hi = ctl_ref[2 * part + 1]
+
+        def per_target(t, carry, part=part, lo=lo, hi=hi):
+            tx = tgt_ref[part, 0, t]
+            ty = tgt_ref[part, 1, t]
+            tz = tgt_ref[part, 2, t]
+            tu = tgt_ref[part, 3, t]
+            tv = tgt_ref[part, 4, t]
+            tw = tgt_ref[part, 5, t]
+
+            def per_tile(s, acc):
+                rows = pl.ds(pl.multiple_of(s * 8, 8), 8)
+                sep_x = src_ref[0, rows, :] - tx
+                sep_y = src_ref[1, rows, :] - ty
+                sep_z = src_ref[2, rows, :] - tz
+                rel_x = src_ref[3, rows, :] - tu
+                rel_y = src_ref[4, rows, :] - tv
+                rel_z = src_ref[5, rows, :] - tw
+                dist_sq = sep_x * sep_x + sep_y * sep_y + sep_z * sep_z + soften_sq
+                inv_r = lax.rsqrt(dist_sq)
+                inv_cube = mass_ref[rows, :] * inv_r * inv_r * inv_r
+                radial = 3.0 * (sep_x * rel_x + sep_y * rel_y + sep_z * rel_z) * inv_r * inv_r
+                return (
+                    acc[0] + inv_cube * sep_x,
+                    acc[1] + inv_cube * sep_y,
+                    acc[2] + inv_cube * sep_z,
+                    acc[3] + inv_cube * (rel_x - radial * sep_x),
+                    acc[4] + inv_cube * (rel_y - radial * sep_y),
+                    acc[5] + inv_cube * (rel_z - radial * sep_z),
+                )
+
+            zero = jnp.zeros((8, 128), jnp.float32)
+            acc = lax.fori_loop(lo, hi, per_tile, (zero,) * 6)
+            for k in range(6):
+                out_ref[part, k, pl.ds(t, 1), :] = jnp.sum(acc[k], axis=0, keepdims=True)
+            return carry
+
+        lax.fori_loop(0, targets, per_target, 0)
+
+
+def kernel_forces(ranges, targets, field, masses):
+    out = pl.pallas_call(
+        _force_kernel,
+        out_shape=jax.ShapeDtypeStruct((2, 6, targets.shape[2], 128), jnp.float32),
+        in_specs=[
+            pl.BlockSpec(memory_space=pltpu.MemorySpace.SMEM),
+            pl.BlockSpec(memory_space=pltpu.MemorySpace.SMEM),
+            pl.BlockSpec(memory_space=pltpu.MemorySpace.VMEM),
+            pl.BlockSpec(memory_space=pltpu.MemorySpace.VMEM),
+        ],
+        out_specs=pl.BlockSpec(memory_space=pltpu.MemorySpace.VMEM),
+    )(ranges, targets, field, masses)
+    return jnp.sum(out, axis=3)
 
 
 def shards(phase_space, derivatives, body_mass, active_lists):
     every = ("ia", "ja", "ha")
     plane = ("ja", "ha")
-    chunks = 4
     local = jnp.concatenate([phase_space, derivatives, body_mass[None, :]], axis=0)
     full = lax.all_gather(local, plane, axis=1, tiled=True)
     total = full.shape[1]
+    block_total = total // BLK
+    full = full.reshape(13, block_total, BLK)
     mass = full[12]
     phase = full[0:6]
     deriv = full[6:12]
-    block_total = total // BLK
+    tiles = block_total // 8
     slots = active_lists.shape[1] * active_lists.shape[2]
+    devices = lax.axis_size("ia") * lax.axis_size("ja") * lax.axis_size("ha")
     my_unit = (
         lax.axis_index("ia") * lax.axis_size("ja") + lax.axis_index("ja")
     ) * lax.axis_size("ha") + lax.axis_index("ha")
     all_blocks = jnp.arange(block_total, dtype=jnp.int32)
-    units = jnp.arange(slots, dtype=jnp.int32)
+    units = jnp.arange(devices, dtype=jnp.int32)
     last_blk = jnp.zeros((block_total,), jnp.float32)
     for step_index in range(STEPS):
         now_time = (step_index + 1) * time_step
@@ -119,40 +170,53 @@
             .at[jnp.where(live, rank, slots)]
             .set(flat, mode="drop")
         )
-        split = jnp.where(
-            live_count * 4 <= slots, 4, jnp.where(live_count * 2 <= slots, 2, 1)
+        work = live_count * tiles
+        share = (work + devices - 1) // devices
+        begin = jnp.minimum(units * share, work)
+        finish = jnp.minimum(begin + share, work)
+        job_a = jnp.minimum(begin // tiles, slots - 1)
+        lo_a = begin - job_a * tiles
+        hi_a = jnp.maximum(jnp.minimum(finish - job_a * tiles, tiles), lo_a)
+        job_b = jnp.minimum(job_a + 1, slots - 1)
+        hi_b = jnp.clip(finish - (job_a + 1) * tiles, 0, tiles)
+        owner_a = jnp.where(hi_a > lo_a, compact[job_a], -1)
+        owner_b = jnp.where(hi_b > 0, compact[job_b], -1)
+        owner_all = jnp.stack([owner_a, owner_b], axis=1).reshape(-1)
+        ranges = jnp.stack(
+            [lo_a[my_unit], hi_a[my_unit], jnp.zeros_like(hi_b[my_unit]), hi_b[my_unit]]
         ).astype(jnp.int32)
+        id_a = jnp.clip(compact[job_a[my_unit]], 0, block_total - 1)
+        id_b = jnp.clip(compact[job_b[my_unit]], 0, block_total - 1)
         elapsed_blk = now_time - last_blk
-        elapsed = jnp.repeat(elapsed_blk, BLK)[None, :]
+        elapsed = elapsed_blk[None, :, None]
         predicted = predict(phase, deriv, elapsed)
-        my_job = my_unit // split
-        my_part = my_unit - my_job * split
-        my_id = jnp.clip(compact[jnp.clip(my_job, 0, slots - 1)], 0, block_total - 1)
-        span = chunks // split
-        count = jnp.where(my_job < live_count, span, 0)
-        targets = lax.dynamic_slice_in_dim(predicted, my_id * BLK, BLK, axis=1)
-        partial = field_forces(targets, predicted, mass, my_part * span, count, chunks)
-        sent = jnp.broadcast_to(partial[None], (slots,) + partial.shape)
-        got = lax.all_to_all(sent, every, 0, 0, tiled=True)
-        job_of = units // split
-        owner = jnp.where(job_of < live_count, compact[jnp.clip(job_of, 0, slots - 1)], -1)
-        onehot = (all_blocks[:, None] == owner[None, :]).astype(jnp.float32)
+        targets = jnp.stack(
+            [
+                lax.dynamic_index_in_dim(predicted, id_a, 1, keepdims=False),
+                lax.dynamic_index_in_dim(predicted, id_b, 1, keepdims=False),
+            ]
+        )
+        partial = kernel_forces(ranges, targets, predicted, mass)
+        sent = jnp.broadcast_to(partial[None], (devices,) + partial.shape)
+        got = lax.all_to_all(sent, every, 0, 0, tiled=True).reshape(2 * devices, 6, BLK)
+        onehot = (all_blocks[:, None] == owner_all[None, :]).astype(jnp.float32)
         mutual = jnp.einsum(
-            "bu,ucl->cbl", onehot, got, precision=lax.Precision.HIGHEST,
-            preferred_element_type=jnp.float32,
-        ).reshape(6, total)
+            "bu,ucl->cbl", onehot, got,
+            precision=lax.Precision.HIGHEST, preferred_element_type=jnp.float32,
+        )
         fresh = mutual + star_terms(predicted)
         corrected = correct(phase, deriv, fresh, elapsed)
         active_flags = jnp.any(flat[:, None] == all_blocks[None, :], axis=0)
-        active = jnp.repeat(active_flags, BLK)[None, :]
+        active = active_flags[None, :, None]
         phase = jnp.where(active, corrected, phase)
         deriv = jnp.where(active, fresh, deriv)
         last_blk = jnp.where(active_flags, jnp.float32(now_time), last_blk)
     local_count = phase_space.shape[1]
-    offset = (lax.axis_index("ja") * lax.axis_size("ha") + lax.axis_index("ha")) * local_count
-    phase_out = lax.dynamic_slice_in_dim(phase, offset, local_count, axis=1)
-    deriv_out = lax.dynamic_slice_in_dim(deriv, offset, local_count, axis=1)
-    return (phase_out, deriv_out)
+    local_blocks = local_count // BLK
+    offset = (lax.axis_index("ja") * lax.axis_size("ha") + lax.axis_index("ha")) * local_blocks
+    phase_out = lax.dynamic_slice_in_dim(phase, offset, local_blocks, axis=1)
+    deriv_out = lax.dynamic_slice_in_dim(deriv, offset, local_blocks, axis=1)
+    return (phase_out.reshape(6, local_count), deriv_out.reshape(6, local_count))
 
 
 def solution(mesh):

time: 465 us -> 633 us (1.36)
  Pallas kernels: 0 us -> 397 us
  other arithmetic: 273 us -> 56.1 us
  between operations: 25.2 us -> 37.4 us
  local copies, waits for them, and re-layouts: 68.3 us -> 57.2 us
    pallas_call x0 -> x4, Pallas kernels: none -> 397 us  [kernel_forces(): pl.pallas_call(_force_kernel, out_shape=jax.ShapeDtypeStruct((2, 6, targe...]
    reduce_sum x12 -> x4, other arithmetic: 200 us -> 5.62 us  [kernel_forces(): return jnp.sum(out, axis=3)]
    slice x12 -> x0, local copies, waits for them, and re-layouts: 37.2 us -> none  [pair_terms(): rel_x = field_rows[3][:, None] - targets[3][None, :]]
    dynamic_slice x18 -> x25, local copies, waits for them, and re-layouts: 2.65 us -> 14.7 us  [the longest x8 4.81 us: shards(): id_a = jnp.clip(compact[job_a[my_unit]], 0, block_total - 1)]
    another operation x4 -> x18, other arithmetic: 0.68 us -> 12.3 us  [the longest x2 8.81 us: shards(): jnp.stack([lo_a[my_unit], hi_a[my_unit], jnp.zeros_like(hi_b[my_unit]), h...]
    unnamed x48 -> x73, local copies, waits for them, and re-layouts: 0.85 us -> 12 us
    reduce_sum x4, other arithmetic: 20.1 us -> 9.88 us  [star_terms(): inv_r = lax.rsqrt(jnp.sum(position * position, axis=0))]
    select_n x4 -> x3, other arithmetic: 12.6 us -> 3.64 us  [shards(): deriv = jnp.where(active, fresh, deriv)]
  transfers between devices with their start and end apart: 5 -> 5, of which waited for: 5 -> 4; matrix products, arithmetic and copies ran while one was open for 8% -> 10% of each run, Pallas kernels for 0% -> 0%
where the time goes in v4:
time: 633 us; the launch traced here: 632 us
  Pallas kernels  397 us (63%)
  local copies, waits for them, and re-layouts  57.2 us (9%)
  other arithmetic  56.1 us (9%)
  waiting for transfers between devices  52 us (8%)
  between operations  37.4 us (6%)
  starting transfers between devices  28.2 us (4%)
    pallas_call x4, Pallas kernels, kernel_forces(): pl.pallas_call(_force_kernel, out_shape=jax.ShapeDtypeStruct((2, 6, targe...  397 us
    all_to_all x4, waiting for transfers between devices, shards(): lax.all_to_all(sent, every, 0, 0, tiled=True).reshape(2 * devices, 6, BLK)  39 us
    all_to_all x4, starting transfers between devices, shards(): lax.all_to_all(sent, every, 0, 0, tiled=True).reshape(2 * devices, 6, BLK)  28.2 us
    all_gather x1, waiting for transfers between devices, shards(): full = lax.all_gather(local, plane, axis=1, tiled=True)  13 us
  transfers between devices with their start and end apart: 5, of which 4 were waited for; matrix products, arithmetic and copies ran while one was open for 10% of the time, Pallas kernels for 0%

profile of v4, /device:TPU:1, one launch (start us, length us, event | category | flops | bytes accessed | tf_op | source)
XLA Modules:
  0.0 631.6 jit_solution(7580272081430879992)
XLA Ops:
  7.2 1.6 pad_maximum_fusion.4
  41.8 4.4 fusion.100
  47.2 13.0 %all-gather.2.cloned.1.call-done = f32[13,65536]{1,0:T(8,128)} async-done(((f32[13,2048]{1,0:T(8,128)}), f32[13,65536]{1,0:T(8,128)}) %all-gather.2.cloned.1.call-update) | async-done | bytes 3407888 | tf_op jit(solution)/shard_map/all_gather | solution.py:146
  60.2 6.7 %multiply_reduce_fusion.1 = (f32[65536]{0:T(1024)S(1)}, f32[65536]{0:T(1024)S(1)}, f32[1,3,512,128]{3,1,2,0:T(4,128)S(1)}, f32[1,3,512,128]{3,1,2,0:T(4,128)S(1)...) fusion(f32[13,65536]{1,0:T(8,128)} %all-gather.2.cloned.1.call-done), kind=kLoop, calls=%fused_computation.45 | loop fusion | flops 2818048 | bytes 6815744 | tf_op jit(solution)/shard_map/reduce_sum | solution.py:59
  71.3 2.5 slice.201
  73.8 56.1 %shard_map.59 = f32[2,6,128,128]{3,2,1,0:T(8,128)} custom-call(s32[4]{0:T(128)} %get-tuple-element.99.ctl_ref, f32[2,6,128]{2,1,0:T(8,128)} %pad_maximum_fusion.5.tgt_ref, f32[6,512,128]{2,1,0:T(8,128)} %pad_maximum_fusion.src_ref, f32[512,128]{1,0:T(8,128)} %bitcast.166), custom_call_target="tpu_custom_call" | custom-call | tf_op jit(solution)/shard_map/pallas_call | solution.py:128
  132.4 7.5 %all-to-all-start = ((f32[128,2,6,128]{3,1,2,0:T(2,128)}), f32[128,2,6,128]{3,1,2,0:T(2,128)}, u32[]{:S(2)}, u32[]{:S(2)}) async-start(f32[128,2,6,128]{3,1,2,0:T(2,128)} %broadcast_in_dim.131), calls=%async_computation | async-start | bytes 1572864 | tf_op jit(solution)/shard_map/all_to_all | solution.py:201
  139.9 4.4 fusion.102
  171.5 5.2 slice_bitcast_fusion
  182.6 1.5 multiply_reduce_fusion.7
  186.5 110.4 %shard_map.60 = f32[2,6,128,128]{3,2,1,0:T(8,128)} custom-call(s32[4]{0:T(128)} %get-tuple-element.100.ctl_ref, f32[2,6,128]{2,1,0:T(8,128)} %pad_maximum_fusion.6.tgt_ref, f32[6,512,128]{2,1,0:T(8,128)} %pad_maximum_fusion.1.src_ref, f32[512,128]{1,0:T(8,128)} %bitcast.167), custom_call_target="tpu_custom_call" | custom-call | tf_op jit(solution)/shard_map/pallas_call | solution.py:128
  299.4 10.8 %all-to-all-start.1 = ((f32[128,2,6,128]{3,1,2,0:T(2,128)}), f32[128,2,6,128]{3,1,2,0:T(2,128)}, u32[]{:S(2)}, u32[]{:S(2)}) async-start(f32[128,2,6,128]{3,1,2,0:T(2,128)} %broadcast_in_dim.134), calls=%async_computation.1 | async-start | bytes 1572864 | tf_op jit(solution)/shard_map/all_to_all | solution.py:201
  311.3 2.5 broadcast_multiply_fusion.2
  313.8 12.4 %all-to-all-done.1 = f32[128,2,6,128]{3,1,2,0:T(2,128)} async-done(((f32[128,2,6,128]{3,1,2,0:T(2,128)}), f32[128,2,6,128]{3,1,2,0:T(2,128)}, u32[]{:S(2)}, u32[]{:S(2)}) %all-to-all-start.1) | async-done | bytes 786464 | tf_op jit(solution)/shard_map/all_to_all | solution.py:201
  326.3 1.5 copy.125
  329.6 2.4 broadcast_select_fusion
  335.4 56.1 %shard_map.61 = f32[2,6,128,128]{3,2,1,0:T(8,128)} custom-call(s32[4]{0:T(128)} %get-tuple-element.101.ctl_ref, f32[2,6,128]{2,1,0:T(8,128)} %pad_maximum_fusion.7.tgt_ref, f32[6,512,128]{2,1,0:T(8,128)} %pad_maximum_fusion.2.src_ref, f32[512,128]{1,0:T(8,128)} %bitcast.168), custom_call_target="tpu_custom_call" | custom-call | tf_op jit(solution)/shard_map/pallas_call | solution.py:128
  394.1 5.4 all-to-all-start.2
  401.5 2.5 broadcast_multiply_fusion.1
  404.0 11.7 %all-to-all-done.2 = f32[128,2,6,128]{3,1,2,0:T(2,128)} async-done(((f32[128,2,6,128]{3,1,2,0:T(2,128)}), f32[128,2,6,128]{3,1,2,0:T(2,128)}, u32[]{:S(2)}, u32[]{:S(2)}) %all-to-all-start.2) | async-done | bytes 786464 | tf_op jit(solution)/shard_map/all_to_all | solution.py:201
  415.7 1.5 copy.135
  423.0 174.3 %shard_map.62 = f32[2,6,128,128]{3,2,1,0:T(8,128)} custom-call(s32[4]{0:T(128)} %get-tuple-element.102.ctl_ref, f32[2,6,128]{2,1,0:T(8,128)} %pad_maximum_fusion.8.tgt_ref, f32[6,512,128]{2,1,0:T(8,128)} %pad_maximum_fusion.3.src_ref, f32[512,128]{1,0:T(8,128)} %bitcast.169), custom_call_target="tpu_custom_call" | custom-call | tf_op jit(solution)/shard_map/pallas_call | solution.py:128
  599.8 4.5 all-to-all-start.3
  605.9 14.9 %all-to-all-done.3 = f32[128,2,6,128]{3,1,2,0:T(2,128)S(1)} async-done(((f32[128,2,6,128]{3,1,2,0:T(2,128)}), f32[128,2,6,128]{3,1,2,0:T(2,128)S(1)}, u32[]{:S(2)}, u32[]{:S(2)}) %all-to-all-start.3) | async-done | bytes 786464 | tf_op jit(solution)/shard_map/all_to_all | solution.py:201
  (251 shorter events, 80.5 us)
Async XLA Ops:
  7.2 53.0 %all-gather.2.cloned.1.call-start = ((), (), s32[]{:S(2)}) async-start(), calls=%async_computation.4 | async-start | bytes 4325376 | tf_op jit(solution)/shard_map/all_gather | solution.py:146
  132.4 44.3 %all-to-all-start = ((f32[128,2,6,128]{3,1,2,0:T(2,128)}), f32[128,2,6,128]{3,1,2,0:T(2,128)}, u32[]{:S(2)}, u32[]{:S(2)}) async-start(f32[128,2,6,128]{3,1,2,0:T(2,128)} %broadcast_in_dim.131), calls=%async_computation | async-start | bytes 1572864 | tf_op jit(solution)/shard_map/all_to_all | solution.py:201
  163.4 4.0 copy-start.33
  170.9 5.8 copy-start.27
  170.9 5.8 copy-start.29
  176.7 1.6 copy-start.22
  179.5 2.2 copy-start.15
  182.5 146.3 %copy-start = (f32[6,512,128]{2,1,0:T(8,128)}, f32[6,512,128]{2,1,0:T(8,128)S(1)}, u32[]{:S(2)}) copy-start(f32[6,512,128]{2,1,0:T(8,128)S(1)} %get-tuple-element.95) | copy-start | bytes 4718596
  182.5 146.3 %copy-start.1 = (f32[6,512,128]{2,1,0:T(8,128)}, f32[6,512,128]{2,1,0:T(8,128)S(1)}, u32[]{:S(2)}) copy-start(f32[6,512,128]{2,1,0:T(8,128)S(1)} %get-tuple-element.96) | copy-start | bytes 4718596
  184.1 1.7 copy-start.11
  299.4 26.9 %all-to-all-start.1 = ((f32[128,2,6,128]{3,1,2,0:T(2,128)}), f32[128,2,6,128]{3,1,2,0:T(2,128)}, u32[]{:S(2)}, u32[]{:S(2)}) async-start(f32[128,2,6,128]{3,1,2,0:T(2,128)} %broadcast_in_dim.134), calls=%async_computation.1 | async-start | bytes 1572864 | tf_op jit(solution)/shard_map/all_to_all | solution.py:201
  313.8 13.9 %copy-start.32 = (s32[256]{0:T(256)S(1)}, s32[256]{0:T(256)}, u32[]{:S(2)}) copy-start(s32[256]{0:T(256)} %eq.141) | copy-start | bytes 3076
  326.2 1.6 copy-start.17
  329.6 2.4 copy-start.24
  333.1 1.7 copy-start.8
  394.1 21.6 %all-to-all-start.2 = ((f32[128,2,6,128]{3,1,2,0:T(2,128)}), f32[128,2,6,128]{3,1,2,0:T(2,128)}, u32[]{:S(2)}, u32[]{:S(2)}) async-start(f32[128,2,6,128]{3,1,2,0:T(2,128)} %broadcast_in_dim.135), calls=%async_computation.2 | async-start | bytes 1572864 | tf_op jit(solution)/shard_map/all_to_all | solution.py:201
  399.5 2.0 copy-start.7
  404.0 13.3 %copy-start.31 = (s32[256]{0:T(256)S(1)}, s32[256]{0:T(256)}, u32[]{:S(2)}) copy-start(s32[256]{0:T(256)} %eq.145) | copy-start | bytes 3076
  415.7 1.6 copy-start.19
  419.5 1.7 copy-start.4
  597.3 7.3 %copy-start.34 = (s32[128]{0:T(128)S(1)}, s32[128]{0:T(128)}, u32[]{:S(2)}) copy-start(s32[128]{0:T(128)} %copy-done.33) | copy-start | bytes 1540
  599.8 21.0 %all-to-all-start.3 = ((f32[128,2,6,128]{3,1,2,0:T(2,128)}), f32[128,2,6,128]{3,1,2,0:T(2,128)S(1)}, u32[]{:S(2)}, u32[]{:S(2)}) async-start(f32[128,2,6,128]{3,1,2,0:T(2,128)} %broadcast_in_dim.136), calls=%async_computation.3 | async-start | bytes 1572864 | tf_op jit(solution)/shard_map/all_to_all | solution.py:201
  605.9 15.1 %copy-start.20 = (f32[3,512,128]{2,1,0:T(8,128)S(1)}, f32[3,512,128]{2,1,0:T(8,128)}, u32[]{:S(2)}) copy-start(f32[3,512,128]{2,1,0:T(8,128)} %get-tuple-element.51) | copy-start | bytes 2359300
  621.1 1.9 copy-start.5
  (16 other events, 19.8 us)
Sparse Core Ops, SparseCore 0:
  10.3 49.8 all-gather.1

commit v5 on v4

--- a/solution.py
+++ b/solution.py
@@ -10,6 +10,7 @@
 from jax.experimental.pallas import tpu as pltpu
 
 BLK = 128
+GROUP = 8
 STEPS = 4
 
 
@@ -115,8 +116,13 @@
                     acc[5] + inv_cube * (rel_z - radial * sep_z),
                 )
 
+            def per_group(g, acc):
+                for k in range(GROUP):
+                    acc = per_tile(g * GROUP + k, acc)
+                return acc
+
             zero = jnp.zeros((8, 128), jnp.float32)
-            acc = lax.fori_loop(lo, hi, per_tile, (zero,) * 6)
+            acc = lax.fori_loop(lo, hi, per_group, (zero,) * 6)
             for k in range(6):
                 out_ref[part, k, pl.ds(t, 1), :] = jnp.sum(acc[k], axis=0, keepdims=True)
             return carry
@@ -150,7 +156,7 @@
     mass = full[12]
     phase = full[0:6]
     deriv = full[6:12]
-    tiles = block_total // 8
+    tiles = block_total // (8 * GROUP)
     slots = active_lists.shape[1] * active_lists.shape[2]
     devices = lax.axis_size("ia") * lax.axis_size("ja") * lax.axis_size("ha")
     my_unit = (

time: 633 us -> 390 us (0.62)
  Pallas kernels: 397 us -> 154 us
    pallas_call x4, Pallas kernels: 397 us -> 154 us  [kernel_forces(): pl.pallas_call(_force_kernel, out_shape=jax.ShapeDtypeStruct((2, 6, targe...]
  transfers between devices with their start and end apart: 5 -> 5, of which waited for: 4 -> 4; matrix products, arithmetic and copies ran while one was open for 10% -> 16% of each run, Pallas kernels for 0% -> 0%
where the time goes in v5:
time: 390 us; the launch traced here: 388 us
  Pallas kernels  154 us (39%)
  local copies, waits for them, and re-layouts  57.2 us (15%)
  other arithmetic  56.1 us (14%)
  waiting for transfers between devices  52 us (13%)
  between operations  37.4 us (10%)
  starting transfers between devices  28 us (7%)
    pallas_call x4, Pallas kernels, kernel_forces(): pl.pallas_call(_force_kernel, out_shape=jax.ShapeDtypeStruct((2, 6, targe...  154 us
    all_to_all x4, waiting for transfers between devices, shards(): lax.all_to_all(sent, every, 0, 0, tiled=True).reshape(2 * devices, 6, BLK)  39 us
    all_to_all x4, starting transfers between devices, shards(): lax.all_to_all(sent, every, 0, 0, tiled=True).reshape(2 * devices, 6, BLK)  27.9 us
    all_gather x1, waiting for transfers between devices, shards(): full = lax.all_gather(local, plane, axis=1, tiled=True)  13 us
    unnamed x73, local copies, waits for them, and re-layouts  12 us
    reduce_sum x4, other arithmetic, star_terms(): inv_r = lax.rsqrt(jnp.sum(position * position, axis=0))  9.88 us
    another operation x2, other arithmetic, shards(): jnp.stack([lo_a[my_unit], hi_a[my_unit], jnp.zeros_like(hi_b[my_unit]), h...  8.81 us
  transfers between devices with their start and end apart: 5, of which 4 were waited for; matrix products, arithmetic and copies ran while one was open for 16% of the time, Pallas kernels for 0%

profile of v5, /device:TPU:1, one launch (start us, length us, event | category | flops | bytes accessed | tf_op | source)
XLA Modules:
  0.0 388.3 jit_solution(6319504781837154784)
XLA Ops:
  7.2 1.6 pad_maximum_fusion.4
  41.8 4.4 %fusion.100 = (s32[4]{0:T(128)}, s32[4]{0:T(128)}) fusion(s32[1]{0:T(128)} %constant.190.clone.1, s32[1]{0:T(128)} %dynamic_slice.117, s32[1]{0:T(128)} %dynamic_slice.116, s32[1]{0:T(128)} %dynamic_slice.115, s32[1]{0:T(128)} %dynamic_slice.126, s32[1]{0:T(128)} %dynamic_slice.125, s32[1]{0:T(128)} %dynamic_slice.124), kind=kLoop, calls=%fused_computation.306 | loop fusion | flops 24 | bytes 60 | tf_op jit(solution)/shard_map/stack | solution.py:191
  47.2 13.0 %all-gather.2.cloned.1.call-done = f32[13,65536]{1,0:T(8,128)} async-done(((f32[13,2048]{1,0:T(8,128)}), f32[13,65536]{1,0:T(8,128)}) %all-gather.2.cloned.1.call-update) | async-done | bytes 3407888 | tf_op jit(solution)/shard_map/all_gather | solution.py:152
  60.2 6.7 %multiply_reduce_fusion.1 = (f32[65536]{0:T(1024)S(1)}, f32[65536]{0:T(1024)S(1)}, f32[1,3,512,128]{3,1,2,0:T(4,128)S(1)}, f32[1,3,512,128]{3,1,2,0:T(4,128)S(1)...) fusion(f32[13,65536]{1,0:T(8,128)} %all-gather.2.cloned.1.call-done), kind=kLoop, calls=%fused_computation.45 | loop fusion | flops 2818048 | bytes 6815744 | tf_op jit(solution)/shard_map/reduce_sum | solution.py:60
  71.3 2.5 slice.201
  73.8 25.8 %shard_map.59 = f32[2,6,128,128]{3,2,1,0:T(8,128)} custom-call(s32[4]{0:T(128)} %get-tuple-element.99.ctl_ref, f32[2,6,128]{2,1,0:T(8,128)} %pad_maximum_fusion.5.tgt_ref, f32[6,512,128]{2,1,0:T(8,128)} %pad_maximum_fusion.src_ref, f32[512,128]{1,0:T(8,128)} %bitcast.166), custom_call_target="tpu_custom_call" | custom-call | tf_op jit(solution)/shard_map/pallas_call | solution.py:134
  102.2 7.7 %all-to-all-start = ((f32[128,2,6,128]{3,1,2,0:T(2,128)}), f32[128,2,6,128]{3,1,2,0:T(2,128)}, u32[]{:S(2)}, u32[]{:S(2)}) async-start(f32[128,2,6,128]{3,1,2,0:T(2,128)} %broadcast_in_dim.131), calls=%async_computation | async-start | bytes 1572864 | tf_op jit(solution)/shard_map/all_to_all | solution.py:207
  109.8 4.4 %fusion.102 = (s32[4]{0:T(128)}, s32[4]{0:T(128)}) fusion(s32[1]{0:T(128)} %constant.190.clone.1, s32[1]{0:T(128)} %dynamic_slice.135, s32[1]{0:T(128)} %dynamic_slice.134, s32[1]{0:T(128)} %dynamic_slice.133, s32[1]{0:T(128)} %dynamic_slice.144, s32[1]{0:T(128)} %dynamic_slice.143, s32[1]{0:T(128)} %dynamic_slice.142), kind=kLoop, calls=%fused_computation.308 | loop fusion | flops 24 | bytes 60 | tf_op jit(solution)/shard_map/stack | solution.py:191
  141.4 5.2 %slice_bitcast_fusion = (f32[1,6,512,128]{3,1,2,0:T(8,128)}, f32[1,6,512,128]{3,1,2,0:T(8,128)}) fusion(f32[13,65536]{1,0:T(8,128)} %all-gather.2.cloned.1.call-done), kind=kLoop, calls=%fused_computation.32 | loop fusion | bytes 6291456
  152.5 1.5 multiply_reduce_fusion.7
  156.4 44.6 %shard_map.60 = f32[2,6,128,128]{3,2,1,0:T(8,128)} custom-call(s32[4]{0:T(128)} %get-tuple-element.100.ctl_ref, f32[2,6,128]{2,1,0:T(8,128)} %pad_maximum_fusion.6.tgt_ref, f32[6,512,128]{2,1,0:T(8,128)} %pad_maximum_fusion.1.src_ref, f32[512,128]{1,0:T(8,128)} %bitcast.167), custom_call_target="tpu_custom_call" | custom-call | tf_op jit(solution)/shard_map/pallas_call | solution.py:134
  203.5 10.4 %all-to-all-start.1 = ((f32[128,2,6,128]{3,1,2,0:T(2,128)}), f32[128,2,6,128]{3,1,2,0:T(2,128)}, u32[]{:S(2)}, u32[]{:S(2)}) async-start(f32[128,2,6,128]{3,1,2,0:T(2,128)} %broadcast_in_dim.134), calls=%async_computation.1 | async-start | bytes 1572864 | tf_op jit(solution)/shard_map/all_to_all | solution.py:207
  215.1 2.5 broadcast_multiply_fusion.2
  217.6 12.4 %all-to-all-done.1 = f32[128,2,6,128]{3,1,2,0:T(2,128)} async-done(((f32[128,2,6,128]{3,1,2,0:T(2,128)}), f32[128,2,6,128]{3,1,2,0:T(2,128)}, u32[]{:S(2)}, u32[]{:S(2)}) %all-to-all-start.1) | async-done | bytes 786464 | tf_op jit(solution)/shard_map/all_to_all | solution.py:207
  230.0 1.5 copy.125
  233.3 2.4 broadcast_select_fusion
  239.2 25.8 %shard_map.61 = f32[2,6,128,128]{3,2,1,0:T(8,128)} custom-call(s32[4]{0:T(128)} %get-tuple-element.101.ctl_ref, f32[2,6,128]{2,1,0:T(8,128)} %pad_maximum_fusion.7.tgt_ref, f32[6,512,128]{2,1,0:T(8,128)} %pad_maximum_fusion.2.src_ref, f32[512,128]{1,0:T(8,128)} %bitcast.168), custom_call_target="tpu_custom_call" | custom-call | tf_op jit(solution)/shard_map/pallas_call | solution.py:134
  267.6 5.4 %all-to-all-start.2 = ((f32[128,2,6,128]{3,1,2,0:T(2,128)}), f32[128,2,6,128]{3,1,2,0:T(2,128)}, u32[]{:S(2)}, u32[]{:S(2)}) async-start(f32[128,2,6,128]{3,1,2,0:T(2,128)} %broadcast_in_dim.135), calls=%async_computation.2 | async-start | bytes 1572864 | tf_op jit(solution)/shard_map/all_to_all | solution.py:207
  275.0 2.5 broadcast_multiply_fusion.1
  277.5 11.7 %all-to-all-done.2 = f32[128,2,6,128]{3,1,2,0:T(2,128)} async-done(((f32[128,2,6,128]{3,1,2,0:T(2,128)}), f32[128,2,6,128]{3,1,2,0:T(2,128)}, u32[]{:S(2)}, u32[]{:S(2)}) %all-to-all-start.2) | async-done | bytes 786464 | tf_op jit(solution)/shard_map/all_to_all | solution.py:207
  289.2 1.5 copy.135
  296.5 57.5 %shard_map.62 = f32[2,6,128,128]{3,2,1,0:T(8,128)} custom-call(s32[4]{0:T(128)} %get-tuple-element.102.ctl_ref, f32[2,6,128]{2,1,0:T(8,128)} %pad_maximum_fusion.8.tgt_ref, f32[6,512,128]{2,1,0:T(8,128)} %pad_maximum_fusion.3.src_ref, f32[512,128]{1,0:T(8,128)} %bitcast.169), custom_call_target="tpu_custom_call" | custom-call | tf_op jit(solution)/shard_map/pallas_call | solution.py:134
  356.5 4.5 %all-to-all-start.3 = ((f32[128,2,6,128]{3,1,2,0:T(2,128)}), f32[128,2,6,128]{3,1,2,0:T(2,128)S(1)}, u32[]{:S(2)}, u32[]{:S(2)}) async-start(f32[128,2,6,128]{3,1,2,0:T(2,128)} %broadcast_in_dim.136), calls=%async_computation.3 | async-start | bytes 1572864 | tf_op jit(solution)/shard_map/all_to_all | solution.py:207
  362.6 14.9 %all-to-all-done.3 = f32[128,2,6,128]{3,1,2,0:T(2,128)S(1)} async-done(((f32[128,2,6,128]{3,1,2,0:T(2,128)}), f32[128,2,6,128]{3,1,2,0:T(2,128)S(1)}, u32[]{:S(2)}, u32[]{:S(2)}) %all-to-all-start.3) | async-done | bytes 786464 | tf_op jit(solution)/shard_map/all_to_all | solution.py:207
  (251 shorter events, 80.5 us)
Async XLA Ops:
  7.2 53.0 %all-gather.2.cloned.1.call-start = ((), (), s32[]{:S(2)}) async-start(), calls=%async_computation.4 | async-start | bytes 4325376 | tf_op jit(solution)/shard_map/all_gather | solution.py:152
  102.2 44.4 %all-to-all-start = ((f32[128,2,6,128]{3,1,2,0:T(2,128)}), f32[128,2,6,128]{3,1,2,0:T(2,128)}, u32[]{:S(2)}, u32[]{:S(2)}) async-start(f32[128,2,6,128]{3,1,2,0:T(2,128)} %broadcast_in_dim.131), calls=%async_computation | async-start | bytes 1572864 | tf_op jit(solution)/shard_map/all_to_all | solution.py:207
  133.3 4.0 %copy-start.33 = (s32[128]{0:T(128)}, s32[128]{0:T(128)S(1)}, u32[]{:S(2)}) copy-start(s32[128]{0:T(128)S(1)} %reshape.998) | copy-start | bytes 1540
  140.8 5.8 %copy-start.27 = (pred[512]{0:T(512)(128)(4,1)}, pred[512]{0:T(512)(128)(4,1)S(1)}, u32[]{:S(2)}) copy-start(pred[512]{0:T(512)(128)(4,1)S(1)} %get-tuple-element.113) | copy-start | bytes 1540
  140.8 5.8 %copy-start.29 = (pred[512]{0:T(512)(128)(4,1)}, pred[512]{0:T(512)(128)(4,1)S(1)}, u32[]{:S(2)}) copy-start(pred[512]{0:T(512)(128)(4,1)S(1)} %get-tuple-element.114) | copy-start | bytes 1540
  146.6 1.6 copy-start.22
  149.4 2.2 copy-start.15
  152.4 80.2 %copy-start = (f32[6,512,128]{2,1,0:T(8,128)}, f32[6,512,128]{2,1,0:T(8,128)S(1)}, u32[]{:S(2)}) copy-start(f32[6,512,128]{2,1,0:T(8,128)S(1)} %get-tuple-element.95) | copy-start | bytes 4718596
  152.4 80.2 %copy-start.1 = (f32[6,512,128]{2,1,0:T(8,128)}, f32[6,512,128]{2,1,0:T(8,128)S(1)}, u32[]{:S(2)}) copy-start(f32[6,512,128]{2,1,0:T(8,128)S(1)} %get-tuple-element.96) | copy-start | bytes 4718596
  154.0 1.7 copy-start.11
  203.5 26.5 %all-to-all-start.1 = ((f32[128,2,6,128]{3,1,2,0:T(2,128)}), f32[128,2,6,128]{3,1,2,0:T(2,128)}, u32[]{:S(2)}, u32[]{:S(2)}) async-start(f32[128,2,6,128]{3,1,2,0:T(2,128)} %broadcast_in_dim.134), calls=%async_computation.1 | async-start | bytes 1572864 | tf_op jit(solution)/shard_map/all_to_all | solution.py:207
  217.6 13.9 %copy-start.32 = (s32[256]{0:T(256)S(1)}, s32[256]{0:T(256)}, u32[]{:S(2)}) copy-start(s32[256]{0:T(256)} %eq.141) | copy-start | bytes 3076
  230.0 1.6 copy-start.17
  233.3 2.4 copy-start.24
  236.9 1.7 copy-start.8
  267.6 21.6 %all-to-all-start.2 = ((f32[128,2,6,128]{3,1,2,0:T(2,128)}), f32[128,2,6,128]{3,1,2,0:T(2,128)}, u32[]{:S(2)}, u32[]{:S(2)}) async-start(f32[128,2,6,128]{3,1,2,0:T(2,128)} %broadcast_in_dim.135), calls=%async_computation.2 | async-start | bytes 1572864 | tf_op jit(solution)/shard_map/all_to_all | solution.py:207
  273.0 2.0 copy-start.7
  277.5 13.3 %copy-start.31 = (s32[256]{0:T(256)S(1)}, s32[256]{0:T(256)}, u32[]{:S(2)}) copy-start(s32[256]{0:T(256)} %eq.145) | copy-start | bytes 3076
  289.2 1.6 copy-start.19
  293.0 1.7 copy-start.4
  354.0 7.3 %copy-start.34 = (s32[128]{0:T(128)S(1)}, s32[128]{0:T(128)}, u32[]{:S(2)}) copy-start(s32[128]{0:T(128)} %copy-done.33) | copy-start | bytes 1540
  356.5 21.0 %all-to-all-start.3 = ((f32[128,2,6,128]{3,1,2,0:T(2,128)}), f32[128,2,6,128]{3,1,2,0:T(2,128)S(1)}, u32[]{:S(2)}, u32[]{:S(2)}) async-start(f32[128,2,6,128]{3,1,2,0:T(2,128)} %broadcast_in_dim.136), calls=%async_computation.3 | async-start | bytes 1572864 | tf_op jit(solution)/shard_map/all_to_all | solution.py:207
  362.6 15.1 %copy-start.20 = (f32[3,512,128]{2,1,0:T(8,128)S(1)}, f32[3,512,128]{2,1,0:T(8,128)}, u32[]{:S(2)}) copy-start(f32[3,512,128]{2,1,0:T(8,128)} %get-tuple-element.51) | copy-start | bytes 2359300
  377.8 1.9 copy-start.5
  (16 other events, 19.8 us)
Sparse Core Ops, SparseCore 0:
  10.3 49.8 all-gather.1

commit v6 on v5

--- a/solution.py
+++ b/solution.py
@@ -153,9 +153,6 @@
     total = full.shape[1]
     block_total = total // BLK
     full = full.reshape(13, block_total, BLK)
-    mass = full[12]
-    phase = full[0:6]
-    deriv = full[6:12]
     tiles = block_total // (8 * GROUP)
     slots = active_lists.shape[1] * active_lists.shape[2]
     devices = lax.axis_size("ia") * lax.axis_size("ja") * lax.axis_size("ha")
@@ -165,8 +162,8 @@
     all_blocks = jnp.arange(block_total, dtype=jnp.int32)
     units = jnp.arange(devices, dtype=jnp.int32)
     last_blk = jnp.zeros((block_total,), jnp.float32)
+    plans = []
     for step_index in range(STEPS):
-        now_time = (step_index + 1) * time_step
         flat = active_lists[step_index].reshape(-1)
         live = flat >= 0
         live_count = jnp.sum(live.astype(jnp.int32))
@@ -193,6 +190,16 @@
         ).astype(jnp.int32)
         id_a = jnp.clip(compact[job_a[my_unit]], 0, block_total - 1)
         id_b = jnp.clip(compact[job_b[my_unit]], 0, block_total - 1)
+        onehot = (all_blocks[:, None] == owner_all[None, :]).astype(jnp.float32)
+        active_flags = jnp.any(flat[:, None] == all_blocks[None, :], axis=0)
+        plans.append((ranges, id_a, id_b, onehot, active_flags))
+    plans, full = lax.optimization_barrier((plans, full))
+    mass = full[12]
+    phase = full[0:6]
+    deriv = full[6:12]
+    for step_index in range(STEPS):
+        now_time = (step_index + 1) * time_step
+        ranges, id_a, id_b, onehot, active_flags = plans[step_index]
         elapsed_blk = now_time - last_blk
         elapsed = elapsed_blk[None, :, None]
         predicted = predict(phase, deriv, elapsed)
@@ -205,14 +212,12 @@
         partial = kernel_forces(ranges, targets, predicted, mass)
         sent = jnp.broadcast_to(partial[None], (devices,) + partial.shape)
         got = lax.all_to_all(sent, every, 0, 0, tiled=True).reshape(2 * devices, 6, BLK)
-        onehot = (all_blocks[:, None] == owner_all[None, :]).astype(jnp.float32)
         mutual = jnp.einsum(
             "bu,ucl->cbl", onehot, got,
             precision=lax.Precision.HIGHEST, preferred_element_type=jnp.float32,
         )
         fresh = mutual + star_terms(predicted)
         corrected = correct(phase, deriv, fresh, elapsed)
-        active_flags = jnp.any(flat[:, None] == all_blocks[None, :], axis=0)
         active = active_flags[None, :, None]
         phase = jnp.where(active, corrected, phase)
         deriv = jnp.where(active, fresh, deriv)

time: 390 us -> 384 us (0.985)
  local copies, waits for them, and re-layouts: 57.2 us -> 50.1 us
  other arithmetic: 56.1 us -> 51.2 us
  matrix products: 3.86 us -> 8.34 us
    all_to_all x4, waiting for transfers between devices: 39 us -> 55.5 us  [shards(): lax.all_to_all(sent, every, 0, 0, tiled=True).reshape(2 * devices, 6, BLK)]
    all_gather x1, waiting for transfers between devices: 13 us -> 0.01 us  [shards(): full = lax.all_gather(local, plane, axis=1, tiled=True)]
    reduce_sum x4, other arithmetic: 9.88 us -> 4.48 us  [star_terms(): inv_r = lax.rsqrt(jnp.sum(position * position, axis=0))]
    dot_general x4, matrix products: 3.86 us -> 8.34 us  [shards(): jnp.einsum('bu,ucl->cbl', onehot, got, precision=lax.Precision.HIGHEST, p...]
    unnamed x73 -> x43, local copies, waits for them, and re-layouts: 12 us -> 9.44 us
  transfers between devices with their start and end apart: 5 -> 5, of which waited for: 4 -> 4; matrix products, arithmetic and copies ran while one was open for 16% -> 15% of each run, Pallas kernels for 0% -> 0%
where the time goes in v6:
time: 384 us; the launch traced here: 382 us
  Pallas kernels  154 us (40%)
  waiting for transfers between devices  55.6 us (14%)
  other arithmetic  51.2 us (13%)
  local copies, waits for them, and re-layouts  50.1 us (13%)
  between operations  37.2 us (10%)
  starting transfers between devices  26.3 us (7%)
  matrix products  8.34 us (2%)
    pallas_call x4, Pallas kernels, kernel_forces(): pl.pallas_call(_force_kernel, out_shape=jax.ShapeDtypeStruct((2, 6, targe...  154 us
    all_to_all x4, waiting for transfers between devices, shards(): lax.all_to_all(sent, every, 0, 0, tiled=True).reshape(2 * devices, 6, BLK)  55.5 us
    all_to_all x4, starting transfers between devices, shards(): lax.all_to_all(sent, every, 0, 0, tiled=True).reshape(2 * devices, 6, BLK)  26.2 us
    unnamed x43, local copies, waits for them, and re-layouts  9.44 us
    another operation x2, other arithmetic, shards(): jnp.stack([lo_a[my_unit], hi_a[my_unit], jnp.zeros_like(hi_b[my_unit]), h...  8.88 us
    dot_general x4, matrix products, shards(): jnp.einsum('bu,ucl->cbl', onehot, got, precision=lax.Precision.HIGHEST, p...  8.34 us
  transfers between devices with their start and end apart: 5, of which 4 were waited for; matrix products, arithmetic and copies ran while one was open for 15% of the time, Pallas kernels for 0%

profile of v6, /device:TPU:1, one launch (start us, length us, event | category | flops | bytes accessed | tf_op | source)
XLA Modules:
  0.0 382.4 jit_solution(10873036075680506157)
XLA Ops:
  7.2 1.6 pad_maximum_fusion.4
  67.7 4.4 %fusion.84 = (s32[4]{0:T(128)}, s32[4]{0:T(128)}) fusion(s32[1]{0:T(128)} %constant.179.clone.1, s32[1]{0:T(128)} %dynamic_slice.131, s32[1]{0:T(128)} %dynamic_slice.130, s32[1]{0:T(128)} %dynamic_slice.129, s32[1]{0:T(128)} %dynamic_slice.138, s32[1]{0:T(128)} %dynamic_slice.137, s32[1]{0:T(128)} %dynamic_slice.136), kind=kLoop, calls=%fused_computation.285 | loop fusion | flops 24 | bytes 60 | tf_op jit(solution)/shard_map/stack | solution.py:188
  72.2 4.4 %fusion.82 = (s32[4]{0:T(128)}, s32[4]{0:T(128)}) fusion(s32[1]{0:T(128)} %constant.179.clone.1, s32[1]{0:T(128)} %dynamic_slice.117, s32[1]{0:T(128)} %dynamic_slice.116, s32[1]{0:T(128)} %dynamic_slice.115, s32[1]{0:T(128)} %dynamic_slice.124, s32[1]{0:T(128)} %dynamic_slice.123, s32[1]{0:T(128)} %dynamic_slice.122), kind=kLoop, calls=%fused_computation.283 | loop fusion | flops 24 | bytes 60 | tf_op jit(solution)/shard_map/stack | solution.py:188
  80.3 3.0 copy.158
  83.6 2.4 multiply_reduce_fusion.7
  86.7 2.6 pad_maximum_fusion.src_ref
  90.7 25.8 %shard_map.59 = f32[2,6,128,128]{3,2,1,0:T(8,128)} custom-call(s32[4]{0:T(128)} %get-tuple-element.28.ctl_ref, f32[2,6,128]{2,1,0:T(8,128)} %pad_maximum_fusion.5.tgt_ref, f32[6,512,128]{2,1,0:T(8,128)} %pad_maximum_fusion.src_ref, f32[512,128]{1,0:T(8,128)} %slice_bitcast_fusion.mass_ref), custom_call_target="tpu_custom_call" | custom-call | tf_op jit(solution)/shard_map/pallas_call | solution.py:134
  119.1 11.7 %all-to-all-start = ((f32[128,2,6,128]{3,1,2,0:T(2,128)}), f32[128,2,6,128]{3,1,2,0:T(2,128)}, u32[]{:S(2)}, u32[]{:S(2)}) async-start(f32[128,2,6,128]{3,1,2,0:T(2,128)} %broadcast_in_dim.131), calls=%async_computation | async-start | bytes 1572864 | tf_op jit(solution)/shard_map/all_to_all | solution.py:214
  132.1 2.5 broadcast_multiply_fusion.3
  134.6 12.3 %all-to-all-done = f32[128,2,6,128]{3,1,2,0:T(2,128)} async-done(((f32[128,2,6,128]{3,1,2,0:T(2,128)}), f32[128,2,6,128]{3,1,2,0:T(2,128)}, u32[]{:S(2)}, u32[]{:S(2)}) %all-to-all-start) | async-done | bytes 786464 | tf_op jit(solution)/shard_map/all_to_all | solution.py:214
  148.5 2.6 maximum_add_fusion
  155.6 44.6 %shard_map.60 = f32[2,6,128,128]{3,2,1,0:T(8,128)} custom-call(s32[4]{0:T(128)} %get-tuple-element.32.ctl_ref, f32[2,6,128]{2,1,0:T(8,128)} %pad_maximum_fusion.6.tgt_ref, f32[6,512,128]{2,1,0:T(8,128)} %pad_maximum_fusion.1.src_ref, f32[512,128]{1,0:T(8,128)} %slice_bitcast_fusion.mass_ref), custom_call_target="tpu_custom_call" | custom-call | tf_op jit(solution)/shard_map/pallas_call | solution.py:134
  202.7 4.6 %all-to-all-start.1 = ((f32[128,2,6,128]{3,1,2,0:T(2,128)}), f32[128,2,6,128]{3,1,2,0:T(2,128)S(1)}, u32[]{:S(2)}, u32[]{:S(2)}) async-start(f32[128,2,6,128]{3,1,2,0:T(2,128)} %broadcast_in_dim.134), calls=%async_computation.1 | async-start | bytes 1572864 | tf_op jit(solution)/shard_map/all_to_all | solution.py:214
  208.5 15.4 %all-to-all-done.1 = f32[128,2,6,128]{3,1,2,0:T(2,128)S(1)} async-done(((f32[128,2,6,128]{3,1,2,0:T(2,128)}), f32[128,2,6,128]{3,1,2,0:T(2,128)S(1)}, u32[]{:S(2)}, u32[]{:S(2)}) %all-to-all-start.1) | async-done | bytes 786464 | tf_op jit(solution)/shard_map/all_to_all | solution.py:214
  224.9 1.6 maximum_add_fusion.1
  231.1 25.8 %shard_map.61 = f32[2,6,128,128]{3,2,1,0:T(8,128)} custom-call(s32[4]{0:T(128)} %get-tuple-element.36.ctl_ref, f32[2,6,128]{2,1,0:T(8,128)} %pad_maximum_fusion.7.tgt_ref, f32[6,512,128]{2,1,0:T(8,128)} %pad_maximum_fusion.2.src_ref, f32[512,128]{1,0:T(8,128)} %slice_bitcast_fusion.mass_ref), custom_call_target="tpu_custom_call" | custom-call | tf_op jit(solution)/shard_map/pallas_call | solution.py:134
  259.5 5.4 %all-to-all-start.2 = ((f32[128,2,6,128]{3,1,2,0:T(2,128)}), f32[128,2,6,128]{3,1,2,0:T(2,128)}, u32[]{:S(2)}, u32[]{:S(2)}) async-start(f32[128,2,6,128]{3,1,2,0:T(2,128)} %broadcast_in_dim.135), calls=%async_computation.2 | async-start | bytes 1572864 | tf_op jit(solution)/shard_map/all_to_all | solution.py:214
  266.1 2.5 broadcast_multiply_fusion.1
  268.6 12.6 %all-to-all-done.2 = f32[128,2,6,128]{3,1,2,0:T(2,128)} async-done(((f32[128,2,6,128]{3,1,2,0:T(2,128)}), f32[128,2,6,128]{3,1,2,0:T(2,128)}, u32[]{:S(2)}, u32[]{:S(2)}) %all-to-all-start.2) | async-done | bytes 786464 | tf_op jit(solution)/shard_map/all_to_all | solution.py:214
  282.7 2.6 maximum_add_fusion.2
  289.9 57.5 %shard_map.62 = f32[2,6,128,128]{3,2,1,0:T(8,128)} custom-call(s32[4]{0:T(128)} %get-tuple-element.40.ctl_ref, f32[2,6,128]{2,1,0:T(8,128)} %pad_maximum_fusion.8.tgt_ref, f32[6,512,128]{2,1,0:T(8,128)} %pad_maximum_fusion.3.src_ref, f32[512,128]{1,0:T(8,128)} %slice_bitcast_fusion.mass_ref), custom_call_target="tpu_custom_call" | custom-call | tf_op jit(solution)/shard_map/pallas_call | solution.py:134
  349.9 4.5 %all-to-all-start.3 = ((f32[128,2,6,128]{3,1,2,0:T(2,128)}), f32[128,2,6,128]{3,1,2,0:T(2,128)S(1)}, u32[]{:S(2)}, u32[]{:S(2)}) async-start(f32[128,2,6,128]{3,1,2,0:T(2,128)} %broadcast_in_dim.136), calls=%async_computation.3 | async-start | bytes 1572864 | tf_op jit(solution)/shard_map/all_to_all | solution.py:214
  355.6 15.2 %all-to-all-done.3 = f32[128,2,6,128]{3,1,2,0:T(2,128)S(1)} async-done(((f32[128,2,6,128]{3,1,2,0:T(2,128)}), f32[128,2,6,128]{3,1,2,0:T(2,128)S(1)}, u32[]{:S(2)}, u32[]{:S(2)}) %all-to-all-start.3) | async-done | bytes 786464 | tf_op jit(solution)/shard_map/all_to_all | solution.py:214
  371.9 1.6 maximum_add_fusion.3
  (224 shorter events, 77.9 us)
Async XLA Ops:
  7.2 73.2 %all-gather.2.cloned.1.call-start = ((), (), s32[]{:S(2)}) async-start(), calls=%async_computation.4 | async-start | bytes 4325376 | tf_op jit(solution)/shard_map/all_gather | solution.py:152
  119.1 27.9 %all-to-all-start = ((f32[128,2,6,128]{3,1,2,0:T(2,128)}), f32[128,2,6,128]{3,1,2,0:T(2,128)}, u32[]{:S(2)}, u32[]{:S(2)}) async-start(f32[128,2,6,128]{3,1,2,0:T(2,128)} %broadcast_in_dim.131), calls=%async_computation | async-start | bytes 1572864 | tf_op jit(solution)/shard_map/all_to_all | solution.py:214
  130.8 1.3 copy-start.8
  146.9 1.5 copy-start.12
  146.9 1.6 copy-start.13
  152.0 1.2 copy-start
  152.0 1.7 copy-start.2
  202.7 21.1 %all-to-all-start.1 = ((f32[128,2,6,128]{3,1,2,0:T(2,128)}), f32[128,2,6,128]{3,1,2,0:T(2,128)S(1)}, u32[]{:S(2)}, u32[]{:S(2)}) async-start(f32[128,2,6,128]{3,1,2,0:T(2,128)} %broadcast_in_dim.134), calls=%async_computation.1 | async-start | bytes 1572864 | tf_op jit(solution)/shard_map/all_to_all | solution.py:214
  208.5 15.7 %copy-start.14 = (f32[3,512,128]{2,1,0:T(8,128)S(1)}, f32[3,512,128]{2,1,0:T(8,128)}, u32[]{:S(2)}) copy-start(f32[3,512,128]{2,1,0:T(8,128)} %get-tuple-element.91) | copy-start | bytes 2359300
  223.9 1.0 copy-start.19
  224.9 1.6 copy-start.1
  224.9 1.9 copy-start.3
  228.8 1.4 copy-start.9
  228.8 1.7 copy-start.11
  259.5 21.6 %all-to-all-start.2 = ((f32[128,2,6,128]{3,1,2,0:T(2,128)}), f32[128,2,6,128]{3,1,2,0:T(2,128)}, u32[]{:S(2)}, u32[]{:S(2)}) async-start(f32[128,2,6,128]{3,1,2,0:T(2,128)} %broadcast_in_dim.135), calls=%async_computation.2 | async-start | bytes 1572864 | tf_op jit(solution)/shard_map/all_to_all | solution.py:214
  264.9 1.2 copy-start.10
  281.1 1.5 copy-start.15
  281.1 1.6 copy-start.16
  286.3 1.2 copy-start.4
  286.3 1.7 copy-start.6
  349.9 21.0 %all-to-all-start.3 = ((f32[128,2,6,128]{3,1,2,0:T(2,128)}), f32[128,2,6,128]{3,1,2,0:T(2,128)S(1)}, u32[]{:S(2)}, u32[]{:S(2)}) async-start(f32[128,2,6,128]{3,1,2,0:T(2,128)} %broadcast_in_dim.136), calls=%async_computation.3 | async-start | bytes 1572864 | tf_op jit(solution)/shard_map/all_to_all | solution.py:214
  355.6 15.5 %copy-start.17 = (f32[3,512,128]{2,1,0:T(8,128)S(1)}, f32[3,512,128]{2,1,0:T(8,128)}, u32[]{:S(2)}) copy-start(f32[3,512,128]{2,1,0:T(8,128)} %get-tuple-element.87) | copy-start | bytes 2359300
  371.9 1.6 copy-start.5
  371.9 1.9 copy-start.7
  (1 other events, 1.0 us)
Sparse Core Ops, SparseCore 0:
  10.3 49.8 all-gather.1

commit v7 on v5

--- a/solution.py
+++ b/solution.py
@@ -165,9 +165,12 @@
     all_blocks = jnp.arange(block_total, dtype=jnp.int32)
     units = jnp.arange(devices, dtype=jnp.int32)
     last_blk = jnp.zeros((block_total,), jnp.float32)
-    for step_index in range(STEPS):
-        now_time = (step_index + 1) * time_step
-        flat = active_lists[step_index].reshape(-1)
+    times = jnp.array([(s + 1) * time_step for s in range(STEPS)], jnp.float32)
+
+    def step(step_index, carry):
+        phase, deriv, last_blk = carry
+        now_time = times[step_index]
+        flat = lax.dynamic_index_in_dim(active_lists, step_index, 0, keepdims=False).reshape(-1)
         live = flat >= 0
         live_count = jnp.sum(live.astype(jnp.int32))
         rank = jnp.cumsum(live.astype(jnp.int32)) - 1
@@ -216,7 +219,10 @@
         active = active_flags[None, :, None]
         phase = jnp.where(active, corrected, phase)
         deriv = jnp.where(active, fresh, deriv)
-        last_blk = jnp.where(active_flags, jnp.float32(now_time), last_blk)
+        last_blk = jnp.where(active_flags, now_time, last_blk)
+        return phase, deriv, last_blk
+
+    phase, deriv, last_blk = lax.fori_loop(0, STEPS, step, (phase, deriv, last_blk))
     local_count = phase_space.shape[1]
     local_blocks = local_count // BLK
     offset = (lax.axis_index("ja") * lax.axis_size("ha") + lax.axis_index("ha")) * local_blocks

time: 390 us -> 426 us (1.092)
  loops' own time: 0 us -> 24.1 us
  between operations: 37.4 us -> 14.1 us
  waiting for transfers between devices: 52 us -> 73.3 us
  local copies, waits for them, and re-layouts: 57.2 us -> 68.1 us
  other arithmetic: 56.1 us -> 63 us
    all_gather x1, waiting for transfers between devices: 13 us -> 51.3 us  [shards(): full = lax.all_gather(local, plane, axis=1, tiled=True)]
    another operation x0 -> x1, loops' own time: none -> 24.1 us  [shards(): lax.fori_loop(0, STEPS, step, (phase, deriv, last_blk))]
    all_to_all x4, waiting for transfers between devices: 39 us -> 22 us  [step(): lax.all_to_all(sent, every, 0, 0, tiled=True).reshape(2 * devices, 6, BLK)]
    gather x16, local copies, waits for them, and re-layouts: 11.3 us -> 22.4 us  [the longest x8 12.4 us: step(): owner_a = jnp.where(hi_a > lo_a, compact[job_a], -1)]
    unnamed x73 -> x7, local copies, waits for them, and re-layouts: 12 us -> 4.53 us
    reduce_sum x4, other arithmetic: 9.88 us -> 4.67 us  [star_terms(): inv_r = lax.rsqrt(jnp.sum(position * position, axis=0))]
    dynamic_slice x25 -> x28, local copies, waits for them, and re-layouts: 14.7 us -> 16.8 us  [the longest x8 4.83 us: step(): id_a = jnp.clip(compact[job_a[my_unit]], 0, block_total - 1)]
    another operation x18 -> x20, other arithmetic: 12.3 us -> 13.1 us  [the longest x4 9.6 us: step(): jnp.stack([lo_a[my_unit], hi_a[my_unit], jnp.zeros_like(hi_b[my_unit]), h...]
  transfers between devices with their start and end apart: 5 -> 5, of which waited for: 4 -> 5; matrix products, arithmetic and copies ran while one was open for 16% -> 10% of each run, Pallas kernels for 0% -> 0%
where the time goes in v7:
time: 426 us; the launch traced here: 424 us
  Pallas kernels  154 us (36%)
  waiting for transfers between devices  73.3 us (17%)
  local copies, waits for them, and re-layouts  68.1 us (16%)
  other arithmetic  63 us (15%)
  loops' own time  24.1 us (6%)
  starting transfers between devices  23.9 us (6%)
  between operations  14.1 us (3%)
    pallas_call x4, Pallas kernels, kernel_forces(): pl.pallas_call(_force_kernel, out_shape=jax.ShapeDtypeStruct((2, 6, targe...  154 us
    all_gather x1, waiting for transfers between devices, shards(): full = lax.all_gather(local, plane, axis=1, tiled=True)  51.3 us
    another operation x1, loops' own time, shards(): lax.fori_loop(0, STEPS, step, (phase, deriv, last_blk))  24.1 us
    all_to_all x4, starting transfers between devices, step(): lax.all_to_all(sent, every, 0, 0, tiled=True).reshape(2 * devices, 6, BLK)  23.9 us
    all_to_all x4, waiting for transfers between devices, step(): lax.all_to_all(sent, every, 0, 0, tiled=True).reshape(2 * devices, 6, BLK)  22 us
    gather x8, local copies, waits for them, and re-layouts, step(): owner_a = jnp.where(hi_a > lo_a, compact[job_a], -1)  12.4 us
    gather x8, local copies, waits for them, and re-layouts, step(): owner_b = jnp.where(hi_b > 0, compact[job_b], -1)  9.94 us
    mul x4, other arithmetic, star_terms(): accel = -inv_cube[None, :] * position  9.88 us
  transfers between devices with their start and end apart: 5, of which 5 were waited for; matrix products, arithmetic and copies ran while one was open for 10% of the time, Pallas kernels for 0%

profile of v7, /device:TPU:1, one launch (start us, length us, event | category | flops | bytes accessed | tf_op | source)
XLA Modules:
  0.0 424.3 jit_solution(3622305737336988763)
XLA Ops:
  8.8 51.3 %all-gather.2.cloned.1.call-done = f32[13,65536]{1,0:T(8,128)} async-done(((f32[13,2048]{1,0:T(8,128)}), f32[13,65536]{1,0:T(8,128)}) %all-gather.2.cloned.1.call-update) | async-done | bytes 3407888 | tf_op jit(solution)/shard_map/all_gather | solution.py:152
  60.1 3.2 slice_bitcast_fusion
  63.9 2.5 slice.144
  66.4 349.7 %while.25 = (s32[]{:T(128)}, f32[6,512,128]{2,1,0:T(8,128)S(1)}, f32[6,512,128]{2,1,0:T(8,128)S(1)}, f32[512]{0:T(512)S(1)}, s32[4,4,32]{2,1,0:T(4,128)}, /*inde...) while((s32[]{:T(128)}, f32[6,512,128]{2,1,0:T(8,128)S(1)}, ...), condition=%wide.region_8.9_spmd.clone.clone.clone, body=%wide.region_0.8_spmd.sunk.clone.clone.clone.sunk | while | flops 1217366400 | bytes 55702864 | solution.py:225
  84.3 2.4 pad_add_fusion.4.ctl_ref
  86.7 25.8 %eval_jaxpr.12 = f32[2,6,128,128]{3,2,1,0:T(8,128)} custom-call(s32[4]{0:T(128)} %pad_add_fusion.4.ctl_ref, f32[2,6,128]{2,1,0:T(8,128)} %pad_maximum_fusion.5.tgt_ref, f32[6,512,128]{2,1,0:T(8,128)} %pad_maximum_fusion.6.src_ref, f32[512,128]{1,0:T(8,128)} %get-tuple-element.650.mass_ref), custom_call_target="tpu_custom_call" | custom-call | tf_op jit(solution)/shard_map/while/body/eval_jaxpr/pallas_call | solution.py:134
  115.1 7.6 %all-to-all-start = ((f32[128,2,6,128]{3,1,2,0:T(2,128)}), f32[128,2,6,128]{3,1,2,0:T(2,128)}, u32[]{:S(2)}, u32[]{:S(2)}) async-start(f32[128,2,6,128]{3,1,2,0:T(2,128)} %broadcast_in_dim.121), calls=%async_computation | async-start | bytes 1572864 | tf_op jit(solution)/shard_map/while/body/eval_jaxpr/all_to_all | solution.py:210
  130.9 2.5 broadcast_multiply_fusion.5
  133.4 5.4 %all-to-all-done = f32[128,2,6,128]{3,1,2,0:T(2,128)} async-done(((f32[128,2,6,128]{3,1,2,0:T(2,128)}), f32[128,2,6,128]{3,1,2,0:T(2,128)}, u32[]{:S(2)}, u32[]{:S(2)}) %all-to-all-start) | async-done | bytes 786464 | tf_op jit(solution)/shard_map/while/body/eval_jaxpr/all_to_all | solution.py:210
  160.6 2.4 pad_add_fusion.4.ctl_ref
  163.0 44.6 %eval_jaxpr.12 = f32[2,6,128,128]{3,2,1,0:T(8,128)} custom-call(s32[4]{0:T(128)} %pad_add_fusion.4.ctl_ref, f32[2,6,128]{2,1,0:T(8,128)} %pad_maximum_fusion.5.tgt_ref, f32[6,512,128]{2,1,0:T(8,128)} %pad_maximum_fusion.6.src_ref, f32[512,128]{1,0:T(8,128)} %get-tuple-element.650.mass_ref), custom_call_target="tpu_custom_call" | custom-call | tf_op jit(solution)/shard_map/while/body/eval_jaxpr/pallas_call | solution.py:134
  210.2 5.6 %all-to-all-start = ((f32[128,2,6,128]{3,1,2,0:T(2,128)}), f32[128,2,6,128]{3,1,2,0:T(2,128)}, u32[]{:S(2)}, u32[]{:S(2)}) async-start(f32[128,2,6,128]{3,1,2,0:T(2,128)} %broadcast_in_dim.121), calls=%async_computation | async-start | bytes 1572864 | tf_op jit(solution)/shard_map/while/body/eval_jaxpr/all_to_all | solution.py:210
  224.0 2.5 broadcast_multiply_fusion.5
  226.5 5.5 %all-to-all-done = f32[128,2,6,128]{3,1,2,0:T(2,128)} async-done(((f32[128,2,6,128]{3,1,2,0:T(2,128)}), f32[128,2,6,128]{3,1,2,0:T(2,128)}, u32[]{:S(2)}, u32[]{:S(2)}) %all-to-all-start) | async-done | bytes 786464 | tf_op jit(solution)/shard_map/while/body/eval_jaxpr/all_to_all | solution.py:210
  253.9 2.4 pad_add_fusion.4.ctl_ref
  256.3 25.8 %eval_jaxpr.12 = f32[2,6,128,128]{3,2,1,0:T(8,128)} custom-call(s32[4]{0:T(128)} %pad_add_fusion.4.ctl_ref, f32[2,6,128]{2,1,0:T(8,128)} %pad_maximum_fusion.5.tgt_ref, f32[6,512,128]{2,1,0:T(8,128)} %pad_maximum_fusion.6.src_ref, f32[512,128]{1,0:T(8,128)} %get-tuple-element.650.mass_ref), custom_call_target="tpu_custom_call" | custom-call | tf_op jit(solution)/shard_map/while/body/eval_jaxpr/pallas_call | solution.py:134
  284.6 5.4 %all-to-all-start = ((f32[128,2,6,128]{3,1,2,0:T(2,128)}), f32[128,2,6,128]{3,1,2,0:T(2,128)}, u32[]{:S(2)}, u32[]{:S(2)}) async-start(f32[128,2,6,128]{3,1,2,0:T(2,128)} %broadcast_in_dim.121), calls=%async_computation | async-start | bytes 1572864 | tf_op jit(solution)/shard_map/while/body/eval_jaxpr/all_to_all | solution.py:210
  298.3 2.5 broadcast_multiply_fusion.5
  300.7 5.5 %all-to-all-done = f32[128,2,6,128]{3,1,2,0:T(2,128)} async-done(((f32[128,2,6,128]{3,1,2,0:T(2,128)}), f32[128,2,6,128]{3,1,2,0:T(2,128)}, u32[]{:S(2)}, u32[]{:S(2)}) %all-to-all-start) | async-done | bytes 786464 | tf_op jit(solution)/shard_map/while/body/eval_jaxpr/all_to_all | solution.py:210
  328.1 2.4 pad_add_fusion.4.ctl_ref
  330.5 57.5 %eval_jaxpr.12 = f32[2,6,128,128]{3,2,1,0:T(8,128)} custom-call(s32[4]{0:T(128)} %pad_add_fusion.4.ctl_ref, f32[2,6,128]{2,1,0:T(8,128)} %pad_maximum_fusion.5.tgt_ref, f32[6,512,128]{2,1,0:T(8,128)} %pad_maximum_fusion.6.src_ref, f32[512,128]{1,0:T(8,128)} %get-tuple-element.650.mass_ref), custom_call_target="tpu_custom_call" | custom-call | tf_op jit(solution)/shard_map/while/body/eval_jaxpr/pallas_call | solution.py:134
  390.5 5.4 %all-to-all-start = ((f32[128,2,6,128]{3,1,2,0:T(2,128)}), f32[128,2,6,128]{3,1,2,0:T(2,128)}, u32[]{:S(2)}, u32[]{:S(2)}) async-start(f32[128,2,6,128]{3,1,2,0:T(2,128)} %broadcast_in_dim.121), calls=%async_computation | async-start | bytes 1572864 | tf_op jit(solution)/shard_map/while/body/eval_jaxpr/all_to_all | solution.py:210
  404.2 2.5 broadcast_multiply_fusion.5
  406.6 5.5 %all-to-all-done = f32[128,2,6,128]{3,1,2,0:T(2,128)} async-done(((f32[128,2,6,128]{3,1,2,0:T(2,128)}), f32[128,2,6,128]{3,1,2,0:T(2,128)}, u32[]{:S(2)}, u32[]{:S(2)}) %all-to-all-start) | async-done | bytes 786464 | tf_op jit(solution)/shard_map/while/body/eval_jaxpr/all_to_all | solution.py:210
  (259 shorter events, 110.0 us)
Async XLA Ops:
  7.2 52.9 %all-gather.2.cloned.1.call-start = ((), (), s32[]{:S(2)}) async-start(), calls=%async_computation.1 | async-start | bytes 4325376 | tf_op jit(solution)/shard_map/all_gather | solution.py:152
  63.3 3.1 copy-start.7
  82.0 1.4 copy-start
  82.0 1.6 copy-start.2
  115.1 23.7 %all-to-all-start = ((f32[128,2,6,128]{3,1,2,0:T(2,128)}), f32[128,2,6,128]{3,1,2,0:T(2,128)}, u32[]{:S(2)}, u32[]{:S(2)}) async-start(f32[128,2,6,128]{3,1,2,0:T(2,128)} %broadcast_in_dim.121), calls=%async_computation | async-start | bytes 1572864 | tf_op jit(solution)/shard_map/while/body/eval_jaxpr/all_to_all | solution.py:210
  129.7 1.2 copy-start.1
  138.8 1.5 copy-start.3
  138.8 1.6 copy-start.4
  158.3 1.4 copy-start
  158.3 1.6 copy-start.2
  210.2 21.8 %all-to-all-start = ((f32[128,2,6,128]{3,1,2,0:T(2,128)}), f32[128,2,6,128]{3,1,2,0:T(2,128)}, u32[]{:S(2)}, u32[]{:S(2)}) async-start(f32[128,2,6,128]{3,1,2,0:T(2,128)} %broadcast_in_dim.121), calls=%async_computation | async-start | bytes 1572864 | tf_op jit(solution)/shard_map/while/body/eval_jaxpr/all_to_all | solution.py:210
  232.0 1.5 copy-start.3
  232.0 1.6 copy-start.4
  251.6 1.4 copy-start
  251.6 1.6 copy-start.2
  284.6 21.6 %all-to-all-start = ((f32[128,2,6,128]{3,1,2,0:T(2,128)}), f32[128,2,6,128]{3,1,2,0:T(2,128)}, u32[]{:S(2)}, u32[]{:S(2)}) async-start(f32[128,2,6,128]{3,1,2,0:T(2,128)} %broadcast_in_dim.121), calls=%async_computation | async-start | bytes 1572864 | tf_op jit(solution)/shard_map/while/body/eval_jaxpr/all_to_all | solution.py:210
  297.0 1.2 copy-start.1
  306.3 1.5 copy-start.3
  306.3 1.6 copy-start.4
  325.8 1.4 copy-start
  325.8 1.6 copy-start.2
  390.5 21.6 %all-to-all-start = ((f32[128,2,6,128]{3,1,2,0:T(2,128)}), f32[128,2,6,128]{3,1,2,0:T(2,128)}, u32[]{:S(2)}, u32[]{:S(2)}) async-start(f32[128,2,6,128]{3,1,2,0:T(2,128)} %broadcast_in_dim.121), calls=%async_computation | async-start | bytes 1572864 | tf_op jit(solution)/shard_map/while/body/eval_jaxpr/all_to_all | solution.py:210
  412.2 1.5 copy-start.3
  412.2 1.6 copy-start.4
  (14 other events, 11.2 us)
Sparse Core Ops, SparseCore 0:
  10.3 49.7 all-gather.1

commit v8 on v6

--- a/solution.py
+++ b/solution.py
@@ -162,44 +162,54 @@
     all_blocks = jnp.arange(block_total, dtype=jnp.int32)
     units = jnp.arange(devices, dtype=jnp.int32)
     last_blk = jnp.zeros((block_total,), jnp.float32)
-    plans = []
-    for step_index in range(STEPS):
-        flat = active_lists[step_index].reshape(-1)
-        live = flat >= 0
-        live_count = jnp.sum(live.astype(jnp.int32))
-        rank = jnp.cumsum(live.astype(jnp.int32)) - 1
-        compact = (
-            jnp.zeros((slots,), jnp.int32)
-            .at[jnp.where(live, rank, slots)]
-            .set(flat, mode="drop")
-        )
-        work = live_count * tiles
-        share = (work + devices - 1) // devices
-        begin = jnp.minimum(units * share, work)
-        finish = jnp.minimum(begin + share, work)
-        job_a = jnp.minimum(begin // tiles, slots - 1)
-        lo_a = begin - job_a * tiles
-        hi_a = jnp.maximum(jnp.minimum(finish - job_a * tiles, tiles), lo_a)
-        job_b = jnp.minimum(job_a + 1, slots - 1)
-        hi_b = jnp.clip(finish - (job_a + 1) * tiles, 0, tiles)
-        owner_a = jnp.where(hi_a > lo_a, compact[job_a], -1)
-        owner_b = jnp.where(hi_b > 0, compact[job_b], -1)
-        owner_all = jnp.stack([owner_a, owner_b], axis=1).reshape(-1)
-        ranges = jnp.stack(
-            [lo_a[my_unit], hi_a[my_unit], jnp.zeros_like(hi_b[my_unit]), hi_b[my_unit]]
-        ).astype(jnp.int32)
-        id_a = jnp.clip(compact[job_a[my_unit]], 0, block_total - 1)
-        id_b = jnp.clip(compact[job_b[my_unit]], 0, block_total - 1)
-        onehot = (all_blocks[:, None] == owner_all[None, :]).astype(jnp.float32)
-        active_flags = jnp.any(flat[:, None] == all_blocks[None, :], axis=0)
-        plans.append((ranges, id_a, id_b, onehot, active_flags))
+    flat = active_lists.reshape(active_lists.shape[0], -1)
+    live = flat >= 0
+    live_count = jnp.sum(live.astype(jnp.int32), axis=1, keepdims=True)
+    rank = jnp.cumsum(live.astype(jnp.int32), axis=1) - 1
+    picks = (rank[:, :, None] == units[None, None, :slots]) & live[:, :, None]
+    compact = jnp.sum(jnp.where(picks, flat[:, :, None], 0), axis=1)
+    work = live_count * tiles
+    share = (work + devices - 1) // devices
+    begin = jnp.minimum(units[None, :] * share, work)
+    finish = jnp.minimum(begin + share, work)
+    job_a = jnp.minimum(begin // tiles, slots - 1)
+    lo_a = begin - job_a * tiles
+    hi_a = jnp.maximum(jnp.minimum(finish - job_a * tiles, tiles), lo_a)
+    job_b = jnp.minimum(job_a + 1, slots - 1)
+    hi_b = jnp.clip(finish - (job_a + 1) * tiles, 0, tiles)
+    owner_a = jnp.where(hi_a > lo_a, jnp.take_along_axis(compact, job_a, axis=1), -1)
+    owner_b = jnp.where(hi_b > 0, jnp.take_along_axis(compact, job_b, axis=1), -1)
+    owner_all = jnp.stack([owner_a, owner_b], axis=2).reshape(flat.shape[0], -1)
+    onehots = (all_blocks[None, :, None] == owner_all[:, None, :]).astype(jnp.float32)
+    active_all = jnp.any(flat[:, :, None] == all_blocks[None, None, :], axis=1)
+    mine = lambda x: lax.dynamic_index_in_dim(x, my_unit, 1, keepdims=False)
+    ranges_all = jnp.stack(
+        [mine(lo_a), mine(hi_a), jnp.zeros_like(mine(hi_b)), mine(hi_b)], axis=1
+    ).astype(jnp.int32)
+    ids_all = jnp.clip(
+        jnp.stack(
+            [
+                jnp.take_along_axis(compact, mine(job_a)[:, None], axis=1)[:, 0],
+                jnp.take_along_axis(compact, mine(job_b)[:, None], axis=1)[:, 0],
+            ],
+            axis=1,
+        ),
+        0,
+        block_total - 1,
+    )
+    plans = (ranges_all, ids_all, onehots, active_all)
     plans, full = lax.optimization_barrier((plans, full))
+    ranges_all, ids_all, onehots, active_all = plans
     mass = full[12]
     phase = full[0:6]
     deriv = full[6:12]
     for step_index in range(STEPS):
         now_time = (step_index + 1) * time_step
-        ranges, id_a, id_b, onehot, active_flags = plans[step_index]
+        ranges = ranges_all[step_index]
+        id_a = ids_all[step_index, 0]
+        id_b = ids_all[step_index, 1]
+        onehot = onehots[step_index]
+        active_flags = active_all[step_index]
         elapsed_blk = now_time - last_blk
         elapsed = elapsed_blk[None, :, None]
         predicted = predict(phase, deriv, elapsed)

time: 384 us -> 360 us (0.938)
  waiting for transfers between devices: 55.6 us -> 81.1 us
  local copies, waits for them, and re-layouts: 50.1 us -> 30 us
  other arithmetic: 51.2 us -> 37.7 us
  between operations: 37.2 us -> 29.8 us
  Pallas kernels: 154 us -> 147 us
  starting transfers between devices: 26.3 us -> 22.1 us
    all_gather x1, waiting for transfers between devices: 0.01 us -> 34.6 us  [shards(): full = lax.all_gather(local, plane, axis=1, tiled=True)]
    dynamic_slice x24 -> x2, local copies, waits for them, and re-layouts: 14.7 us -> 0.14 us  [shards(): mine = lambda x: lax.dynamic_index_in_dim(x, my_unit, 1, keepdims=False)]
    another operation x10 -> x4, other arithmetic: 9.89 us -> 0.49 us  [the longest x1 0.31 us: shards(): rank = jnp.cumsum(live.astype(jnp.int32), axis=1) - 1]
    all_to_all x4, waiting for transfers between devices: 55.5 us -> 46.4 us  [shards(): lax.all_to_all(sent, every, 0, 0, tiled=True).reshape(2 * devices, 6, BLK)]
    pallas_call x4, Pallas kernels: 154 us -> 147 us  [kernel_forces(): pl.pallas_call(_force_kernel, out_shape=jax.ShapeDtypeStruct((2, 6, targe...]
    all_to_all x4, starting transfers between devices: 26.2 us -> 22.1 us  [shards(): lax.all_to_all(sent, every, 0, 0, tiled=True).reshape(2 * devices, 6, BLK)]
    scatter x4 -> x0, local copies, waits for them, and re-layouts: 3.93 us -> none  [shards(): compact = jnp.zeros((slots,), jnp.int32).at[jnp.where(live, rank, slots)]...]
    unnamed x43 -> x47, local copies, waits for them, and re-layouts: 9.44 us -> 7.71 us
  transfers between devices with their start and end apart: 5 -> 5, of which waited for: 4 -> 5; matrix products, arithmetic and copies ran while one was open for 15% -> 7% of each run, Pallas kernels for 0% -> 0%
where the time goes in v8:
time: 360 us; the launch traced here: 359 us
  Pallas kernels  147 us (41%)
  waiting for transfers between devices  81.1 us (23%)
  other arithmetic  37.7 us (10%)
  local copies, waits for them, and re-layouts  30 us (8%)
  between operations  29.8 us (8%)
  starting transfers between devices  22.1 us (6%)
  matrix products  10.7 us (3%)
    pallas_call x4, Pallas kernels, kernel_forces(): pl.pallas_call(_force_kernel, out_shape=jax.ShapeDtypeStruct((2, 6, targe...  147 us
    all_to_all x4, waiting for transfers between devices, shards(): lax.all_to_all(sent, every, 0, 0, tiled=True).reshape(2 * devices, 6, BLK)  46.4 us
    all_gather x1, waiting for transfers between devices, shards(): full = lax.all_gather(local, plane, axis=1, tiled=True)  34.6 us
    all_to_all x4, starting transfers between devices, shards(): lax.all_to_all(sent, every, 0, 0, tiled=True).reshape(2 * devices, 6, BLK)  22.1 us
    dot_general x4, matrix products, shards(): jnp.einsum('bu,ucl->cbl', onehot, got, precision=lax.Precision.HIGHEST, p...  10.7 us
    unnamed x47, local copies, waits for them, and re-layouts  7.71 us
  transfers between devices with their start and end apart: 5, of which 5 were waited for; matrix products, arithmetic and copies ran while one was open for 7% of the time, Pallas kernels for 0%

profile of v8, /device:TPU:1, one launch (start us, length us, event | category | flops | bytes accessed | tf_op | source)
XLA Modules:
  0.0 358.8 jit_solution(16786220505479020251)
XLA Ops:
  11.2 4.7 %gather_fusion.2 = s32[512]{0:T(512)S(1)} fusion(s32[4,128]{1,0:T(4,128)S(1)} %select_reduce_fusion, s32[512]{0:T(512)S(1)} %get-tuple-element.95), kind=kCustom, calls=%fused_computation.1.clone | custom fusion | bytes 8192 | tf_op jit(solution)/shard_map/jit(take_along_axis)/gather | solution.py:180
  15.8 4.7 %gather_fusion.3 = s32[512]{0:T(512)S(1)} fusion(s32[4,128]{1,0:T(4,128)S(1)} %select_reduce_fusion, s32[512]{0:T(512)S(1)} %get-tuple-element.96), kind=kCustom, calls=%fused_computation.3.clone | custom fusion | bytes 8192 | tf_op jit(solution)/shard_map/jit(take_along_axis)/gather | solution.py:181
  25.5 34.6 %all-gather.2.cloned.1.call-done = f32[13,65536]{1,0:T(8,128)} async-done(((f32[13,2048]{1,0:T(8,128)}), f32[13,65536]{1,0:T(8,128)}) %all-gather.2.cloned.1.call-update) | async-done | bytes 3407888 | tf_op jit(solution)/shard_map/all_gather | solution.py:152
  60.1 3.0 copy.116
  66.4 2.4 multiply_reduce_fusion.7
  73.9 2.7 pad_maximum_fusion.src_ref
  77.2 25.8 %shard_map.59 = f32[2,6,128,128]{3,2,1,0:T(8,128)} custom-call(s32[4]{0:T(128)} %get-tuple-element.81.ctl_ref, f32[2,6,128]{2,1,0:T(8,128)} %pad_maximum_fusion.5.tgt_ref, f32[6,512,128]{2,1,0:T(8,128)} %pad_maximum_fusion.src_ref, f32[512,128]{1,0:T(8,128)} %slice_bitcast_fusion.mass_ref), custom_call_target="tpu_custom_call" | custom-call | tf_op jit(solution)/shard_map/pallas_call | solution.py:134
  105.6 7.6 %all-to-all-start = ((f32[128,2,6,128]{3,1,2,0:T(2,128)}), f32[128,2,6,128]{3,1,2,0:T(2,128)}, u32[]{:S(2)}, u32[]{:S(2)}) async-start(f32[128,2,6,128]{3,1,2,0:T(2,128)} %broadcast_in_dim.132), calls=%async_computation | async-start | bytes 1572864 | tf_op jit(solution)/shard_map/all_to_all | solution.py:224
  115.7 2.5 broadcast_multiply_fusion.3
  118.2 11.1 %all-to-all-done = f32[128,2,6,128]{3,1,2,0:T(2,128)} async-done(((f32[128,2,6,128]{3,1,2,0:T(2,128)}), f32[128,2,6,128]{3,1,2,0:T(2,128)}, u32[]{:S(2)}, u32[]{:S(2)}) %all-to-all-start) | async-done | bytes 786464 | tf_op jit(solution)/shard_map/all_to_all | solution.py:224
  130.9 2.6 maximum_add_fusion
  138.0 38.3 %shard_map.60 = f32[2,6,128,128]{3,2,1,0:T(8,128)} custom-call(s32[4]{0:T(128)} %get-tuple-element.80.ctl_ref, f32[2,6,128]{2,1,0:T(8,128)} %pad_maximum_fusion.6.tgt_ref, f32[6,512,128]{2,1,0:T(8,128)} %pad_maximum_fusion.1.src_ref, f32[512,128]{1,0:T(8,128)} %slice_bitcast_fusion.mass_ref), custom_call_target="tpu_custom_call" | custom-call | tf_op jit(solution)/shard_map/pallas_call | solution.py:134
  178.8 4.6 %all-to-all-start.1 = ((f32[128,2,6,128]{3,1,2,0:T(2,128)}), f32[128,2,6,128]{3,1,2,0:T(2,128)S(1)}, u32[]{:S(2)}, u32[]{:S(2)}) async-start(f32[128,2,6,128]{3,1,2,0:T(2,128)} %broadcast_in_dim.135), calls=%async_computation.1 | async-start | bytes 1572864 | tf_op jit(solution)/shard_map/all_to_all | solution.py:224
  188.6 11.3 %all-to-all-done.1 = f32[128,2,6,128]{3,1,2,0:T(2,128)S(1)} async-done(((f32[128,2,6,128]{3,1,2,0:T(2,128)}), f32[128,2,6,128]{3,1,2,0:T(2,128)S(1)}, u32[]{:S(2)}, u32[]{:S(2)}) %all-to-all-start.1) | async-done | bytes 786464 | tf_op jit(solution)/shard_map/all_to_all | solution.py:224
  200.2 2.7 maximum_add_fusion.1
  207.3 25.8 %shard_map.61 = f32[2,6,128,128]{3,2,1,0:T(8,128)} custom-call(s32[4]{0:T(128)} %get-tuple-element.79.ctl_ref, f32[2,6,128]{2,1,0:T(8,128)} %pad_maximum_fusion.7.tgt_ref, f32[6,512,128]{2,1,0:T(8,128)} %pad_maximum_fusion.2.src_ref, f32[512,128]{1,0:T(8,128)} %slice_bitcast_fusion.mass_ref), custom_call_target="tpu_custom_call" | custom-call | tf_op jit(solution)/shard_map/pallas_call | solution.py:134
  235.6 5.4 %all-to-all-start.2 = ((f32[128,2,6,128]{3,1,2,0:T(2,128)}), f32[128,2,6,128]{3,1,2,0:T(2,128)}, u32[]{:S(2)}, u32[]{:S(2)}) async-start(f32[128,2,6,128]{3,1,2,0:T(2,128)} %broadcast_in_dim.136), calls=%async_computation.2 | async-start | bytes 1572864 | tf_op jit(solution)/shard_map/all_to_all | solution.py:224
  246.0 2.5 broadcast_multiply_fusion.1
  248.5 8.8 %all-to-all-done.2 = f32[128,2,6,128]{3,1,2,0:T(2,128)} async-done(((f32[128,2,6,128]{3,1,2,0:T(2,128)}), f32[128,2,6,128]{3,1,2,0:T(2,128)}, u32[]{:S(2)}, u32[]{:S(2)}) %all-to-all-start.2) | async-done | bytes 786464 | tf_op jit(solution)/shard_map/all_to_all | solution.py:224
  258.9 2.6 maximum_add_fusion.2
  266.0 57.5 %shard_map.62 = f32[2,6,128,128]{3,2,1,0:T(8,128)} custom-call(s32[4]{0:T(128)} %get-tuple-element.78.ctl_ref, f32[2,6,128]{2,1,0:T(8,128)} %pad_maximum_fusion.8.tgt_ref, f32[6,512,128]{2,1,0:T(8,128)} %pad_maximum_fusion.3.src_ref, f32[512,128]{1,0:T(8,128)} %slice_bitcast_fusion.mass_ref), custom_call_target="tpu_custom_call" | custom-call | tf_op jit(solution)/shard_map/pallas_call | solution.py:134
  326.1 4.5 %all-to-all-start.3 = ((f32[128,2,6,128]{3,1,2,0:T(2,128)}), f32[128,2,6,128]{3,1,2,0:T(2,128)S(1)}, u32[]{:S(2)}, u32[]{:S(2)}) async-start(f32[128,2,6,128]{3,1,2,0:T(2,128)} %broadcast_in_dim.137), calls=%async_computation.3 | async-start | bytes 1572864 | tf_op jit(solution)/shard_map/all_to_all | solution.py:224
  331.8 15.2 %all-to-all-done.3 = f32[128,2,6,128]{3,1,2,0:T(2,128)S(1)} async-done(((f32[128,2,6,128]{3,1,2,0:T(2,128)}), f32[128,2,6,128]{3,1,2,0:T(2,128)S(1)}, u32[]{:S(2)}, u32[]{:S(2)}) %all-to-all-start.3) | async-done | bytes 786464 | tf_op jit(solution)/shard_map/all_to_all | solution.py:224
  347.3 2.7 maximum_add_fusion.3
  (140 shorter events, 45.3 us)
Async XLA Ops:
  7.2 53.0 %all-gather.2.cloned.1.call-start = ((), (), s32[]{:S(2)}) async-start(), calls=%async_computation.4 | async-start | bytes 4325376 | tf_op jit(solution)/shard_map/all_gather | solution.py:152
  73.8 2.8 copy-start.8
  73.8 2.8 copy-start.10
  105.6 23.7 %all-to-all-start = ((f32[128,2,6,128]{3,1,2,0:T(2,128)}), f32[128,2,6,128]{3,1,2,0:T(2,128)}, u32[]{:S(2)}, u32[]{:S(2)}) async-start(f32[128,2,6,128]{3,1,2,0:T(2,128)} %broadcast_in_dim.132), calls=%async_computation | async-start | bytes 1572864 | tf_op jit(solution)/shard_map/all_to_all | solution.py:224
  114.5 1.3 copy-start.9
  129.3 1.5 copy-start.15
  129.3 1.6 copy-start.16
  134.4 1.2 copy-start
  134.4 1.7 copy-start.2
  178.8 21.2 %all-to-all-start.1 = ((f32[128,2,6,128]{3,1,2,0:T(2,128)}), f32[128,2,6,128]{3,1,2,0:T(2,128)S(1)}, u32[]{:S(2)}, u32[]{:S(2)}) async-start(f32[128,2,6,128]{3,1,2,0:T(2,128)} %broadcast_in_dim.135), calls=%async_computation.1 | async-start | bytes 1572864 | tf_op jit(solution)/shard_map/all_to_all | solution.py:224
  188.6 11.6 %copy-start.17 = (f32[3,512,128]{2,1,0:T(8,128)S(1)}, f32[3,512,128]{2,1,0:T(8,128)}, u32[]{:S(2)}) copy-start(f32[3,512,128]{2,1,0:T(8,128)} %get-tuple-element.59) | copy-start | bytes 2359300
  200.2 2.8 copy-start.1
  200.2 2.8 copy-start.3
  205.0 1.4 copy-start.11
  205.0 1.7 copy-start.13
  235.6 21.6 %all-to-all-start.2 = ((f32[128,2,6,128]{3,1,2,0:T(2,128)}), f32[128,2,6,128]{3,1,2,0:T(2,128)}, u32[]{:S(2)}, u32[]{:S(2)}) async-start(f32[128,2,6,128]{3,1,2,0:T(2,128)} %broadcast_in_dim.136), calls=%async_computation.2 | async-start | bytes 1572864 | tf_op jit(solution)/shard_map/all_to_all | solution.py:224
  244.8 1.2 copy-start.12
  257.3 1.5 copy-start.18
  257.3 1.6 copy-start.19
  262.5 1.7 copy-start.6
  326.1 21.0 %all-to-all-start.3 = ((f32[128,2,6,128]{3,1,2,0:T(2,128)}), f32[128,2,6,128]{3,1,2,0:T(2,128)S(1)}, u32[]{:S(2)}, u32[]{:S(2)}) async-start(f32[128,2,6,128]{3,1,2,0:T(2,128)} %broadcast_in_dim.137), calls=%async_computation.3 | async-start | bytes 1572864 | tf_op jit(solution)/shard_map/all_to_all | solution.py:224
  331.8 15.5 %copy-start.14 = (f32[3,512,128]{2,1,0:T(8,128)S(1)}, f32[3,512,128]{2,1,0:T(8,128)}, u32[]{:S(2)}) copy-start(f32[3,512,128]{2,1,0:T(8,128)} %get-tuple-element.55) | copy-start | bytes 2359300
  347.3 2.8 copy-start.5
  347.3 2.8 copy-start.7
  (1 other events, 1.2 us)
Sparse Core Ops, SparseCore 0:
  10.3 49.8 all-gather.1

commit v9 on v8

--- a/solution.py
+++ b/solution.py
@@ -10,7 +10,7 @@
 from jax.experimental.pallas import tpu as pltpu
 
 BLK = 128
-GROUP = 8
+GROUP = 4
 STEPS = 4
 
 

time: 360 us -> 390 us (1.083)
  Pallas kernels: 147 us -> 178 us
    pallas_call x4, Pallas kernels: 147 us -> 178 us  [kernel_forces(): pl.pallas_call(_force_kernel, out_shape=jax.ShapeDtypeStruct((2, 6, targe...]
where the time goes in v9:
time: 390 us; the launch traced here: 389 us
  Pallas kernels  178 us (46%)
  waiting for transfers between devices  81 us (21%)
  other arithmetic  37.7 us (10%)
  local copies, waits for them, and re-layouts  30 us (8%)
  between operations  29.8 us (8%)
  starting transfers between devices  22.3 us (6%)
  matrix products  10.7 us (3%)
    pallas_call x4, Pallas kernels, kernel_forces(): pl.pallas_call(_force_kernel, out_shape=jax.ShapeDtypeStruct((2, 6, targe...  178 us
    all_to_all x4, waiting for transfers between devices, shards(): lax.all_to_all(sent, every, 0, 0, tiled=True).reshape(2 * devices, 6, BLK)  46.3 us
    all_gather x1, waiting for transfers between devices, shards(): full = lax.all_gather(local, plane, axis=1, tiled=True)  34.6 us
    all_to_all x4, starting transfers between devices, shards(): lax.all_to_all(sent, every, 0, 0, tiled=True).reshape(2 * devices, 6, BLK)  22.2 us
    dot_general x4, matrix products, shards(): jnp.einsum('bu,ucl->cbl', onehot, got, precision=lax.Precision.HIGHEST, p...  10.7 us
  transfers between devices with their start and end apart: 5, of which 5 were waited for; matrix products, arithmetic and copies ran while one was open for 7% of the time, Pallas kernels for 0%

profile of v9, /device:TPU:1, one launch (start us, length us, event | category | flops | bytes accessed | tf_op | source)
XLA Modules:
  0.0 389.1 jit_solution(2235965874897165697)
XLA Ops:
  11.2 4.7 %gather_fusion.2 = s32[512]{0:T(512)S(1)} fusion(s32[4,128]{1,0:T(4,128)S(1)} %select_reduce_fusion, s32[512]{0:T(512)S(1)} %get-tuple-element.95), kind=kCustom, calls=%fused_computation.1.clone | custom fusion | bytes 8192 | tf_op jit(solution)/shard_map/jit(take_along_axis)/gather | solution.py:180
  15.8 4.7 %gather_fusion.3 = s32[512]{0:T(512)S(1)} fusion(s32[4,128]{1,0:T(4,128)S(1)} %select_reduce_fusion, s32[512]{0:T(512)S(1)} %get-tuple-element.96), kind=kCustom, calls=%fused_computation.3.clone | custom fusion | bytes 8192 | tf_op jit(solution)/shard_map/jit(take_along_axis)/gather | solution.py:181
  25.5 34.6 %all-gather.2.cloned.1.call-done = f32[13,65536]{1,0:T(8,128)} async-done(((f32[13,2048]{1,0:T(8,128)}), f32[13,65536]{1,0:T(8,128)}) %all-gather.2.cloned.1.call-update) | async-done | bytes 3407888 | tf_op jit(solution)/shard_map/all_gather | solution.py:152
  60.1 3.0 copy.116
  66.4 2.4 multiply_reduce_fusion.7
  73.9 2.7 pad_maximum_fusion.src_ref
  77.2 29.4 %shard_map.59 = f32[2,6,128,128]{3,2,1,0:T(8,128)} custom-call(s32[4]{0:T(128)} %get-tuple-element.81.ctl_ref, f32[2,6,128]{2,1,0:T(8,128)} %pad_maximum_fusion.5.tgt_ref, f32[6,512,128]{2,1,0:T(8,128)} %pad_maximum_fusion.src_ref, f32[512,128]{1,0:T(8,128)} %slice_bitcast_fusion.mass_ref), custom_call_target="tpu_custom_call" | custom-call | tf_op jit(solution)/shard_map/pallas_call | solution.py:134
  109.1 7.6 %all-to-all-start = ((f32[128,2,6,128]{3,1,2,0:T(2,128)}), f32[128,2,6,128]{3,1,2,0:T(2,128)}, u32[]{:S(2)}, u32[]{:S(2)}) async-start(f32[128,2,6,128]{3,1,2,0:T(2,128)} %broadcast_in_dim.132), calls=%async_computation | async-start | bytes 1572864 | tf_op jit(solution)/shard_map/all_to_all | solution.py:224
  119.3 2.5 broadcast_multiply_fusion.3
  121.8 11.1 %all-to-all-done = f32[128,2,6,128]{3,1,2,0:T(2,128)} async-done(((f32[128,2,6,128]{3,1,2,0:T(2,128)}), f32[128,2,6,128]{3,1,2,0:T(2,128)}, u32[]{:S(2)}, u32[]{:S(2)}) %all-to-all-start) | async-done | bytes 786464 | tf_op jit(solution)/shard_map/all_to_all | solution.py:224
  134.5 2.6 maximum_add_fusion
  141.5 51.8 %shard_map.60 = f32[2,6,128,128]{3,2,1,0:T(8,128)} custom-call(s32[4]{0:T(128)} %get-tuple-element.80.ctl_ref, f32[2,6,128]{2,1,0:T(8,128)} %pad_maximum_fusion.6.tgt_ref, f32[6,512,128]{2,1,0:T(8,128)} %pad_maximum_fusion.1.src_ref, f32[512,128]{1,0:T(8,128)} %slice_bitcast_fusion.mass_ref), custom_call_target="tpu_custom_call" | custom-call | tf_op jit(solution)/shard_map/pallas_call | solution.py:134
  195.8 4.8 %all-to-all-start.1 = ((f32[128,2,6,128]{3,1,2,0:T(2,128)}), f32[128,2,6,128]{3,1,2,0:T(2,128)S(1)}, u32[]{:S(2)}, u32[]{:S(2)}) async-start(f32[128,2,6,128]{3,1,2,0:T(2,128)} %broadcast_in_dim.135), calls=%async_computation.1 | async-start | bytes 1572864 | tf_op jit(solution)/shard_map/all_to_all | solution.py:224
  205.8 11.2 %all-to-all-done.1 = f32[128,2,6,128]{3,1,2,0:T(2,128)S(1)} async-done(((f32[128,2,6,128]{3,1,2,0:T(2,128)}), f32[128,2,6,128]{3,1,2,0:T(2,128)S(1)}, u32[]{:S(2)}, u32[]{:S(2)}) %all-to-all-start.1) | async-done | bytes 786464 | tf_op jit(solution)/shard_map/all_to_all | solution.py:224
  217.3 2.7 maximum_add_fusion.1
  224.4 29.4 %shard_map.61 = f32[2,6,128,128]{3,2,1,0:T(8,128)} custom-call(s32[4]{0:T(128)} %get-tuple-element.79.ctl_ref, f32[2,6,128]{2,1,0:T(8,128)} %pad_maximum_fusion.7.tgt_ref, f32[6,512,128]{2,1,0:T(8,128)} %pad_maximum_fusion.2.src_ref, f32[512,128]{1,0:T(8,128)} %slice_bitcast_fusion.mass_ref), custom_call_target="tpu_custom_call" | custom-call | tf_op jit(solution)/shard_map/pallas_call | solution.py:134
  256.3 5.4 %all-to-all-start.2 = ((f32[128,2,6,128]{3,1,2,0:T(2,128)}), f32[128,2,6,128]{3,1,2,0:T(2,128)}, u32[]{:S(2)}, u32[]{:S(2)}) async-start(f32[128,2,6,128]{3,1,2,0:T(2,128)} %broadcast_in_dim.136), calls=%async_computation.2 | async-start | bytes 1572864 | tf_op jit(solution)/shard_map/all_to_all | solution.py:224
  266.7 2.5 broadcast_multiply_fusion.1
  269.2 8.8 %all-to-all-done.2 = f32[128,2,6,128]{3,1,2,0:T(2,128)} async-done(((f32[128,2,6,128]{3,1,2,0:T(2,128)}), f32[128,2,6,128]{3,1,2,0:T(2,128)}, u32[]{:S(2)}, u32[]{:S(2)}) %all-to-all-start.2) | async-done | bytes 786464 | tf_op jit(solution)/shard_map/all_to_all | solution.py:224
  279.6 2.6 maximum_add_fusion.2
  286.7 67.1 %shard_map.62 = f32[2,6,128,128]{3,2,1,0:T(8,128)} custom-call(s32[4]{0:T(128)} %get-tuple-element.78.ctl_ref, f32[2,6,128]{2,1,0:T(8,128)} %pad_maximum_fusion.8.tgt_ref, f32[6,512,128]{2,1,0:T(8,128)} %pad_maximum_fusion.3.src_ref, f32[512,128]{1,0:T(8,128)} %slice_bitcast_fusion.mass_ref), custom_call_target="tpu_custom_call" | custom-call | tf_op jit(solution)/shard_map/pallas_call | solution.py:134
  356.4 4.5 %all-to-all-start.3 = ((f32[128,2,6,128]{3,1,2,0:T(2,128)}), f32[128,2,6,128]{3,1,2,0:T(2,128)S(1)}, u32[]{:S(2)}, u32[]{:S(2)}) async-start(f32[128,2,6,128]{3,1,2,0:T(2,128)} %broadcast_in_dim.137), calls=%async_computation.3 | async-start | bytes 1572864 | tf_op jit(solution)/shard_map/all_to_all | solution.py:224
  362.1 15.2 %all-to-all-done.3 = f32[128,2,6,128]{3,1,2,0:T(2,128)S(1)} async-done(((f32[128,2,6,128]{3,1,2,0:T(2,128)}), f32[128,2,6,128]{3,1,2,0:T(2,128)S(1)}, u32[]{:S(2)}, u32[]{:S(2)}) %all-to-all-start.3) | async-done | bytes 786464 | tf_op jit(solution)/shard_map/all_to_all | solution.py:224
  377.6 2.7 maximum_add_fusion.3
  (140 shorter events, 45.3 us)
Async XLA Ops:
  7.2 53.0 %all-gather.2.cloned.1.call-start = ((), (), s32[]{:S(2)}) async-start(), calls=%async_computation.4 | async-start | bytes 4325376 | tf_op jit(solution)/shard_map/all_gather | solution.py:152
  73.8 2.8 copy-start.8
  73.8 2.8 copy-start.10
  109.1 23.7 %all-to-all-start = ((f32[128,2,6,128]{3,1,2,0:T(2,128)}), f32[128,2,6,128]{3,1,2,0:T(2,128)}, u32[]{:S(2)}, u32[]{:S(2)}) async-start(f32[128,2,6,128]{3,1,2,0:T(2,128)} %broadcast_in_dim.132), calls=%async_computation | async-start | bytes 1572864 | tf_op jit(solution)/shard_map/all_to_all | solution.py:224
  118.0 1.3 copy-start.9
  132.9 1.5 copy-start.15
  132.9 1.6 copy-start.16
  138.0 1.2 copy-start
  138.0 1.7 copy-start.2
  195.8 21.2 %all-to-all-start.1 = ((f32[128,2,6,128]{3,1,2,0:T(2,128)}), f32[128,2,6,128]{3,1,2,0:T(2,128)S(1)}, u32[]{:S(2)}, u32[]{:S(2)}) async-start(f32[128,2,6,128]{3,1,2,0:T(2,128)} %broadcast_in_dim.135), calls=%async_computation.1 | async-start | bytes 1572864 | tf_op jit(solution)/shard_map/all_to_all | solution.py:224
  205.8 11.5 %copy-start.17 = (f32[3,512,128]{2,1,0:T(8,128)S(1)}, f32[3,512,128]{2,1,0:T(8,128)}, u32[]{:S(2)}) copy-start(f32[3,512,128]{2,1,0:T(8,128)} %get-tuple-element.59) | copy-start | bytes 2359300
  217.3 2.8 copy-start.1
  217.3 2.8 copy-start.3
  222.1 1.4 copy-start.11
  222.1 1.7 copy-start.13
  256.3 21.6 %all-to-all-start.2 = ((f32[128,2,6,128]{3,1,2,0:T(2,128)}), f32[128,2,6,128]{3,1,2,0:T(2,128)}, u32[]{:S(2)}, u32[]{:S(2)}) async-start(f32[128,2,6,128]{3,1,2,0:T(2,128)} %broadcast_in_dim.136), calls=%async_computation.2 | async-start | bytes 1572864 | tf_op jit(solution)/shard_map/all_to_all | solution.py:224
  265.5 1.2 copy-start.12
  278.0 1.5 copy-start.18
  278.0 1.6 copy-start.19
  283.2 1.7 copy-start.6
  356.4 21.0 %all-to-all-start.3 = ((f32[128,2,6,128]{3,1,2,0:T(2,128)}), f32[128,2,6,128]{3,1,2,0:T(2,128)S(1)}, u32[]{:S(2)}, u32[]{:S(2)}) async-start(f32[128,2,6,128]{3,1,2,0:T(2,128)} %broadcast_in_dim.137), calls=%async_computation.3 | async-start | bytes 1572864 | tf_op jit(solution)/shard_map/all_to_all | solution.py:224
  362.1 15.5 %copy-start.14 = (f32[3,512,128]{2,1,0:T(8,128)S(1)}, f32[3,512,128]{2,1,0:T(8,128)}, u32[]{:S(2)}) copy-start(f32[3,512,128]{2,1,0:T(8,128)} %get-tuple-element.55) | copy-start | bytes 2359300
  377.6 2.8 copy-start.5
  377.6 2.8 copy-start.7
  (1 other events, 1.2 us)
Sparse Core Ops, SparseCore 0:
  10.3 49.8 all-gather.1

commit v10 on v8

--- a/solution.py
+++ b/solution.py
@@ -105,15 +105,22 @@
                 rel_z = src_ref[5, rows, :] - tw
                 dist_sq = sep_x * sep_x + sep_y * sep_y + sep_z * sep_z + soften_sq
                 inv_r = lax.rsqrt(dist_sq)
-                inv_cube = mass_ref[rows, :] * inv_r * inv_r * inv_r
-                radial = 3.0 * (sep_x * rel_x + sep_y * rel_y + sep_z * rel_z) * inv_r * inv_r
+                inv_sq = inv_r * inv_r
+                inv_cube = mass_ref[rows, :] * inv_sq * inv_r
+                radial = (sep_x * rel_x + sep_y * rel_y + sep_z * rel_z) * inv_sq
+                pull_x = inv_cube * sep_x
+                pull_y = inv_cube * sep_y
+                pull_z = inv_cube * sep_z
                 return (
-                    acc[0] + inv_cube * sep_x,
-                    acc[1] + inv_cube * sep_y,
-                    acc[2] + inv_cube * sep_z,
-                    acc[3] + inv_cube * (rel_x - radial * sep_x),
-                    acc[4] + inv_cube * (rel_y - radial * sep_y),
-                    acc[5] + inv_cube * (rel_z - radial * sep_z),
+                    acc[0] + pull_x,
+                    acc[1] + pull_y,
+                    acc[2] + pull_z,
+                    acc[3] + inv_cube * rel_x,
+                    acc[4] + inv_cube * rel_y,
+                    acc[5] + inv_cube * rel_z,
+                    acc[6] + radial * pull_x,
+                    acc[7] + radial * pull_y,
+                    acc[8] + radial * pull_z,
                 )
 
             def per_group(g, acc):
@@ -122,8 +129,8 @@
                 return acc
 
             zero = jnp.zeros((8, 128), jnp.float32)
-            acc = lax.fori_loop(lo, hi, per_group, (zero,) * 6)
-            for k in range(6):
+            acc = lax.fori_loop(lo, hi, per_group, (zero,) * 9)
+            for k in range(9):
                 out_ref[part, k, pl.ds(t, 1), :] = jnp.sum(acc[k], axis=0, keepdims=True)
             return carry
 
@@ -133,7 +140,7 @@
 def kernel_forces(ranges, targets, field, masses):
     out = pl.pallas_call(
         _force_kernel,
-        out_shape=jax.ShapeDtypeStruct((2, 6, targets.shape[2], 128), jnp.float32),
+        out_shape=jax.ShapeDtypeStruct((2, 9, targets.shape[2], 128), jnp.float32),
         in_specs=[
             pl.BlockSpec(memory_space=pltpu.MemorySpace.SMEM),
             pl.BlockSpec(memory_space=pltpu.MemorySpace.SMEM),
@@ -142,17 +149,17 @@
         ],
         out_specs=pl.BlockSpec(memory_space=pltpu.MemorySpace.VMEM),
     )(ranges, targets, field, masses)
-    return jnp.sum(out, axis=3)
+    sums = jnp.sum(out, axis=3)
+    return jnp.concatenate([sums[:, 0:3], sums[:, 3:6] - 3.0 * sums[:, 6:9]], axis=1)
 
 
 def shards(phase_space, derivatives, body_mass, active_lists):
     every = ("ia", "ja", "ha")
     plane = ("ja", "ha")
     local = jnp.concatenate([phase_space, derivatives, body_mass[None, :]], axis=0)
+    local = local.reshape(13, local.shape[1] // BLK, BLK)
     full = lax.all_gather(local, plane, axis=1, tiled=True)
-    total = full.shape[1]
-    block_total = total // BLK
-    full = full.reshape(13, block_total, BLK)
+    block_total = full.shape[1]
     tiles = block_total // (8 * GROUP)
     slots = active_lists.shape[1] * active_lists.shape[2]
     devices = lax.axis_size("ia") * lax.axis_size("ja") * lax.axis_size("ha")

time: 360 us -> 368 us (1.022)
  Pallas kernels: 147 us -> 154 us
    pallas_call x4, Pallas kernels: 147 us -> 154 us  [kernel_forces(): pl.pallas_call(_force_kernel, out_shape=jax.ShapeDtypeStruct((2, 9, targe...]
    unnamed x47 -> x48, local copies, waits for them, and re-layouts: 7.71 us -> 4.7 us
where the time goes in v10:
time: 368 us; the launch traced here: 366 us
  Pallas kernels  154 us (42%)
  waiting for transfers between devices  81.4 us (22%)
  other arithmetic  40.6 us (11%)
  between operations  29.8 us (8%)
  local copies, waits for them, and re-layouts  27.7 us (8%)
  starting transfers between devices  22.2 us (6%)
  matrix products  10.7 us (3%)
    pallas_call x4, Pallas kernels, kernel_forces(): pl.pallas_call(_force_kernel, out_shape=jax.ShapeDtypeStruct((2, 9, targe...  154 us
    all_to_all x4, waiting for transfers between devices, shards(): lax.all_to_all(sent, every, 0, 0, tiled=True).reshape(2 * devices, 6, BLK)  46.7 us
    all_gather x1, waiting for transfers between devices, shards(): full = lax.all_gather(local, plane, axis=1, tiled=True)  34.7 us
    all_to_all x4, starting transfers between devices, shards(): lax.all_to_all(sent, every, 0, 0, tiled=True).reshape(2 * devices, 6, BLK)  22.2 us
    dot_general x4, matrix products, shards(): jnp.einsum('bu,ucl->cbl', onehot, got, precision=lax.Precision.HIGHEST, p...  10.7 us
  transfers between devices with their start and end apart: 5, of which 5 were waited for; matrix products, arithmetic and copies ran while one was open for 7% of the time, Pallas kernels for 0%

profile of v10, /device:TPU:1, one launch (start us, length us, event | category | flops | bytes accessed | tf_op | source)
XLA Modules:
  0.0 366.4 jit_solution(13495631957724780421)
XLA Ops:
  11.9 4.7 %gather_fusion.2 = s32[512]{0:T(512)S(1)} fusion(s32[4,128]{1,0:T(4,128)S(1)} %select_reduce_fusion, s32[512]{0:T(512)S(1)} %get-tuple-element.103), kind=kCustom, calls=%fused_computation.1.clone | custom fusion | bytes 8192 | tf_op jit(solution)/shard_map/jit(take_along_axis)/gather | solution.py:187
  16.5 4.7 %gather_fusion.3 = s32[512]{0:T(512)S(1)} fusion(s32[4,128]{1,0:T(4,128)S(1)} %select_reduce_fusion, s32[512]{0:T(512)S(1)} %get-tuple-element.104), kind=kCustom, calls=%fused_computation.3.clone | custom fusion | bytes 8192 | tf_op jit(solution)/shard_map/jit(take_along_axis)/gather | solution.py:188
  26.2 34.7 %all-gather.2.cloned.1.call-done = f32[13,512,128]{2,1,0:T(8,128)} async-done(((f32[13,16,128]{2,1,0:T(8,128)}), f32[13,512,128]{2,1,0:T(8,128)}) %all-gather.2.cloned.1.call-update) | async-done | bytes 3407888 | tf_op jit(solution)/shard_map/all_gather | solution.py:161
  64.2 4.4 %multiply_reduce_fusion.7 = (f32[512,128]{1,0:T(8,128)}, f32[512,128]{1,0:T(8,128)}, f32[3,512,128]{2,1,0:T(8,128)}, f32[3,512,128]{2,1,0:T(8,128)}) fusion(f32[13,512,128]{2,1,0:T(8,128)} %all-gather.2.cloned.1.call-done), kind=kLoop, calls=%fused_computation.71 | loop fusion | flops 2818048 | bytes 5242880 | tf_op jit(solution)/shard_map/reduce_sum | solution.py:60
  73.6 2.8 pad_maximum_fusion.src_ref
  77.0 26.4 %shard_map.59 = f32[2,9,128,128]{3,2,1,0:T(8,128)} custom-call(s32[4]{0:T(128)} %get-tuple-element.89.ctl_ref, f32[2,6,128]{2,1,0:T(8,128)} %pad_maximum_fusion.5.tgt_ref, f32[6,512,128]{2,1,0:T(8,128)} %pad_maximum_fusion.src_ref, f32[512,128]{1,0:T(8,128)} %slice_bitcast_fusion.mass_ref), custom_call_target="tpu_custom_call" | custom-call | tf_op jit(solution)/shard_map/pallas_call | solution.py:141
  106.2 7.7 %all-to-all-start = ((f32[128,2,6,128]{3,1,2,0:T(2,128)}), f32[128,2,6,128]{3,1,2,0:T(2,128)}, u32[]{:S(2)}, u32[]{:S(2)}) async-start(f32[128,2,6,128]{3,1,2,0:T(2,128)} %broadcast_in_dim.129), calls=%async_computation | async-start | bytes 1572864 | tf_op jit(solution)/shard_map/all_to_all | solution.py:231
  116.5 2.5 broadcast_multiply_fusion.3
  119.0 11.1 %all-to-all-done = f32[128,2,6,128]{3,1,2,0:T(2,128)} async-done(((f32[128,2,6,128]{3,1,2,0:T(2,128)}), f32[128,2,6,128]{3,1,2,0:T(2,128)}, u32[]{:S(2)}, u32[]{:S(2)}) %all-to-all-start) | async-done | bytes 786464 | tf_op jit(solution)/shard_map/all_to_all | solution.py:231
  131.6 2.6 maximum_add_fusion
  138.7 44.5 %shard_map.60 = f32[2,9,128,128]{3,2,1,0:T(8,128)} custom-call(s32[4]{0:T(128)} %get-tuple-element.88.ctl_ref, f32[2,6,128]{2,1,0:T(8,128)} %pad_maximum_fusion.7.tgt_ref, f32[6,512,128]{2,1,0:T(8,128)} %pad_maximum_fusion.1.src_ref, f32[512,128]{1,0:T(8,128)} %slice_bitcast_fusion.mass_ref), custom_call_target="tpu_custom_call" | custom-call | tf_op jit(solution)/shard_map/pallas_call | solution.py:141
  186.0 4.6 %all-to-all-start.1 = ((f32[128,2,6,128]{3,1,2,0:T(2,128)}), f32[128,2,6,128]{3,1,2,0:T(2,128)S(1)}, u32[]{:S(2)}, u32[]{:S(2)}) async-start(f32[128,2,6,128]{3,1,2,0:T(2,128)} %broadcast_in_dim.132), calls=%async_computation.1 | async-start | bytes 1572864 | tf_op jit(solution)/shard_map/all_to_all | solution.py:231
  195.6 11.5 %all-to-all-done.1 = f32[128,2,6,128]{3,1,2,0:T(2,128)S(1)} async-done(((f32[128,2,6,128]{3,1,2,0:T(2,128)}), f32[128,2,6,128]{3,1,2,0:T(2,128)S(1)}, u32[]{:S(2)}, u32[]{:S(2)}) %all-to-all-start.1) | async-done | bytes 786464 | tf_op jit(solution)/shard_map/all_to_all | solution.py:231
  207.4 2.7 maximum_add_fusion.1
  214.5 26.4 %shard_map.61 = f32[2,9,128,128]{3,2,1,0:T(8,128)} custom-call(s32[4]{0:T(128)} %get-tuple-element.87.ctl_ref, f32[2,6,128]{2,1,0:T(8,128)} %pad_maximum_fusion.9.tgt_ref, f32[6,512,128]{2,1,0:T(8,128)} %pad_maximum_fusion.2.src_ref, f32[512,128]{1,0:T(8,128)} %slice_bitcast_fusion.mass_ref), custom_call_target="tpu_custom_call" | custom-call | tf_op jit(solution)/shard_map/pallas_call | solution.py:141
  241.0 1.6 reduce_sum.134
  243.8 5.4 %all-to-all-start.2 = ((f32[128,2,6,128]{3,1,2,0:T(2,128)}), f32[128,2,6,128]{3,1,2,0:T(2,128)}, u32[]{:S(2)}, u32[]{:S(2)}) async-start(f32[128,2,6,128]{3,1,2,0:T(2,128)} %broadcast_in_dim.133), calls=%async_computation.2 | async-start | bytes 1572864 | tf_op jit(solution)/shard_map/all_to_all | solution.py:231
  254.0 2.5 broadcast_multiply_fusion.1
  256.5 8.9 %all-to-all-done.2 = f32[128,2,6,128]{3,1,2,0:T(2,128)} async-done(((f32[128,2,6,128]{3,1,2,0:T(2,128)}), f32[128,2,6,128]{3,1,2,0:T(2,128)}, u32[]{:S(2)}, u32[]{:S(2)}) %all-to-all-start.2) | async-done | bytes 786464 | tf_op jit(solution)/shard_map/all_to_all | solution.py:231
  267.0 2.6 maximum_add_fusion.2
  274.2 56.8 %shard_map.62 = f32[2,9,128,128]{3,2,1,0:T(8,128)} custom-call(s32[4]{0:T(128)} %get-tuple-element.86.ctl_ref, f32[2,6,128]{2,1,0:T(8,128)} %pad_maximum_fusion.11.tgt_ref, f32[6,512,128]{2,1,0:T(8,128)} %pad_maximum_fusion.3.src_ref, f32[512,128]{1,0:T(8,128)} %slice_bitcast_fusion.mass_ref), custom_call_target="tpu_custom_call" | custom-call | tf_op jit(solution)/shard_map/pallas_call | solution.py:141
  333.7 4.5 %all-to-all-start.3 = ((f32[128,2,6,128]{3,1,2,0:T(2,128)}), f32[128,2,6,128]{3,1,2,0:T(2,128)S(1)}, u32[]{:S(2)}, u32[]{:S(2)}) async-start(f32[128,2,6,128]{3,1,2,0:T(2,128)} %broadcast_in_dim.134), calls=%async_computation.3 | async-start | bytes 1572864 | tf_op jit(solution)/shard_map/all_to_all | solution.py:231
  339.5 15.2 %all-to-all-done.3 = f32[128,2,6,128]{3,1,2,0:T(2,128)S(1)} async-done(((f32[128,2,6,128]{3,1,2,0:T(2,128)}), f32[128,2,6,128]{3,1,2,0:T(2,128)S(1)}, u32[]{:S(2)}, u32[]{:S(2)}) %all-to-all-start.3) | async-done | bytes 786464 | tf_op jit(solution)/shard_map/all_to_all | solution.py:231
  355.0 2.7 maximum_add_fusion.3
  (149 shorter events, 45.3 us)
Async XLA Ops:
  7.2 53.8 %all-gather.2.cloned.1.call-start = ((), (), s32[]{:S(2)}) async-start(), calls=%async_computation.4 | async-start | bytes 3514368 | tf_op jit(solution)/shard_map/all_gather | solution.py:161
  64.2 4.4 %copy-start = (f32[13,512,128]{2,1,0:T(8,128)S(1)}, f32[13,512,128]{2,1,0:T(8,128)}, u32[]{:S(2)}) copy-start(f32[13,512,128]{2,1,0:T(8,128)} %all-gather.2.cloned.1.call-done) | copy-start | bytes 10223620
  73.6 2.8 copy-start.9
  73.6 2.8 copy-start.11
  106.2 23.8 %all-to-all-start = ((f32[128,2,6,128]{3,1,2,0:T(2,128)}), f32[128,2,6,128]{3,1,2,0:T(2,128)}, u32[]{:S(2)}, u32[]{:S(2)}) async-start(f32[128,2,6,128]{3,1,2,0:T(2,128)} %broadcast_in_dim.129), calls=%async_computation | async-start | bytes 1572864 | tf_op jit(solution)/shard_map/all_to_all | solution.py:231
  115.2 1.3 copy-start.10
  130.0 1.5 copy-start.16
  130.0 1.6 copy-start.17
  135.1 1.6 copy-start.3
  186.0 21.2 %all-to-all-start.1 = ((f32[128,2,6,128]{3,1,2,0:T(2,128)}), f32[128,2,6,128]{3,1,2,0:T(2,128)S(1)}, u32[]{:S(2)}, u32[]{:S(2)}) async-start(f32[128,2,6,128]{3,1,2,0:T(2,128)} %broadcast_in_dim.132), calls=%async_computation.1 | async-start | bytes 1572864 | tf_op jit(solution)/shard_map/all_to_all | solution.py:231
  195.6 11.8 %copy-start.18 = (f32[3,512,128]{2,1,0:T(8,128)S(1)}, f32[3,512,128]{2,1,0:T(8,128)}, u32[]{:S(2)}) copy-start(f32[3,512,128]{2,1,0:T(8,128)} %get-tuple-element.59) | copy-start | bytes 2359300
  207.4 2.8 copy-start.2
  207.4 2.8 copy-start.4
  212.2 1.4 copy-start.12
  212.2 1.7 copy-start.14
  243.8 21.6 %all-to-all-start.2 = ((f32[128,2,6,128]{3,1,2,0:T(2,128)}), f32[128,2,6,128]{3,1,2,0:T(2,128)}, u32[]{:S(2)}, u32[]{:S(2)}) async-start(f32[128,2,6,128]{3,1,2,0:T(2,128)} %broadcast_in_dim.133), calls=%async_computation.2 | async-start | bytes 1572864 | tf_op jit(solution)/shard_map/all_to_all | solution.py:231
  252.8 1.2 copy-start.13
  265.4 1.5 copy-start.19
  265.4 1.6 copy-start.20
  270.6 1.6 copy-start.7
  333.7 21.0 %all-to-all-start.3 = ((f32[128,2,6,128]{3,1,2,0:T(2,128)}), f32[128,2,6,128]{3,1,2,0:T(2,128)S(1)}, u32[]{:S(2)}, u32[]{:S(2)}) async-start(f32[128,2,6,128]{3,1,2,0:T(2,128)} %broadcast_in_dim.134), calls=%async_computation.3 | async-start | bytes 1572864 | tf_op jit(solution)/shard_map/all_to_all | solution.py:231
  339.5 15.4 %copy-start.15 = (f32[3,512,128]{2,1,0:T(8,128)S(1)}, f32[3,512,128]{2,1,0:T(8,128)}, u32[]{:S(2)}) copy-start(f32[3,512,128]{2,1,0:T(8,128)} %get-tuple-element.55) | copy-start | bytes 2359300
  355.0 2.8 copy-start.6
  355.0 2.8 copy-start.8
  (2 other events, 2.3 us)
Sparse Core Ops, SparseCore 0:
  10.2 50.7 all-gather.1

commit v11 on v10

--- a/solution.py
+++ b/solution.py
@@ -229,6 +229,8 @@
         partial = kernel_forces(ranges, targets, predicted, mass)
         sent = jnp.broadcast_to(partial[None], (devices,) + partial.shape)
         got = lax.all_to_all(sent, every, 0, 0, tiled=True).reshape(2 * devices, 6, BLK)
+        if step_index == STEPS - 1:
+            break
         mutual = jnp.einsum(
             "bu,ucl->cbl", onehot, got,
             precision=lax.Precision.HIGHEST, preferred_element_type=jnp.float32,
@@ -242,8 +244,19 @@
     local_count = phase_space.shape[1]
     local_blocks = local_count // BLK
     offset = (lax.axis_index("ja") * lax.axis_size("ha") + lax.axis_index("ha")) * local_blocks
-    phase_out = lax.dynamic_slice_in_dim(phase, offset, local_blocks, axis=1)
-    deriv_out = lax.dynamic_slice_in_dim(deriv, offset, local_blocks, axis=1)
+    own = lambda x: lax.dynamic_slice_in_dim(x, offset, local_blocks, axis=1)
+    mutual = jnp.einsum(
+        "bu,ucl->cbl", lax.dynamic_slice_in_dim(onehot, offset, local_blocks, axis=0), got,
+        precision=lax.Precision.HIGHEST, preferred_element_type=jnp.float32,
+    )
+    own_phase = own(phase)
+    own_deriv = own(deriv)
+    own_elapsed = own(elapsed)
+    fresh = mutual + star_terms(own(predicted))
+    corrected = correct(own_phase, own_deriv, fresh, own_elapsed)
+    active = lax.dynamic_slice_in_dim(active_flags, offset, local_blocks)[None, :, None]
+    phase_out = jnp.where(active, corrected, own_phase)
+    deriv_out = jnp.where(active, fresh, own_deriv)
     return (phase_out.reshape(6, local_count), deriv_out.reshape(6, local_count))
 
 

time: 368 us -> 367 us (level)
    dot_general x4 -> x3, matrix products: 10.7 us -> 7.96 us  [shards(): jnp.einsum('bu,ucl->cbl', onehot, got, precision=lax.Precision.HIGHEST, p...]
where the time goes in v11:
time: 367 us; the launch traced here: 366 us
  Pallas kernels  154 us (42%)
  waiting for transfers between devices  82.7 us (23%)
  other arithmetic  40.7 us (11%)
  between operations  29.7 us (8%)
  local copies, waits for them, and re-layouts  27.6 us (8%)
  starting transfers between devices  22.3 us (6%)
  matrix products  8.46 us (2%)
    pallas_call x4, Pallas kernels, kernel_forces(): pl.pallas_call(_force_kernel, out_shape=jax.ShapeDtypeStruct((2, 9, targe...  154 us
    all_to_all x4, waiting for transfers between devices, shards(): lax.all_to_all(sent, every, 0, 0, tiled=True).reshape(2 * devices, 6, BLK)  47.9 us
    all_gather x1, waiting for transfers between devices, shards(): full = lax.all_gather(local, plane, axis=1, tiled=True)  34.8 us
    all_to_all x4, starting transfers between devices, shards(): lax.all_to_all(sent, every, 0, 0, tiled=True).reshape(2 * devices, 6, BLK)  22.3 us
    dot_general x3, matrix products, shards(): jnp.einsum('bu,ucl->cbl', onehot, got, precision=lax.Precision.HIGHEST, p...  7.96 us
  transfers between devices with their start and end apart: 5, of which 5 were waited for; matrix products, arithmetic and copies ran while one was open for 7% of the time, Pallas kernels for 0%

profile of v11, /device:TPU:1, one launch (start us, length us, event | category | flops | bytes accessed | tf_op | source)
XLA Modules:
  0.0 365.5 jit_solution(7407081246276206777)
XLA Ops:
  11.9 4.7 %gather_fusion.2 = s32[512]{0:T(512)S(1)} fusion(s32[4,128]{1,0:T(4,128)S(1)} %select_reduce_fusion, s32[512]{0:T(512)S(1)} %get-tuple-element.103), kind=kCustom, calls=%fused_computation.1.clone | custom fusion | bytes 8192 | tf_op jit(solution)/shard_map/jit(take_along_axis)/gather | solution.py:187
  16.5 4.7 %gather_fusion.3 = s32[512]{0:T(512)S(1)} fusion(s32[4,128]{1,0:T(4,128)S(1)} %select_reduce_fusion, s32[512]{0:T(512)S(1)} %get-tuple-element.104), kind=kCustom, calls=%fused_computation.3.clone | custom fusion | bytes 8192 | tf_op jit(solution)/shard_map/jit(take_along_axis)/gather | solution.py:188
  26.2 34.8 %all-gather.2.cloned.1.call-done = f32[13,512,128]{2,1,0:T(8,128)} async-done(((f32[13,16,128]{2,1,0:T(8,128)}), f32[13,512,128]{2,1,0:T(8,128)}) %all-gather.2.cloned.1.call-update) | async-done | bytes 3407888 | tf_op jit(solution)/shard_map/all_gather | solution.py:161
  64.2 4.4 %multiply_reduce_fusion.5 = (f32[512,128]{1,0:T(8,128)}, f32[512,128]{1,0:T(8,128)}, f32[3,512,128]{2,1,0:T(8,128)}, f32[3,512,128]{2,1,0:T(8,128)}) fusion(f32[13,512,128]{2,1,0:T(8,128)} %all-gather.2.cloned.1.call-done), kind=kLoop, calls=%fused_computation.66 | loop fusion | flops 2818048 | bytes 5242880 | tf_op jit(solution)/shard_map/reduce_sum | solution.py:60
  73.8 2.7 pad_maximum_fusion.1.src_ref
  77.2 26.4 %shard_map.59 = f32[2,9,128,128]{3,2,1,0:T(8,128)} custom-call(s32[4]{0:T(128)} %get-tuple-element.91.ctl_ref, f32[2,6,128]{2,1,0:T(8,128)} %pad_maximum_fusion.5.tgt_ref, f32[6,512,128]{2,1,0:T(8,128)} %pad_maximum_fusion.1.src_ref, f32[512,128]{1,0:T(8,128)} %slice_bitcast_fusion.mass_ref), custom_call_target="tpu_custom_call" | custom-call | tf_op jit(solution)/shard_map/pallas_call | solution.py:141
  103.6 1.6 reduce_sum.128
  106.4 7.7 %all-to-all-start = ((f32[128,2,6,128]{3,1,2,0:T(2,128)}), f32[128,2,6,128]{3,1,2,0:T(2,128)}, u32[]{:S(2)}, u32[]{:S(2)}) async-start(f32[128,2,6,128]{3,1,2,0:T(2,128)} %broadcast_in_dim.133), calls=%async_computation | async-start | bytes 1572864 | tf_op jit(solution)/shard_map/all_to_all | solution.py:231
  116.8 2.5 broadcast_multiply_fusion.2
  119.3 10.9 %all-to-all-done = f32[128,2,6,128]{3,1,2,0:T(2,128)} async-done(((f32[128,2,6,128]{3,1,2,0:T(2,128)}), f32[128,2,6,128]{3,1,2,0:T(2,128)}, u32[]{:S(2)}, u32[]{:S(2)}) %all-to-all-start) | async-done | bytes 786464 | tf_op jit(solution)/shard_map/all_to_all | solution.py:231
  131.8 2.6 maximum_add_fusion
  138.9 44.4 %shard_map.60 = f32[2,9,128,128]{3,2,1,0:T(8,128)} custom-call(s32[4]{0:T(128)} %get-tuple-element.90.ctl_ref, f32[2,6,128]{2,1,0:T(8,128)} %pad_maximum_fusion.7.tgt_ref, f32[6,512,128]{2,1,0:T(8,128)} %pad_maximum_fusion.2.src_ref, f32[512,128]{1,0:T(8,128)} %slice_bitcast_fusion.mass_ref), custom_call_target="tpu_custom_call" | custom-call | tf_op jit(solution)/shard_map/pallas_call | solution.py:141
  183.3 1.6 reduce_sum.131
  186.1 4.7 %all-to-all-start.1 = ((f32[128,2,6,128]{3,1,2,0:T(2,128)}), f32[128,2,6,128]{3,1,2,0:T(2,128)S(1)}, u32[]{:S(2)}, u32[]{:S(2)}) async-start(f32[128,2,6,128]{3,1,2,0:T(2,128)} %broadcast_in_dim.136), calls=%async_computation.1 | async-start | bytes 1572864 | tf_op jit(solution)/shard_map/all_to_all | solution.py:231
  195.5 11.7 %all-to-all-done.1 = f32[128,2,6,128]{3,1,2,0:T(2,128)S(1)} async-done(((f32[128,2,6,128]{3,1,2,0:T(2,128)}), f32[128,2,6,128]{3,1,2,0:T(2,128)S(1)}, u32[]{:S(2)}, u32[]{:S(2)}) %all-to-all-start.1) | async-done | bytes 786464 | tf_op jit(solution)/shard_map/all_to_all | solution.py:231
  207.6 2.7 maximum_add_fusion.1
  214.6 26.4 %shard_map.61 = f32[2,9,128,128]{3,2,1,0:T(8,128)} custom-call(s32[4]{0:T(128)} %get-tuple-element.89.ctl_ref, f32[2,6,128]{2,1,0:T(8,128)} %pad_maximum_fusion.9.tgt_ref, f32[6,512,128]{2,1,0:T(8,128)} %pad_maximum_fusion.3.src_ref, f32[512,128]{1,0:T(8,128)} %slice_bitcast_fusion.mass_ref), custom_call_target="tpu_custom_call" | custom-call | tf_op jit(solution)/shard_map/pallas_call | solution.py:141
  243.9 5.4 %all-to-all-start.2 = ((f32[128,2,6,128]{3,1,2,0:T(2,128)}), f32[128,2,6,128]{3,1,2,0:T(2,128)}, u32[]{:S(2)}, u32[]{:S(2)}) async-start(f32[128,2,6,128]{3,1,2,0:T(2,128)} %broadcast_in_dim.137), calls=%async_computation.2 | async-start | bytes 1572864 | tf_op jit(solution)/shard_map/all_to_all | solution.py:231
  254.1 2.5 broadcast_multiply_fusion
  256.5 9.0 %all-to-all-done.2 = f32[128,2,6,128]{3,1,2,0:T(2,128)} async-done(((f32[128,2,6,128]{3,1,2,0:T(2,128)}), f32[128,2,6,128]{3,1,2,0:T(2,128)}, u32[]{:S(2)}, u32[]{:S(2)}) %all-to-all-start.2) | async-done | bytes 786464 | tf_op jit(solution)/shard_map/all_to_all | solution.py:231
  267.1 2.6 maximum_add_fusion.2
  274.3 56.8 %shard_map.62 = f32[2,9,128,128]{3,2,1,0:T(8,128)} custom-call(s32[4]{0:T(128)} %get-tuple-element.88.ctl_ref, f32[2,6,128]{2,1,0:T(8,128)} %pad_maximum_fusion.11.tgt_ref, f32[6,512,128]{2,1,0:T(8,128)} %pad_maximum_fusion.src_ref, f32[512,128]{1,0:T(8,128)} %slice_bitcast_fusion.mass_ref), custom_call_target="tpu_custom_call" | custom-call | tf_op jit(solution)/shard_map/pallas_call | solution.py:141
  333.8 4.5 %all-to-all-start.3 = ((f32[128,2,6,128]{3,1,2,0:T(2,128)}), f32[128,2,6,128]{3,1,2,0:T(2,128)S(1)}, u32[]{:S(2)}, u32[]{:S(2)}) async-start(f32[128,2,6,128]{3,1,2,0:T(2,128)} %broadcast_in_dim.138), calls=%async_computation.3 | async-start | bytes 1572864 | tf_op jit(solution)/shard_map/all_to_all | solution.py:231
  338.5 16.3 %all-to-all-done.3 = f32[128,2,6,128]{3,1,2,0:T(2,128)S(1)} async-done(((f32[128,2,6,128]{3,1,2,0:T(2,128)}), f32[128,2,6,128]{3,1,2,0:T(2,128)S(1)}, u32[]{:S(2)}, u32[]{:S(2)}) %all-to-all-start.3) | async-done | bytes 786464 | tf_op jit(solution)/shard_map/all_to_all | solution.py:231
  (148 shorter events, 44.2 us)
Async XLA Ops:
  7.2 53.8 %all-gather.2.cloned.1.call-start = ((), (), s32[]{:S(2)}) async-start(), calls=%async_computation.4 | async-start | bytes 3514368 | tf_op jit(solution)/shard_map/all_gather | solution.py:161
  64.1 4.4 %copy-start = (f32[13,512,128]{2,1,0:T(8,128)S(1)}, f32[13,512,128]{2,1,0:T(8,128)}, u32[]{:S(2)}) copy-start(f32[13,512,128]{2,1,0:T(8,128)} %all-gather.2.cloned.1.call-done) | copy-start | bytes 10223620
  73.8 2.8 copy-start.5
  73.8 2.8 copy-start.7
  106.4 23.8 %all-to-all-start = ((f32[128,2,6,128]{3,1,2,0:T(2,128)}), f32[128,2,6,128]{3,1,2,0:T(2,128)}, u32[]{:S(2)}, u32[]{:S(2)}) async-start(f32[128,2,6,128]{3,1,2,0:T(2,128)} %broadcast_in_dim.133), calls=%async_computation | async-start | bytes 1572864 | tf_op jit(solution)/shard_map/all_to_all | solution.py:231
  115.5 1.3 copy-start.6
  130.2 1.5 copy-start.15
  130.2 1.6 copy-start.16
  135.3 1.2 copy-start.1
  135.3 1.6 copy-start.3
  186.1 21.1 %all-to-all-start.1 = ((f32[128,2,6,128]{3,1,2,0:T(2,128)}), f32[128,2,6,128]{3,1,2,0:T(2,128)S(1)}, u32[]{:S(2)}, u32[]{:S(2)}) async-start(f32[128,2,6,128]{3,1,2,0:T(2,128)} %broadcast_in_dim.136), calls=%async_computation.1 | async-start | bytes 1572864 | tf_op jit(solution)/shard_map/all_to_all | solution.py:231
  195.5 12.0 %copy-start.17 = (f32[3,512,128]{2,1,0:T(8,128)S(1)}, f32[3,512,128]{2,1,0:T(8,128)}, u32[]{:S(2)}) copy-start(f32[3,512,128]{2,1,0:T(8,128)} %get-tuple-element.56) | copy-start | bytes 2359300
  207.5 2.8 copy-start.2
  207.6 2.8 copy-start.4
  212.3 1.4 copy-start.8
  212.3 1.7 copy-start.10
  243.9 21.7 %all-to-all-start.2 = ((f32[128,2,6,128]{3,1,2,0:T(2,128)}), f32[128,2,6,128]{3,1,2,0:T(2,128)}, u32[]{:S(2)}, u32[]{:S(2)}) async-start(f32[128,2,6,128]{3,1,2,0:T(2,128)} %broadcast_in_dim.137), calls=%async_computation.2 | async-start | bytes 1572864 | tf_op jit(solution)/shard_map/all_to_all | solution.py:231
  252.8 1.2 copy-start.9
  265.5 1.5 copy-start.13
  265.5 1.6 copy-start.14
  270.7 1.2 copy-start.11
  270.7 1.6 copy-start.12
  333.8 21.0 %all-to-all-start.3 = ((f32[128,2,6,128]{3,1,2,0:T(2,128)}), f32[128,2,6,128]{3,1,2,0:T(2,128)S(1)}, u32[]{:S(2)}, u32[]{:S(2)}) async-start(f32[128,2,6,128]{3,1,2,0:T(2,128)} %broadcast_in_dim.138), calls=%async_computation.3 | async-start | bytes 1572864 | tf_op jit(solution)/shard_map/all_to_all | solution.py:231
  338.4 16.6 %slice-start = ((f32[4,512,256]{2,1,0:T(8,128)}), f32[1,512,256]{2,1,0:T(8,128)S(1)}, s32[]{:S(2)}) async-start(f32[4,512,256]{2,1,0:T(8,128)} %fusion), calls=%async_computation.5 | async-start | bytes 1048576 | tf_op jit(solution)/shard_map/slice | solution.py:218
Sparse Core Ops, SparseCore 0:
  10.2 50.7 all-gather.1

commit v12 on v11

--- a/solution.py
+++ b/solution.py
@@ -229,13 +229,14 @@
         partial = kernel_forces(ranges, targets, predicted, mass)
         sent = jnp.broadcast_to(partial[None], (devices,) + partial.shape)
         got = lax.all_to_all(sent, every, 0, 0, tiled=True).reshape(2 * devices, 6, BLK)
+        later, _ = lax.optimization_barrier((predicted, partial))
         if step_index == STEPS - 1:
             break
         mutual = jnp.einsum(
             "bu,ucl->cbl", onehot, got,
             precision=lax.Precision.HIGHEST, preferred_element_type=jnp.float32,
         )
-        fresh = mutual + star_terms(predicted)
+        fresh = mutual + star_terms(later)
         corrected = correct(phase, deriv, fresh, elapsed)
         active = active_flags[None, :, None]
         phase = jnp.where(active, corrected, phase)
@@ -252,7 +253,7 @@
     own_phase = own(phase)
     own_deriv = own(deriv)
     own_elapsed = own(elapsed)
-    fresh = mutual + star_terms(own(predicted))
+    fresh = mutual + star_terms(own(later))
     corrected = correct(own_phase, own_deriv, fresh, own_elapsed)
     active = lax.dynamic_slice_in_dim(active_flags, offset, local_blocks)[None, :, None]
     phase_out = jnp.where(active, corrected, own_phase)

time: 367 us -> 356 us (0.970)
  Pallas kernels: 154 us -> 148 us
  waiting for transfers between devices: 82.7 us -> 76.9 us
    pallas_call x4, Pallas kernels: 154 us -> 148 us  [kernel_forces(): pl.pallas_call(_force_kernel, out_shape=jax.ShapeDtypeStruct((2, 9, targe...]
    all_to_all x4, waiting for transfers between devices: 47.9 us -> 42.2 us  [shards(): lax.all_to_all(sent, every, 0, 0, tiled=True).reshape(2 * devices, 6, BLK)]
    add x1 -> x4, other arithmetic: 0.38 us -> 4.59 us  [predict(): position + elapsed * (velocity + elapsed * (acceleration * 0.5 + elapsed...]
  transfers between devices with their start and end apart: 5 -> 5, of which waited for: 5 -> 5; matrix products, arithmetic and copies ran while one was open for 7% -> 8% of each run, Pallas kernels for 0% -> 0%
where the time goes in v12:
time: 356 us; the launch traced here: 355 us
  Pallas kernels  148 us (42%)
  waiting for transfers between devices  76.9 us (22%)
  other arithmetic  42.5 us (12%)
  between operations  29.4 us (8%)
  local copies, waits for them, and re-layouts  27.3 us (8%)
  starting transfers between devices  22.2 us (6%)
  matrix products  8.46 us (2%)
    pallas_call x4, Pallas kernels, kernel_forces(): pl.pallas_call(_force_kernel, out_shape=jax.ShapeDtypeStruct((2, 9, targe...  148 us
    all_to_all x4, waiting for transfers between devices, shards(): lax.all_to_all(sent, every, 0, 0, tiled=True).reshape(2 * devices, 6, BLK)  42.2 us
    all_gather x1, waiting for transfers between devices, shards(): full = lax.all_gather(local, plane, axis=1, tiled=True)  34.8 us
    all_to_all x4, starting transfers between devices, shards(): lax.all_to_all(sent, every, 0, 0, tiled=True).reshape(2 * devices, 6, BLK)  22.2 us
    dot_general x3, matrix products, shards(): jnp.einsum('bu,ucl->cbl', onehot, got, precision=lax.Precision.HIGHEST, p...  7.96 us
  transfers between devices with their start and end apart: 5, of which 5 were waited for; matrix products, arithmetic and copies ran while one was open for 8% of the time, Pallas kernels for 0%

profile of v12, /device:TPU:1, one launch (start us, length us, event | category | flops | bytes accessed | tf_op | source)
XLA Modules:
  0.0 354.8 jit_solution(1878728068935649859)
XLA Ops:
  11.8 4.7 %gather_fusion.3 = s32[512]{0:T(512)S(1)} fusion(s32[4,128]{1,0:T(4,128)S(1)} %select_reduce_fusion, s32[512]{0:T(512)S(1)} %get-tuple-element.112), kind=kCustom, calls=%fused_computation.3.clone | custom fusion | bytes 8192 | tf_op jit(solution)/shard_map/jit(take_along_axis)/gather | solution.py:188
  16.5 4.7 %gather_fusion.2 = s32[512]{0:T(512)S(1)} fusion(s32[4,128]{1,0:T(4,128)S(1)} %select_reduce_fusion, s32[512]{0:T(512)S(1)} %get-tuple-element.111), kind=kCustom, calls=%fused_computation.1.clone | custom fusion | bytes 8192 | tf_op jit(solution)/shard_map/jit(take_along_axis)/gather | solution.py:187
  26.2 34.8 %all-gather.2.cloned.1.call-done = f32[13,512,128]{2,1,0:T(8,128)} async-done(((f32[13,16,128]{2,1,0:T(8,128)}), f32[13,512,128]{2,1,0:T(8,128)}) %all-gather.2.cloned.1.call-update) | async-done | bytes 3407888 | tf_op jit(solution)/shard_map/all_gather | solution.py:161
  64.2 3.5 multiply_add_fusion.9
  69.7 2.7 pad_maximum_fusion.src_ref
  73.6 26.4 %shard_map.59 = f32[2,9,128,128]{3,2,1,0:T(8,128)} custom-call(s32[4]{0:T(128)} %get-tuple-element.99.ctl_ref, f32[2,6,128]{2,1,0:T(8,128)} %pad_maximum_fusion.5.tgt_ref, f32[6,512,128]{2,1,0:T(8,128)} %pad_maximum_fusion.src_ref, f32[512,128]{1,0:T(8,128)} %slice_bitcast_fusion.mass_ref), custom_call_target="tpu_custom_call" | custom-call | tf_op jit(solution)/shard_map/pallas_call | solution.py:141
  102.9 7.7 %all-to-all-start = ((f32[128,2,6,128]{3,1,2,0:T(2,128)}), f32[128,2,6,128]{3,1,2,0:T(2,128)}, u32[]{:S(2)}, u32[]{:S(2)}) async-start(f32[128,2,6,128]{3,1,2,0:T(2,128)} %broadcast_in_dim.133), calls=%async_computation | async-start | bytes 1572864 | tf_op jit(solution)/shard_map/all_to_all | solution.py:231
  110.6 2.3 multiply_reduce_fusion.5
  117.7 2.7 slice_multiply_fusion.5
  120.4 6.2 %all-to-all-done = f32[128,2,6,128]{3,1,2,0:T(2,128)} async-done(((f32[128,2,6,128]{3,1,2,0:T(2,128)}), f32[128,2,6,128]{3,1,2,0:T(2,128)}, u32[]{:S(2)}, u32[]{:S(2)}) %all-to-all-start) | async-done | bytes 786464 | tf_op jit(solution)/shard_map/all_to_all | solution.py:231
  128.3 2.6 maximum_add_fusion
  135.3 38.4 %shard_map.60 = f32[2,9,128,128]{3,2,1,0:T(8,128)} custom-call(s32[4]{0:T(128)} %get-tuple-element.98.ctl_ref, f32[2,6,128]{2,1,0:T(8,128)} %pad_maximum_fusion.7.tgt_ref, f32[6,512,128]{2,1,0:T(8,128)} %pad_maximum_fusion.1.src_ref, f32[512,128]{1,0:T(8,128)} %slice_bitcast_fusion.mass_ref), custom_call_target="tpu_custom_call" | custom-call | tf_op jit(solution)/shard_map/pallas_call | solution.py:141
  173.7 1.8 reduce_sum.131
  176.6 4.6 %all-to-all-start.1 = ((f32[128,2,6,128]{3,1,2,0:T(2,128)}), f32[128,2,6,128]{3,1,2,0:T(2,128)S(1)}, u32[]{:S(2)}, u32[]{:S(2)}) async-start(f32[128,2,6,128]{3,1,2,0:T(2,128)} %broadcast_in_dim.136), calls=%async_computation.1 | async-start | bytes 1572864 | tf_op jit(solution)/shard_map/all_to_all | solution.py:231
  186.0 11.7 %all-to-all-done.1 = f32[128,2,6,128]{3,1,2,0:T(2,128)S(1)} async-done(((f32[128,2,6,128]{3,1,2,0:T(2,128)}), f32[128,2,6,128]{3,1,2,0:T(2,128)S(1)}, u32[]{:S(2)}, u32[]{:S(2)}) %all-to-all-start.1) | async-done | bytes 786464 | tf_op jit(solution)/shard_map/all_to_all | solution.py:231
  198.0 2.7 maximum_add_fusion.1
  203.9 26.4 %shard_map.61 = f32[2,9,128,128]{3,2,1,0:T(8,128)} custom-call(s32[4]{0:T(128)} %get-tuple-element.97.ctl_ref, f32[2,6,128]{2,1,0:T(8,128)} %pad_maximum_fusion.9.tgt_ref, f32[6,512,128]{2,1,0:T(8,128)} %pad_maximum_fusion.2.src_ref, f32[512,128]{1,0:T(8,128)} %slice_bitcast_fusion.mass_ref), custom_call_target="tpu_custom_call" | custom-call | tf_op jit(solution)/shard_map/pallas_call | solution.py:141
  233.2 5.4 %all-to-all-start.2 = ((f32[128,2,6,128]{3,1,2,0:T(2,128)}), f32[128,2,6,128]{3,1,2,0:T(2,128)}, u32[]{:S(2)}, u32[]{:S(2)}) async-start(f32[128,2,6,128]{3,1,2,0:T(2,128)} %broadcast_in_dim.137), calls=%async_computation.2 | async-start | bytes 1572864 | tf_op jit(solution)/shard_map/all_to_all | solution.py:231
  242.1 1.6 multiply_reduce_fusion.1
  245.3 9.5 %all-to-all-done.2 = f32[128,2,6,128]{3,1,2,0:T(2,128)} async-done(((f32[128,2,6,128]{3,1,2,0:T(2,128)}), f32[128,2,6,128]{3,1,2,0:T(2,128)}, u32[]{:S(2)}, u32[]{:S(2)}) %all-to-all-start.2) | async-done | bytes 786464 | tf_op jit(solution)/shard_map/all_to_all | solution.py:231
  256.4 2.6 maximum_add_fusion.2
  263.6 56.8 %shard_map.62 = f32[2,9,128,128]{3,2,1,0:T(8,128)} custom-call(s32[4]{0:T(128)} %get-tuple-element.96.ctl_ref, f32[2,6,128]{2,1,0:T(8,128)} %pad_maximum_fusion.11.tgt_ref, f32[6,512,128]{2,1,0:T(8,128)} %pad_maximum_fusion.3.src_ref, f32[512,128]{1,0:T(8,128)} %slice_bitcast_fusion.mass_ref), custom_call_target="tpu_custom_call" | custom-call | tf_op jit(solution)/shard_map/pallas_call | solution.py:141
  323.1 4.5 %all-to-all-start.3 = ((f32[128,2,6,128]{3,1,2,0:T(2,128)}), f32[128,2,6,128]{3,1,2,0:T(2,128)S(1)}, u32[]{:S(2)}, u32[]{:S(2)}) async-start(f32[128,2,6,128]{3,1,2,0:T(2,128)} %broadcast_in_dim.138), calls=%async_computation.3 | async-start | bytes 1572864 | tf_op jit(solution)/shard_map/all_to_all | solution.py:231
  329.3 14.7 %all-to-all-done.3 = f32[128,2,6,128]{3,1,2,0:T(2,128)S(1)} async-done(((f32[128,2,6,128]{3,1,2,0:T(2,128)}), f32[128,2,6,128]{3,1,2,0:T(2,128)S(1)}, u32[]{:S(2)}, u32[]{:S(2)}) %all-to-all-start.3) | async-done | bytes 786464 | tf_op jit(solution)/shard_map/all_to_all | solution.py:231
  (146 shorter events, 46.4 us)
Async XLA Ops:
  7.2 53.8 %all-gather.2.cloned.1.call-start = ((), (), s32[]{:S(2)}) async-start(), calls=%async_computation.4 | async-start | bytes 3514368 | tf_op jit(solution)/shard_map/all_gather | solution.py:161
  64.2 3.5 copy-start
  69.6 2.8 copy-start.7
  69.7 2.8 copy-start.8
  102.9 23.8 %all-to-all-start = ((f32[128,2,6,128]{3,1,2,0:T(2,128)}), f32[128,2,6,128]{3,1,2,0:T(2,128)}, u32[]{:S(2)}, u32[]{:S(2)}) async-start(f32[128,2,6,128]{3,1,2,0:T(2,128)} %broadcast_in_dim.133), calls=%async_computation | async-start | bytes 1572864 | tf_op jit(solution)/shard_map/all_to_all | solution.py:231
  126.7 1.5 copy-start.11
  126.7 1.6 copy-start.12
  131.8 1.1 copy-start.1
  131.8 1.6 copy-start.3
  173.7 11.1 %copy-start.6 = (f32[6,512,128]{2,1,0:T(8,128)S(1)}, f32[6,512,128]{2,1,0:T(8,128)}, u32[]{:S(2)}) copy-start(f32[6,512,128]{2,1,0:T(8,128)} %pad_maximum_fusion.1.src_ref) | copy-start | bytes 4718596
  176.6 21.1 %all-to-all-start.1 = ((f32[128,2,6,128]{3,1,2,0:T(2,128)}), f32[128,2,6,128]{3,1,2,0:T(2,128)S(1)}, u32[]{:S(2)}, u32[]{:S(2)}) async-start(f32[128,2,6,128]{3,1,2,0:T(2,128)} %broadcast_in_dim.136), calls=%async_computation.1 | async-start | bytes 1572864 | tf_op jit(solution)/shard_map/all_to_all | solution.py:231
  186.0 12.0 %copy-start.13 = (f32[3,512,128]{2,1,0:T(8,128)S(1)}, f32[3,512,128]{2,1,0:T(8,128)}, u32[]{:S(2)}) copy-start(f32[3,512,128]{2,1,0:T(8,128)} %get-tuple-element.56) | copy-start | bytes 2359300
  198.0 2.8 copy-start.2
  198.0 2.8 copy-start.4
  233.2 21.6 %all-to-all-start.2 = ((f32[128,2,6,128]{3,1,2,0:T(2,128)}), f32[128,2,6,128]{3,1,2,0:T(2,128)}, u32[]{:S(2)}, u32[]{:S(2)}) async-start(f32[128,2,6,128]{3,1,2,0:T(2,128)} %broadcast_in_dim.137), calls=%async_computation.2 | async-start | bytes 1572864 | tf_op jit(solution)/shard_map/all_to_all | solution.py:231
  242.1 1.9 copy-start.5
  254.8 1.5 copy-start.14
  254.8 1.6 copy-start.15
  260.0 1.1 copy-start.9
  260.0 1.6 copy-start.10
  323.1 21.0 %all-to-all-start.3 = ((f32[128,2,6,128]{3,1,2,0:T(2,128)}), f32[128,2,6,128]{3,1,2,0:T(2,128)S(1)}, u32[]{:S(2)}, u32[]{:S(2)}) async-start(f32[128,2,6,128]{3,1,2,0:T(2,128)} %broadcast_in_dim.138), calls=%async_computation.3 | async-start | bytes 1572864 | tf_op jit(solution)/shard_map/all_to_all | solution.py:231
  327.6 16.7 %slice-start = ((f32[4,512,256]{2,1,0:T(8,128)}), f32[1,512,256]{2,1,0:T(8,128)S(1)}, s32[]{:S(2)}) async-start(f32[4,512,256]{2,1,0:T(8,128)} %fusion), calls=%async_computation.5 | async-start | bytes 1048576 | tf_op jit(solution)/shard_map/slice | solution.py:218
Sparse Core Ops, SparseCore 0:
  10.1 50.7 all-gather.1

commit v13 on v12

--- a/solution.py
+++ b/solution.py
@@ -228,12 +228,12 @@
         )
         partial = kernel_forces(ranges, targets, predicted, mass)
         sent = jnp.broadcast_to(partial[None], (devices,) + partial.shape)
-        got = lax.all_to_all(sent, every, 0, 0, tiled=True).reshape(2 * devices, 6, BLK)
+        got = lax.all_to_all(sent, every, 0, 0, tiled=True)
         later, _ = lax.optimization_barrier((predicted, partial))
         if step_index == STEPS - 1:
             break
         mutual = jnp.einsum(
-            "bu,ucl->cbl", onehot, got,
+            "bup,upcl->cbl", onehot.reshape(block_total, devices, 2), got,
             precision=lax.Precision.HIGHEST, preferred_element_type=jnp.float32,
         )
         fresh = mutual + star_terms(later)
@@ -247,7 +247,9 @@
     offset = (lax.axis_index("ja") * lax.axis_size("ha") + lax.axis_index("ha")) * local_blocks
     own = lambda x: lax.dynamic_slice_in_dim(x, offset, local_blocks, axis=1)
     mutual = jnp.einsum(
-        "bu,ucl->cbl", lax.dynamic_slice_in_dim(onehot, offset, local_blocks, axis=0), got,
+        "bup,upcl->cbl",
+        lax.dynamic_slice_in_dim(onehot, offset, local_blocks, axis=0).reshape(local_blocks, devices, 2),
+        got,
         precision=lax.Precision.HIGHEST, preferred_element_type=jnp.float32,
     )
     own_phase = own(phase)

time: 356 us -> 365 us (1.025)
  waiting for transfers between devices: 76.9 us -> 65.1 us
  local copies, waits for them, and re-layouts: 27.3 us -> 37.5 us
  Pallas kernels: 148 us -> 154 us
  starting transfers between devices: 22.2 us -> 27.7 us
    all_to_all x4, waiting for transfers between devices: 42.2 us -> 30.4 us  [shards(): got = lax.all_to_all(sent, every, 0, 0, tiled=True)]
    another operation x1 -> x7, local copies, waits for them, and re-layouts: 0.01 us -> 9.68 us  [the longest x6 9.68 us: shards(): onehot.reshape(block_total, devices, 2)]
    pallas_call x4, Pallas kernels: 148 us -> 154 us  [kernel_forces(): pl.pallas_call(_force_kernel, out_shape=jax.ShapeDtypeStruct((2, 9, targe...]
    all_to_all x4, starting transfers between devices: 22.2 us -> 27.6 us  [shards(): got = lax.all_to_all(sent, every, 0, 0, tiled=True)]
  transfers between devices with their start and end apart: 5 -> 5, of which waited for: 5 -> 5; matrix products, arithmetic and copies ran while one was open for 8% -> 11% of each run, Pallas kernels for 0% -> 0%
where the time goes in v13:
time: 365 us; the launch traced here: 364 us
  Pallas kernels  154 us (42%)
  waiting for transfers between devices  65.1 us (18%)
  other arithmetic  40.2 us (11%)
  local copies, waits for them, and re-layouts  37.5 us (10%)
  between operations  29.2 us (8%)
  starting transfers between devices  27.7 us (8%)
  matrix products  10.1 us (3%)
    pallas_call x4, Pallas kernels, kernel_forces(): pl.pallas_call(_force_kernel, out_shape=jax.ShapeDtypeStruct((2, 9, targe...  154 us
    all_gather x1, waiting for transfers between devices, shards(): full = lax.all_gather(local, plane, axis=1, tiled=True)  34.7 us
    all_to_all x4, waiting for transfers between devices, shards(): got = lax.all_to_all(sent, every, 0, 0, tiled=True)  30.4 us
    all_to_all x4, starting transfers between devices, shards(): got = lax.all_to_all(sent, every, 0, 0, tiled=True)  27.6 us
    another operation x6, local copies, waits for them, and re-layouts, shards(): onehot.reshape(block_total, devices, 2)  9.68 us
    dot_general x3, matrix products, shards(): jnp.einsum('bup,upcl->cbl', onehot.reshape(block_total, devices, 2), got,...  9.64 us
  transfers between devices with their start and end apart: 5, of which 5 were waited for; matrix products, arithmetic and copies ran while one was open for 11% of the time, Pallas kernels for 0%

profile of v13, /device:TPU:1, one launch (start us, length us, event | category | flops | bytes accessed | tf_op | source)
XLA Modules:
  0.0 363.9 jit_solution(1783123392797409417)
XLA Ops:
  11.9 4.7 %gather_fusion.3 = s32[512]{0:T(512)S(1)} fusion(s32[4,128]{1,0:T(4,128)S(1)} %select_reduce_fusion, s32[512]{0:T(512)S(1)} %get-tuple-element.116), kind=kCustom, calls=%fused_computation.3.clone | custom fusion | bytes 8192 | tf_op jit(solution)/shard_map/jit(take_along_axis)/gather | solution.py:188
  16.5 4.7 %gather_fusion.2 = s32[512]{0:T(512)S(1)} fusion(s32[4,128]{1,0:T(4,128)S(1)} %select_reduce_fusion, s32[512]{0:T(512)S(1)} %get-tuple-element.115), kind=kCustom, calls=%fused_computation.1.clone | custom fusion | bytes 8192 | tf_op jit(solution)/shard_map/jit(take_along_axis)/gather | solution.py:187
  26.2 34.7 %all-gather.2.cloned.1.call-done = f32[13,512,128]{2,1,0:T(8,128)} async-done(((f32[13,16,128]{2,1,0:T(8,128)}), f32[13,512,128]{2,1,0:T(8,128)}) %all-gather.2.cloned.1.call-update) | async-done | bytes 3407888 | tf_op jit(solution)/shard_map/all_gather | solution.py:161
  64.2 3.5 multiply_add_fusion.9
  69.7 2.8 pad_maximum_fusion.src_ref
  73.7 26.4 %shard_map.59 = f32[2,9,128,128]{3,2,1,0:T(8,128)} custom-call(s32[4]{0:T(128)} %get-tuple-element.103.ctl_ref, f32[2,6,128]{2,1,0:T(8,128)} %pad_maximum_fusion.5.tgt_ref, f32[6,512,128]{2,1,0:T(8,128)} %pad_maximum_fusion.src_ref, f32[512,128]{1,0:T(8,128)} %slice_bitcast_fusion.mass_ref), custom_call_target="tpu_custom_call" | custom-call | tf_op jit(solution)/shard_map/pallas_call | solution.py:141
  103.0 7.7 %all-to-all-start = ((f32[128,2,6,128]{3,1,2,0:T(2,128)}), f32[128,2,6,128]{3,1,2,0:T(2,128)}, u32[]{:S(2)}, u32[]{:S(2)}) async-start(f32[128,2,6,128]{3,1,2,0:T(2,128)} %broadcast_in_dim.133), calls=%async_computation | async-start | bytes 1572864 | tf_op jit(solution)/shard_map/all_to_all | solution.py:231
  110.6 3.0 fusion.71
  117.2 2.1 reshape_squeeze.9
  119.3 2.1 copy.81
  123.7 2.7 slice_multiply_fusion.5
  126.8 3.3 maximum_add_fusion
  134.5 44.5 %shard_map.60 = f32[2,9,128,128]{3,2,1,0:T(8,128)} custom-call(s32[4]{0:T(128)} %get-tuple-element.102.ctl_ref, f32[2,6,128]{2,1,0:T(8,128)} %pad_maximum_fusion.7.tgt_ref, f32[6,512,128]{2,1,0:T(8,128)} %pad_maximum_fusion.1.src_ref, f32[512,128]{1,0:T(8,128)} %slice_bitcast_fusion.mass_ref), custom_call_target="tpu_custom_call" | custom-call | tf_op jit(solution)/shard_map/pallas_call | solution.py:141
  181.8 10.1 %all-to-all-start.1 = ((f32[128,2,6,128]{3,1,2,0:T(2,128)}), f32[128,2,6,128]{3,1,2,0:T(2,128)}, u32[]{:S(2)}, u32[]{:S(2)}) async-start(f32[128,2,6,128]{3,1,2,0:T(2,128)} %broadcast_in_dim.136), calls=%async_computation.1 | async-start | bytes 1572864 | tf_op jit(solution)/shard_map/all_to_all | solution.py:231
  197.0 11.0 %all-to-all-done.1 = f32[128,2,6,128]{3,1,2,0:T(2,128)} async-done(((f32[128,2,6,128]{3,1,2,0:T(2,128)}), f32[128,2,6,128]{3,1,2,0:T(2,128)}, u32[]{:S(2)}, u32[]{:S(2)}) %all-to-all-start.1) | async-done | bytes 786464 | tf_op jit(solution)/shard_map/all_to_all | solution.py:231
  208.0 3.0 maximum_add_fusion.1
  214.2 26.4 %shard_map.61 = f32[2,9,128,128]{3,2,1,0:T(8,128)} custom-call(s32[4]{0:T(128)} %get-tuple-element.101.ctl_ref, f32[2,6,128]{2,1,0:T(8,128)} %pad_maximum_fusion.9.tgt_ref, f32[6,512,128]{2,1,0:T(8,128)} %pad_maximum_fusion.2.src_ref, f32[512,128]{1,0:T(8,128)} %slice_bitcast_fusion.mass_ref), custom_call_target="tpu_custom_call" | custom-call | tf_op jit(solution)/shard_map/pallas_call | solution.py:141
  243.4 5.4 %all-to-all-start.2 = ((f32[128,2,6,128]{3,1,2,0:T(2,128)}), f32[128,2,6,128]{3,1,2,0:T(2,128)}, u32[]{:S(2)}, u32[]{:S(2)}) async-start(f32[128,2,6,128]{3,1,2,0:T(2,128)} %broadcast_in_dim.137), calls=%async_computation.2 | async-start | bytes 1572864 | tf_op jit(solution)/shard_map/all_to_all | solution.py:231
  251.1 2.1 reshape_squeeze.11
  259.7 5.4 %all-to-all-done.2 = f32[128,2,6,128]{3,1,2,0:T(2,128)} async-done(((f32[128,2,6,128]{3,1,2,0:T(2,128)}), f32[128,2,6,128]{3,1,2,0:T(2,128)}, u32[]{:S(2)}, u32[]{:S(2)}) %all-to-all-start.2) | async-done | bytes 786464 | tf_op jit(solution)/shard_map/all_to_all | solution.py:231
  265.1 3.3 maximum_add_fusion.2
  272.9 56.8 %shard_map.62 = f32[2,9,128,128]{3,2,1,0:T(8,128)} custom-call(s32[4]{0:T(128)} %get-tuple-element.100.ctl_ref, f32[2,6,128]{2,1,0:T(8,128)} %pad_maximum_fusion.11.tgt_ref, f32[6,512,128]{2,1,0:T(8,128)} %pad_maximum_fusion.3.src_ref, f32[512,128]{1,0:T(8,128)} %slice_bitcast_fusion.mass_ref), custom_call_target="tpu_custom_call" | custom-call | tf_op jit(solution)/shard_map/pallas_call | solution.py:141
  332.5 4.5 %all-to-all-start.3 = ((f32[128,2,6,128]{3,1,2,0:T(2,128)}), f32[128,2,6,128]{3,1,2,0:T(2,128)S(1)}, u32[]{:S(2)}, u32[]{:S(2)}) async-start(f32[128,2,6,128]{3,1,2,0:T(2,128)} %broadcast_in_dim.138), calls=%async_computation.3 | async-start | bytes 1572864 | tf_op jit(solution)/shard_map/all_to_all | solution.py:231
  339.8 13.6 %all-to-all-done.3 = f32[128,2,6,128]{3,1,2,0:T(2,128)S(1)} async-done(((f32[128,2,6,128]{3,1,2,0:T(2,128)}), f32[128,2,6,128]{3,1,2,0:T(2,128)S(1)}, u32[]{:S(2)}, u32[]{:S(2)}) %all-to-all-start.3) | async-done | bytes 786464 | tf_op jit(solution)/shard_map/all_to_all | solution.py:231
  (143 shorter events, 50.9 us)
Async XLA Ops:
  7.2 53.8 %all-gather.2.cloned.1.call-start = ((), (), s32[]{:S(2)}) async-start(), calls=%async_computation.4 | async-start | bytes 3514368 | tf_op jit(solution)/shard_map/all_gather | solution.py:161
  64.2 3.5 copy-start
  69.7 2.8 copy-start.8
  69.7 2.8 copy-start.9
  103.0 23.8 %all-to-all-start = ((f32[128,2,6,128]{3,1,2,0:T(2,128)}), f32[128,2,6,128]{3,1,2,0:T(2,128)}, u32[]{:S(2)}, u32[]{:S(2)}) async-start(f32[128,2,6,128]{3,1,2,0:T(2,128)} %broadcast_in_dim.133), calls=%async_computation | async-start | bytes 1572864 | tf_op jit(solution)/shard_map/all_to_all | solution.py:231
  110.6 3.1 copy-start.5
  131.0 1.2 copy-start.1
  131.0 1.6 copy-start.3
  179.0 15.2 %copy-start.12 = (f32[1,512,256]{1,2,0:T(8,128)S(1)}, f32[1,512,256]{1,2,0:T(8,128)}, u32[]{:S(2)}) copy-start(f32[1,512,256]{1,2,0:T(8,128)} %get-tuple-element.55) | copy-start | bytes 1572868
  181.8 14.8 %copy-start.7 = (f32[6,512,128]{2,1,0:T(8,128)S(1)}, f32[6,512,128]{2,1,0:T(8,128)}, u32[]{:S(2)}) copy-start(f32[6,512,128]{2,1,0:T(8,128)} %pad_maximum_fusion.1.src_ref) | copy-start | bytes 4718596
  181.8 26.2 %all-to-all-start.1 = ((f32[128,2,6,128]{3,1,2,0:T(2,128)}), f32[128,2,6,128]{3,1,2,0:T(2,128)}, u32[]{:S(2)}, u32[]{:S(2)}) async-start(f32[128,2,6,128]{3,1,2,0:T(2,128)} %broadcast_in_dim.136), calls=%async_computation.1 | async-start | bytes 1572864 | tf_op jit(solution)/shard_map/all_to_all | solution.py:231
  208.0 3.0 copy-start.2
  208.0 3.0 copy-start.4
  243.4 21.6 %all-to-all-start.2 = ((f32[128,2,6,128]{3,1,2,0:T(2,128)}), f32[128,2,6,128]{3,1,2,0:T(2,128)}, u32[]{:S(2)}, u32[]{:S(2)}) async-start(f32[128,2,6,128]{3,1,2,0:T(2,128)} %broadcast_in_dim.137), calls=%async_computation.2 | async-start | bytes 1572864 | tf_op jit(solution)/shard_map/all_to_all | solution.py:231
  256.5 1.9 copy-start.6
  269.4 1.2 copy-start.10
  269.4 1.6 copy-start.11
  332.5 21.0 %all-to-all-start.3 = ((f32[128,2,6,128]{3,1,2,0:T(2,128)}), f32[128,2,6,128]{3,1,2,0:T(2,128)S(1)}, u32[]{:S(2)}, u32[]{:S(2)}) async-start(f32[128,2,6,128]{3,1,2,0:T(2,128)} %broadcast_in_dim.138), calls=%async_computation.3 | async-start | bytes 1572864 | tf_op jit(solution)/shard_map/all_to_all | solution.py:231
Sparse Core Ops, SparseCore 0:
  10.1 50.7 all-gather.1

commit v14 on v13

--- a/solution.py
+++ b/solution.py
@@ -134,7 +134,13 @@
                 out_ref[part, k, pl.ds(t, 1), :] = jnp.sum(acc[k], axis=0, keepdims=True)
             return carry
 
-        lax.fori_loop(0, targets, per_target, 0)
+        @pl.when(hi > lo)
+        def _(per_target=per_target):
+            lax.fori_loop(0, targets, per_target, 0)
+
+        @pl.when(hi <= lo)
+        def _(part=part):
+            out_ref[part] = jnp.zeros(out_ref.shape[1:], out_ref.dtype)
 
 
 def kernel_forces(ranges, targets, field, masses):

time: 365 us -> 359 us (0.984)
  Pallas kernels: 154 us -> 145 us
    pallas_call x4, Pallas kernels: 154 us -> 145 us  [kernel_forces(): pl.pallas_call(_force_kernel, out_shape=jax.ShapeDtypeStruct((2, 9, targe...]
where the time goes in v14:
time: 359 us; the launch traced here: 358 us
  Pallas kernels  145 us (40%)
  waiting for transfers between devices  65 us (18%)
  other arithmetic  40.2 us (11%)
  local copies, waits for them, and re-layouts  37.5 us (10%)
  starting transfers between devices  30.8 us (9%)
  between operations  29.2 us (8%)
  matrix products  10.1 us (3%)
    pallas_call x4, Pallas kernels, kernel_forces(): pl.pallas_call(_force_kernel, out_shape=jax.ShapeDtypeStruct((2, 9, targe...  145 us
    all_gather x1, waiting for transfers between devices, shards(): full = lax.all_gather(local, plane, axis=1, tiled=True)  34.7 us
    all_to_all x4, starting transfers between devices, shards(): got = lax.all_to_all(sent, every, 0, 0, tiled=True)  30.8 us
    all_to_all x4, waiting for transfers between devices, shards(): got = lax.all_to_all(sent, every, 0, 0, tiled=True)  30.2 us
    another operation x6, local copies, waits for them, and re-layouts, shards(): onehot.reshape(block_total, devices, 2)  9.68 us
    dot_general x3, matrix products, shards(): jnp.einsum('bup,upcl->cbl', onehot.reshape(block_total, devices, 2), got,...  9.65 us
  transfers between devices with their start and end apart: 5, of which 5 were waited for; matrix products, arithmetic and copies ran while one was open for 11% of the time, Pallas kernels for 0%

profile of v14, /device:TPU:1, one launch (start us, length us, event | category | flops | bytes accessed | tf_op | source)
XLA Modules:
  0.0 357.7 jit_solution(8001338486561521255)
XLA Ops:
  11.9 4.7 %gather_fusion.3 = s32[512]{0:T(512)S(1)} fusion(s32[4,128]{1,0:T(4,128)S(1)} %select_reduce_fusion, s32[512]{0:T(512)S(1)} %get-tuple-element.116), kind=kCustom, calls=%fused_computation.3.clone | custom fusion | bytes 8192 | tf_op jit(solution)/shard_map/jit(take_along_axis)/gather | solution.py:194
  16.5 4.7 %gather_fusion.2 = s32[512]{0:T(512)S(1)} fusion(s32[4,128]{1,0:T(4,128)S(1)} %select_reduce_fusion, s32[512]{0:T(512)S(1)} %get-tuple-element.115), kind=kCustom, calls=%fused_computation.1.clone | custom fusion | bytes 8192 | tf_op jit(solution)/shard_map/jit(take_along_axis)/gather | solution.py:193
  26.2 34.7 %all-gather.2.cloned.1.call-done = f32[13,512,128]{2,1,0:T(8,128)} async-done(((f32[13,16,128]{2,1,0:T(8,128)}), f32[13,512,128]{2,1,0:T(8,128)}) %all-gather.2.cloned.1.call-update) | async-done | bytes 3407888 | tf_op jit(solution)/shard_map/all_gather | solution.py:167
  64.2 3.5 multiply_add_fusion.9
  69.7 2.8 pad_maximum_fusion.src_ref
  73.7 23.4 %shard_map.59 = f32[2,9,128,128]{3,2,1,0:T(8,128)} custom-call(s32[4]{0:T(128)} %get-tuple-element.103.ctl_ref, f32[2,6,128]{2,1,0:T(8,128)} %pad_maximum_fusion.5.tgt_ref, f32[6,512,128]{2,1,0:T(8,128)} %pad_maximum_fusion.src_ref, f32[512,128]{1,0:T(8,128)} %slice_bitcast_fusion.mass_ref), custom_call_target="tpu_custom_call" | custom-call | tf_op jit(solution)/shard_map/pallas_call | solution.py:147
  99.9 10.3 %all-to-all-start = ((f32[128,2,6,128]{3,1,2,0:T(2,128)}), f32[128,2,6,128]{3,1,2,0:T(2,128)}, u32[]{:S(2)}, u32[]{:S(2)}) async-start(f32[128,2,6,128]{3,1,2,0:T(2,128)} %broadcast_in_dim.133), calls=%async_computation | async-start | bytes 1572864 | tf_op jit(solution)/shard_map/all_to_all | solution.py:237
  110.2 3.0 fusion.71
  116.7 2.1 reshape_squeeze.9
  118.8 2.1 copy.81
  123.3 2.7 slice_multiply_fusion.5
  126.3 3.3 maximum_add_fusion
  134.1 44.3 %shard_map.60 = f32[2,9,128,128]{3,2,1,0:T(8,128)} custom-call(s32[4]{0:T(128)} %get-tuple-element.102.ctl_ref, f32[2,6,128]{2,1,0:T(8,128)} %pad_maximum_fusion.7.tgt_ref, f32[6,512,128]{2,1,0:T(8,128)} %pad_maximum_fusion.1.src_ref, f32[512,128]{1,0:T(8,128)} %slice_bitcast_fusion.mass_ref), custom_call_target="tpu_custom_call" | custom-call | tf_op jit(solution)/shard_map/pallas_call | solution.py:147
  181.3 9.6 %all-to-all-start.1 = ((f32[128,2,6,128]{3,1,2,0:T(2,128)}), f32[128,2,6,128]{3,1,2,0:T(2,128)}, u32[]{:S(2)}, u32[]{:S(2)}) async-start(f32[128,2,6,128]{3,1,2,0:T(2,128)} %broadcast_in_dim.136), calls=%async_computation.1 | async-start | bytes 1572864 | tf_op jit(solution)/shard_map/all_to_all | solution.py:237
  195.9 11.0 %all-to-all-done.1 = f32[128,2,6,128]{3,1,2,0:T(2,128)} async-done(((f32[128,2,6,128]{3,1,2,0:T(2,128)}), f32[128,2,6,128]{3,1,2,0:T(2,128)}, u32[]{:S(2)}, u32[]{:S(2)}) %all-to-all-start.1) | async-done | bytes 786464 | tf_op jit(solution)/shard_map/all_to_all | solution.py:237
  207.0 3.0 maximum_add_fusion.1
  213.1 23.4 %shard_map.61 = f32[2,9,128,128]{3,2,1,0:T(8,128)} custom-call(s32[4]{0:T(128)} %get-tuple-element.101.ctl_ref, f32[2,6,128]{2,1,0:T(8,128)} %pad_maximum_fusion.9.tgt_ref, f32[6,512,128]{2,1,0:T(8,128)} %pad_maximum_fusion.2.src_ref, f32[512,128]{1,0:T(8,128)} %slice_bitcast_fusion.mass_ref), custom_call_target="tpu_custom_call" | custom-call | tf_op jit(solution)/shard_map/pallas_call | solution.py:147
  239.3 6.4 %all-to-all-start.2 = ((f32[128,2,6,128]{3,1,2,0:T(2,128)}), f32[128,2,6,128]{3,1,2,0:T(2,128)}, u32[]{:S(2)}, u32[]{:S(2)}) async-start(f32[128,2,6,128]{3,1,2,0:T(2,128)} %broadcast_in_dim.137), calls=%async_computation.2 | async-start | bytes 1572864 | tf_op jit(solution)/shard_map/all_to_all | solution.py:237
  248.1 2.1 reshape_squeeze.11
  256.6 5.3 %all-to-all-done.2 = f32[128,2,6,128]{3,1,2,0:T(2,128)} async-done(((f32[128,2,6,128]{3,1,2,0:T(2,128)}), f32[128,2,6,128]{3,1,2,0:T(2,128)}, u32[]{:S(2)}, u32[]{:S(2)}) %all-to-all-start.2) | async-done | bytes 786464 | tf_op jit(solution)/shard_map/all_to_all | solution.py:237
  261.9 3.3 maximum_add_fusion.2
  269.7 53.7 %shard_map.62 = f32[2,9,128,128]{3,2,1,0:T(8,128)} custom-call(s32[4]{0:T(128)} %get-tuple-element.100.ctl_ref, f32[2,6,128]{2,1,0:T(8,128)} %pad_maximum_fusion.11.tgt_ref, f32[6,512,128]{2,1,0:T(8,128)} %pad_maximum_fusion.3.src_ref, f32[512,128]{1,0:T(8,128)} %slice_bitcast_fusion.mass_ref), custom_call_target="tpu_custom_call" | custom-call | tf_op jit(solution)/shard_map/pallas_call | solution.py:147
  326.3 4.5 %all-to-all-start.3 = ((f32[128,2,6,128]{3,1,2,0:T(2,128)}), f32[128,2,6,128]{3,1,2,0:T(2,128)S(1)}, u32[]{:S(2)}, u32[]{:S(2)}) async-start(f32[128,2,6,128]{3,1,2,0:T(2,128)} %broadcast_in_dim.138), calls=%async_computation.3 | async-start | bytes 1572864 | tf_op jit(solution)/shard_map/all_to_all | solution.py:237
  333.6 13.6 %all-to-all-done.3 = f32[128,2,6,128]{3,1,2,0:T(2,128)S(1)} async-done(((f32[128,2,6,128]{3,1,2,0:T(2,128)}), f32[128,2,6,128]{3,1,2,0:T(2,128)S(1)}, u32[]{:S(2)}, u32[]{:S(2)}) %all-to-all-start.3) | async-done | bytes 786464 | tf_op jit(solution)/shard_map/all_to_all | solution.py:237
  (143 shorter events, 50.9 us)
Async XLA Ops:
  7.2 53.8 %all-gather.2.cloned.1.call-start = ((), (), s32[]{:S(2)}) async-start(), calls=%async_computation.4 | async-start | bytes 3514368 | tf_op jit(solution)/shard_map/all_gather | solution.py:167
  64.2 3.5 copy-start
  69.7 2.8 copy-start.8
  69.7 2.8 copy-start.9
  99.9 26.4 %all-to-all-start = ((f32[128,2,6,128]{3,1,2,0:T(2,128)}), f32[128,2,6,128]{3,1,2,0:T(2,128)}, u32[]{:S(2)}, u32[]{:S(2)}) async-start(f32[128,2,6,128]{3,1,2,0:T(2,128)} %broadcast_in_dim.133), calls=%async_computation | async-start | bytes 1572864 | tf_op jit(solution)/shard_map/all_to_all | solution.py:237
  110.2 3.1 copy-start.5
  130.5 1.2 copy-start.1
  130.5 1.6 copy-start.3
  178.4 14.7 %copy-start.12 = (f32[1,512,256]{1,2,0:T(8,128)S(1)}, f32[1,512,256]{1,2,0:T(8,128)}, u32[]{:S(2)}) copy-start(f32[1,512,256]{1,2,0:T(8,128)} %get-tuple-element.55) | copy-start | bytes 1572868
  181.3 14.3 %copy-start.7 = (f32[6,512,128]{2,1,0:T(8,128)S(1)}, f32[6,512,128]{2,1,0:T(8,128)}, u32[]{:S(2)}) copy-start(f32[6,512,128]{2,1,0:T(8,128)} %pad_maximum_fusion.1.src_ref) | copy-start | bytes 4718596
  181.3 25.7 %all-to-all-start.1 = ((f32[128,2,6,128]{3,1,2,0:T(2,128)}), f32[128,2,6,128]{3,1,2,0:T(2,128)}, u32[]{:S(2)}, u32[]{:S(2)}) async-start(f32[128,2,6,128]{3,1,2,0:T(2,128)} %broadcast_in_dim.136), calls=%async_computation.1 | async-start | bytes 1572864 | tf_op jit(solution)/shard_map/all_to_all | solution.py:237
  207.0 3.0 copy-start.2
  207.0 3.0 copy-start.4
  239.3 22.6 %all-to-all-start.2 = ((f32[128,2,6,128]{3,1,2,0:T(2,128)}), f32[128,2,6,128]{3,1,2,0:T(2,128)}, u32[]{:S(2)}, u32[]{:S(2)}) async-start(f32[128,2,6,128]{3,1,2,0:T(2,128)} %broadcast_in_dim.137), calls=%async_computation.2 | async-start | bytes 1572864 | tf_op jit(solution)/shard_map/all_to_all | solution.py:237
  253.5 1.9 copy-start.6
  266.2 1.2 copy-start.10
  266.2 1.6 copy-start.11
  326.3 21.0 %all-to-all-start.3 = ((f32[128,2,6,128]{3,1,2,0:T(2,128)}), f32[128,2,6,128]{3,1,2,0:T(2,128)S(1)}, u32[]{:S(2)}, u32[]{:S(2)}) async-start(f32[128,2,6,128]{3,1,2,0:T(2,128)} %broadcast_in_dim.138), calls=%async_computation.3 | async-start | bytes 1572864 | tf_op jit(solution)/shard_map/all_to_all | solution.py:237
Sparse Core Ops, SparseCore 0:
  10.1 50.7 all-gather.1

commit v15 on v13

--- a/solution.py
+++ b/solution.py
@@ -219,7 +219,7 @@
         active_flags = active_all[step_index]
         elapsed_blk = now_time - last_blk
         elapsed = elapsed_blk[None, :, None]
-        predicted = predict(phase, deriv, elapsed)
+        predicted = lax.optimization_barrier(predict(phase, deriv, elapsed))
         targets = jnp.stack(
             [
                 lax.dynamic_index_in_dim(predicted, id_a, 1, keepdims=False),

time: 365 us -> 362 us (level)
  other arithmetic: 40.2 us -> 32.8 us
    concatenate x4, other arithmetic: 6.53 us -> 1.57 us  [predict(): return jnp.concatenate([pos_next, vel_next], axis=0)]
where the time goes in v15:
time: 362 us; the launch traced here: 361 us
  Pallas kernels  154 us (43%)
  waiting for transfers between devices  66.4 us (18%)
  local copies, waits for them, and re-layouts  40.1 us (11%)
  other arithmetic  32.8 us (9%)
  between operations  29.5 us (8%)
  starting transfers between devices  27.6 us (8%)
  matrix products  10.3 us (3%)
    pallas_call x4, Pallas kernels, kernel_forces(): pl.pallas_call(_force_kernel, out_shape=jax.ShapeDtypeStruct((2, 9, targe...  154 us
    all_gather x1, waiting for transfers between devices, shards(): full = lax.all_gather(local, plane, axis=1, tiled=True)  34.7 us
    all_to_all x4, waiting for transfers between devices, shards(): got = lax.all_to_all(sent, every, 0, 0, tiled=True)  31.7 us
    all_to_all x4, starting transfers between devices, shards(): got = lax.all_to_all(sent, every, 0, 0, tiled=True)  27.6 us
    dot_general x3, matrix products, shards(): jnp.einsum('bup,upcl->cbl', onehot.reshape(block_total, devices, 2), got,...  9.76 us
    another operation x6, local copies, waits for them, and re-layouts, shards(): onehot.reshape(block_total, devices, 2)  9.71 us
  transfers between devices with their start and end apart: 5, of which 5 were waited for; matrix products, arithmetic and copies ran while one was open for 11% of the time, Pallas kernels for 0%

profile of v15, /device:TPU:1, one launch (start us, length us, event | category | flops | bytes accessed | tf_op | source)
XLA Modules:
  0.0 360.9 jit_solution(677073206126701085)
XLA Ops:
  11.9 4.7 %gather_fusion.3 = s32[512]{0:T(512)S(1)} fusion(s32[4,128]{1,0:T(4,128)S(1)} %select_reduce_fusion, s32[512]{0:T(512)S(1)} %get-tuple-element.116), kind=kCustom, calls=%fused_computation.3.clone | custom fusion | bytes 8192 | tf_op jit(solution)/shard_map/jit(take_along_axis)/gather | solution.py:188
  16.5 4.7 %gather_fusion.2 = s32[512]{0:T(512)S(1)} fusion(s32[4,128]{1,0:T(4,128)S(1)} %select_reduce_fusion, s32[512]{0:T(512)S(1)} %get-tuple-element.115), kind=kCustom, calls=%fused_computation.1.clone | custom fusion | bytes 8192 | tf_op jit(solution)/shard_map/jit(take_along_axis)/gather | solution.py:187
  26.2 34.7 %all-gather.2.cloned.1.call-done = f32[13,512,128]{2,1,0:T(8,128)} async-done(((f32[13,16,128]{2,1,0:T(8,128)}), f32[13,512,128]{2,1,0:T(8,128)}) %all-gather.2.cloned.1.call-update) | async-done | bytes 3407888 | tf_op jit(solution)/shard_map/all_gather | solution.py:161
  64.2 2.3 multiply_add_fusion.9
  72.4 26.4 %shard_map.59 = f32[2,9,128,128]{3,2,1,0:T(8,128)} custom-call(s32[4]{0:T(128)} %get-tuple-element.103.ctl_ref, f32[2,6,128]{2,1,0:T(8,128)} %pad_maximum_fusion.5.tgt_ref, f32[6,512,128]{2,1,0:T(8,128)} %pad_maximum_fusion.src_ref, f32[512,128]{1,0:T(8,128)} %slice_bitcast_fusion.mass_ref), custom_call_target="tpu_custom_call" | custom-call | tf_op jit(solution)/shard_map/pallas_call | solution.py:141
  101.6 7.7 %all-to-all-start = ((f32[128,2,6,128]{3,1,2,0:T(2,128)}), f32[128,2,6,128]{3,1,2,0:T(2,128)}, u32[]{:S(2)}, u32[]{:S(2)}) async-start(f32[128,2,6,128]{3,1,2,0:T(2,128)} %broadcast_in_dim.133), calls=%async_computation | async-start | bytes 1572864 | tf_op jit(solution)/shard_map/all_to_all | solution.py:231
  109.3 3.0 fusion.63
  115.7 2.1 reshape_squeeze.9
  117.8 2.0 copy.81
  122.2 2.7 slice_multiply_fusion.5
  125.4 3.3 maximum_add_fusion
  132.5 44.5 %shard_map.60 = f32[2,9,128,128]{3,2,1,0:T(8,128)} custom-call(s32[4]{0:T(128)} %get-tuple-element.102.ctl_ref, f32[2,6,128]{2,1,0:T(8,128)} %pad_maximum_fusion.7.tgt_ref, f32[6,512,128]{2,1,0:T(8,128)} %copy-done.4, f32[512,128]{1,0:T(8,128)} %slice_bitcast_fusion.mass_ref), custom_call_target="tpu_custom_call" | custom-call | tf_op jit(solution)/shard_map/pallas_call | solution.py:141
  179.9 9.9 %all-to-all-start.1 = ((f32[128,2,6,128]{3,1,2,0:T(2,128)}), f32[128,2,6,128]{3,1,2,0:T(2,128)}, u32[]{:S(2)}, u32[]{:S(2)}) async-start(f32[128,2,6,128]{3,1,2,0:T(2,128)} %broadcast_in_dim.136), calls=%async_computation.1 | async-start | bytes 1572864 | tf_op jit(solution)/shard_map/all_to_all | solution.py:231
  195.4 10.5 %all-to-all-done.1 = f32[128,2,6,128]{3,1,2,0:T(2,128)} async-done(((f32[128,2,6,128]{3,1,2,0:T(2,128)}), f32[128,2,6,128]{3,1,2,0:T(2,128)}, u32[]{:S(2)}, u32[]{:S(2)}) %all-to-all-start.1) | async-done | bytes 786464 | tf_op jit(solution)/shard_map/all_to_all | solution.py:231
  205.9 3.0 maximum_add_fusion.1
  212.2 26.4 %shard_map.61 = f32[2,9,128,128]{3,2,1,0:T(8,128)} custom-call(s32[4]{0:T(128)} %get-tuple-element.101.ctl_ref, f32[2,6,128]{2,1,0:T(8,128)} %pad_maximum_fusion.9.tgt_ref, f32[6,512,128]{2,1,0:T(8,128)} %copy-done.2, f32[512,128]{1,0:T(8,128)} %slice_bitcast_fusion.mass_ref), custom_call_target="tpu_custom_call" | custom-call | tf_op jit(solution)/shard_map/pallas_call | solution.py:141
  241.4 5.5 %all-to-all-start.2 = ((f32[128,2,6,128]{3,1,2,0:T(2,128)}), f32[128,2,6,128]{3,1,2,0:T(2,128)}, u32[]{:S(2)}, u32[]{:S(2)}) async-start(f32[128,2,6,128]{3,1,2,0:T(2,128)} %broadcast_in_dim.137), calls=%async_computation.2 | async-start | bytes 1572864 | tf_op jit(solution)/shard_map/all_to_all | solution.py:231
  249.2 2.2 reshape_squeeze.11
  251.3 2.0 copy.93
  256.0 7.2 %all-to-all-done.2 = f32[128,2,6,128]{3,1,2,0:T(2,128)} async-done(((f32[128,2,6,128]{3,1,2,0:T(2,128)}), f32[128,2,6,128]{3,1,2,0:T(2,128)}, u32[]{:S(2)}, u32[]{:S(2)}) %all-to-all-start.2) | async-done | bytes 786464 | tf_op jit(solution)/shard_map/all_to_all | solution.py:231
  263.2 3.4 maximum_add_fusion.2
  270.0 56.8 %shard_map.62 = f32[2,9,128,128]{3,2,1,0:T(8,128)} custom-call(s32[4]{0:T(128)} %get-tuple-element.100.ctl_ref, f32[2,6,128]{2,1,0:T(8,128)} %pad_maximum_fusion.11.tgt_ref, f32[6,512,128]{2,1,0:T(8,128)} %copy-done.12, f32[512,128]{1,0:T(8,128)} %slice_bitcast_fusion.mass_ref), custom_call_target="tpu_custom_call" | custom-call | tf_op jit(solution)/shard_map/pallas_call | solution.py:141
  329.5 4.5 %all-to-all-start.3 = ((f32[128,2,6,128]{3,1,2,0:T(2,128)}), f32[128,2,6,128]{3,1,2,0:T(2,128)S(1)}, u32[]{:S(2)}, u32[]{:S(2)}) async-start(f32[128,2,6,128]{3,1,2,0:T(2,128)} %broadcast_in_dim.138), calls=%async_computation.3 | async-start | bytes 1572864 | tf_op jit(solution)/shard_map/all_to_all | solution.py:231
  336.9 13.6 %all-to-all-done.3 = f32[128,2,6,128]{3,1,2,0:T(2,128)S(1)} async-done(((f32[128,2,6,128]{3,1,2,0:T(2,128)}), f32[128,2,6,128]{3,1,2,0:T(2,128)S(1)}, u32[]{:S(2)}, u32[]{:S(2)}) %all-to-all-start.3) | async-done | bytes 786464 | tf_op jit(solution)/shard_map/all_to_all | solution.py:231
  (147 shorter events, 48.2 us)
Async XLA Ops:
  7.2 53.8 %all-gather.2.cloned.1.call-start = ((), (), s32[]{:S(2)}) async-start(), calls=%async_computation.4 | async-start | bytes 3514368 | tf_op jit(solution)/shard_map/all_gather | solution.py:161
  64.2 2.9 copy-start
  101.6 23.8 %all-to-all-start = ((f32[128,2,6,128]{3,1,2,0:T(2,128)}), f32[128,2,6,128]{3,1,2,0:T(2,128)}, u32[]{:S(2)}, u32[]{:S(2)}) async-start(f32[128,2,6,128]{3,1,2,0:T(2,128)} %broadcast_in_dim.133), calls=%async_computation | async-start | bytes 1572864 | tf_op jit(solution)/shard_map/all_to_all | solution.py:231
  109.3 3.1 copy-start.1
  129.6 1.2 copy-start.8
  129.6 1.6 copy-start.10
  131.4 1.2 copy-start.4
  177.0 15.4 %copy-start.14 = (f32[1,512,256]{1,2,0:T(8,128)S(1)}, f32[1,512,256]{1,2,0:T(8,128)}, u32[]{:S(2)}) copy-start(f32[1,512,256]{1,2,0:T(8,128)} %get-tuple-element.55) | copy-start | bytes 1572868
  179.8 15.2 %copy-start.5 = (f32[6,512,128]{2,1,0:T(8,128)S(1)}, f32[6,512,128]{2,1,0:T(8,128)}, u32[]{:S(2)}) copy-start(f32[6,512,128]{2,1,0:T(8,128)} %copy-done.4) | copy-start | bytes 4718596
  179.9 26.0 %all-to-all-start.1 = ((f32[128,2,6,128]{3,1,2,0:T(2,128)}), f32[128,2,6,128]{3,1,2,0:T(2,128)}, u32[]{:S(2)}, u32[]{:S(2)}) async-start(f32[128,2,6,128]{3,1,2,0:T(2,128)} %broadcast_in_dim.136), calls=%async_computation.1 | async-start | bytes 1572864 | tf_op jit(solution)/shard_map/all_to_all | solution.py:231
  205.9 3.0 copy-start.9
  205.9 3.0 copy-start.11
  209.8 1.2 copy-start.6
  211.0 1.2 copy-start.2
  241.4 13.1 %copy-start.3 = (f32[6,512,128]{2,1,0:T(8,128)S(1)}, f32[6,512,128]{2,1,0:T(8,128)}, u32[]{:S(2)}) copy-start(f32[6,512,128]{2,1,0:T(8,128)} %copy-done.2) | copy-start | bytes 4718596
  241.4 21.8 %all-to-all-start.2 = ((f32[128,2,6,128]{3,1,2,0:T(2,128)}), f32[128,2,6,128]{3,1,2,0:T(2,128)}, u32[]{:S(2)}, u32[]{:S(2)}) async-start(f32[128,2,6,128]{3,1,2,0:T(2,128)} %broadcast_in_dim.137), calls=%async_computation.2 | async-start | bytes 1572864 | tf_op jit(solution)/shard_map/all_to_all | solution.py:231
  263.2 3.5 copy-start.7
  267.6 1.2 copy-start.13
  268.9 1.2 copy-start.12
  329.5 21.0 %all-to-all-start.3 = ((f32[128,2,6,128]{3,1,2,0:T(2,128)}), f32[128,2,6,128]{3,1,2,0:T(2,128)S(1)}, u32[]{:S(2)}, u32[]{:S(2)}) async-start(f32[128,2,6,128]{3,1,2,0:T(2,128)} %broadcast_in_dim.138), calls=%async_computation.3 | async-start | bytes 1572864 | tf_op jit(solution)/shard_map/all_to_all | solution.py:231
Sparse Core Ops, SparseCore 0:
  10.1 50.7 all-gather.1
